TPU v7x, 32 devices: a whole 2x2x4 slice. The times are simulated.
32 devices in a mesh: groups: 2 (over x), gx: 8 (over z, y), gy: 2 (over core).
Axes of the slice: x: 2, y: 2, z: 4, core: 2. Of those that a mesh axis runs over, the one named last changes fastest.
Arguments:
- features: bfloat16 [64, 512, 1280], P(('groups', 'gy'), 'gx'), parts along dimension 0, may hold values from -600 to 600
- probe_weight: bfloat16 [1280, 32], replicated, may hold values from -0.15625 to 0.15625
- probe_bias: float32 [32], replicated, may hold values from -4 to 4
- labels: int32 [896, 7168], P(('groups', 'gy'), 'gx'), parts along dimension 0, may hold values from 0 to 31
- valid_mask: int32 [896, 7168], P(('groups', 'gy'), 'gx'), parts along dimension 0, may hold values 0 or 1
- valid_count: int32 [4, 8], P(('groups', 'gy'), 'gx'), parts along dimension 0, may hold values from 50176 to 301056
Outputs:
- loss: float32 [2], P('groups'), parts along dimension 0
- grad_weight: float32 [2560, 32], P('groups'), parts along dimension 0
- grad_bias: float32 [64], P('groups'), parts along dimension 0
There are 2 independent parts, one for each index of `groups`. A program takes and returns all parts, laid end to end along the dimension named above; an argument that names none is the same for every part. Nothing has to cross between parts.
All inputs are finite; a program needn't handle non-finite values. No bound on the sum of `valid_mask` on one device may be relied on, other than what follows from the above.
Results may differ from a plain program's by a relative error of at most 0.0016.
Values sent between devices are 32-bit elements; how exact they have to be, the bound alone decides.
No kernel may reach another device: no remote copies, remote signals or barrier semaphores. Data moves between devices by JAX's collectives and lax.ppermute only.
A program may use at most 128 MiB of HBM per device.

v0:
```python
import jax
import jax.numpy as jnp
from jax import lax
from jax.sharding import PartitionSpec as P

PATCH = 14
ROWBLOCK = 4


def padded_2(block, sides, width):
    for axis, dim in sides:
        count = lax.axis_size(axis)
        forward = [(i, i + 1) for i in range(count - 1)]
        backward = [(target, source) for source, target in forward]
        low = lax.ppermute(
            lax.slice_in_dim(block, block.shape[dim] - width, None, axis=dim), axis, forward
        )
        high = lax.ppermute(lax.slice_in_dim(block, 0, width, axis=dim), axis, backward)
        block = jnp.concatenate([low, block, high], axis=dim)
    return block


def from_behind(shard, axis, by):
    peers = lax.axis_size(axis)
    pairs = [(i, i + by) for i in range(peers) if 0 <= i + by < peers]
    return lax.ppermute(shard, axis, pairs)


def weights_table():
    offset = jnp.arange(PATCH, dtype=jnp.float32)
    shift = (offset + 0.5) / PATCH - 0.5
    return (jnp.maximum(-shift, 0.0), jnp.abs(shift) * -1.0 + 1.0, jnp.maximum(shift, 0.0))


def widen_cols(padded):
    before, centre, after = weights_table()
    chans, height, width = (padded.shape[0], padded.shape[1], padded.shape[2] - 2)
    out = (
        padded[:, :, 1:-1, None] * centre
        + padded[:, :, :-2, None] * before
        + padded[:, :, 2:, None] * after
    )
    return out.reshape(chans, height, width * PATCH)


def narrow_cols(grad):
    before, centre, after = weights_table()
    chans, height, span = grad.shape
    parts = grad.reshape(chans, height, span // PATCH, PATCH)
    mid = jnp.sum(parts * centre, axis=3)
    low = jnp.sum(parts * before, axis=3)
    high = jnp.sum(parts * after, axis=3)
    return (
        jnp.pad(mid, ((0, 0), (0, 0), (1, 1)))
        + jnp.pad(low, ((0, 0), (0, 0), (0, 2)))
        + jnp.pad(high, ((0, 0), (0, 0), (2, 0)))
    )


def widen_rows(slab):
    before, centre, after = weights_table()
    chans, count, span = (slab.shape[0], slab.shape[1] - 2, slab.shape[2])
    out = (
        slab[:, 1:-1, None, :] * centre[:, None]
        + slab[:, :-2, None, :] * before[:, None]
        + slab[:, 2:, None, :] * after[:, None]
    )
    return out.reshape(chans, count * PATCH, span)


def narrow_rows(grad):
    before, centre, after = weights_table()
    chans, pixrows, span = grad.shape
    parts = grad.reshape(chans, pixrows // PATCH, PATCH, span)
    mid = jnp.sum(parts * centre[:, None], axis=2)
    low = jnp.sum(parts * before[:, None], axis=2)
    high = jnp.sum(parts * after[:, None], axis=2)
    return (
        jnp.pad(mid, ((0, 0), (1, 1), (0, 0)))
        + jnp.pad(low, ((0, 0), (0, 2), (0, 0)))
        + jnp.pad(high, ((0, 0), (2, 0), (0, 0)))
    )


def run_blocks(widened, labels, valid_mask):
    chans = widened.shape[0]
    blocks = labels.shape[0] // PATCH // ROWBLOCK
    classes = jnp.arange(chans, dtype=jnp.int32)

    def step(carry, index):
        grad_pad, total = carry
        start = index * ROWBLOCK
        slab = lax.dynamic_slice_in_dim(widened, start, ROWBLOCK + 2, 1)
        label_rows = lax.dynamic_slice_in_dim(labels, start * PATCH, ROWBLOCK * PATCH, 0)
        mask_rows = lax.dynamic_slice_in_dim(valid_mask, start * PATCH, ROWBLOCK * PATCH, 0)
        scores = widen_rows(slab)
        top = jnp.max(scores, axis=0)
        lse = top + jnp.log(jnp.sum(jnp.exp(scores - top[None]), axis=0))
        onehot = (classes[:, None, None] == label_rows[None]).astype(jnp.float32)
        weight = mask_rows.astype(jnp.float32)
        picked = jnp.sum(onehot * scores, axis=0)
        total = total + jnp.sum(weight * (lse - picked))
        pixel_grad = weight[None] * (jnp.exp(scores - lse[None]) - onehot)
        back = narrow_rows(pixel_grad)
        old = lax.dynamic_slice_in_dim(grad_pad, start, ROWBLOCK + 2, 1)
        grad_pad = lax.dynamic_update_slice_in_dim(grad_pad, old + back, start, 1)
        return ((grad_pad, total), None)

    init = (jnp.zeros(widened.shape, jnp.float32), jnp.zeros((), jnp.float32))
    (grad_pad, total), unused = lax.scan(step, init, jnp.arange(blocks, dtype=jnp.int32))
    return (grad_pad, total)


def body(features, probe_weight, probe_bias, labels, valid_mask, valid_count):
    rows, cols, width = features.shape
    count = jnp.sum(valid_count).astype(jnp.float32)
    total = lax.psum(count, ("gx", "gy"))
    flat = features.reshape(rows * cols, width)
    logits = jnp.dot(flat, probe_weight, preferred_element_type=jnp.float32) + probe_bias[None, :]
    chans = logits.shape[1]
    logits = logits.reshape(rows, cols, chans).transpose(2, 0, 1)
    padded = padded_2(logits, (("gx", 2), ("gy", 1)), 1)
    col_index = lax.axis_index("gx")
    row_index = lax.axis_index("gy")
    col_first = col_index == 0
    col_last = col_index == lax.axis_size("gx") - 1
    row_first = row_index == 0
    row_last = row_index == lax.axis_size("gy") - 1
    left = jnp.where(col_first, padded[:, :, 1:2], padded[:, :, 0:1])
    right = jnp.where(col_last, padded[:, :, -2:-1], padded[:, :, -1:])
    padded = jnp.concatenate([left, padded[:, :, 1:-1], right], axis=2)
    upper = jnp.where(row_first, padded[:, 1:2], padded[:, 0:1])
    lower = jnp.where(row_last, padded[:, -2:-1], padded[:, -1:])
    padded = jnp.concatenate([upper, padded[:, 1:-1], lower], axis=1)
    widened = widen_cols(padded)
    grad_pad, loss_part = run_blocks(widened, labels, valid_mask)
    grad = narrow_cols(grad_pad)
    zeros_row = jnp.zeros_like(grad[:, 0:1])
    top_add = jnp.where(row_first, grad[:, 0:1], zeros_row)
    bottom_add = jnp.where(row_last, grad[:, -1:], zeros_row)
    grad = jnp.concatenate(
        [
            grad[:, 0:1],
            grad[:, 1:2] + top_add,
            grad[:, 2:-2],
            grad[:, -2:-1] + bottom_add,
            grad[:, -1:],
        ],
        axis=1,
    )
    zeros_col = jnp.zeros_like(grad[:, :, 0:1])
    left_add = jnp.where(col_first, grad[:, :, 0:1], zeros_col)
    right_add = jnp.where(col_last, grad[:, :, -1:], zeros_col)
    grad = jnp.concatenate(
        [
            grad[:, :, 0:1],
            grad[:, :, 1:2] + left_add,
            grad[:, :, 2:-2],
            grad[:, :, -2:-1] + right_add,
            grad[:, :, -1:],
        ],
        axis=2,
    )
    from_below = from_behind(grad[:, 0:1, :], "gy", -1)
    from_above = from_behind(grad[:, -1:, :], "gy", 1)
    inner = jnp.concatenate(
        [grad[:, 1:2] + from_above, grad[:, 2:-2], grad[:, -2:-1] + from_below], axis=1
    )
    from_right = from_behind(inner[:, :, 0:1], "gx", -1)
    from_left = from_behind(inner[:, :, -1:], "gx", 1)
    patch_grad = jnp.concatenate(
        [inner[:, :, 1:2] + from_left, inner[:, :, 2:-2], inner[:, :, -2:-1] + from_right], axis=2
    )
    rounded = patch_grad.astype(jnp.bfloat16).reshape(chans, rows * cols).T
    weight_part = lax.dot_general(
        flat, rounded, (((0,), (0,)), ((), ())), preferred_element_type=jnp.float32
    )
    bias_part = jnp.sum(patch_grad, axis=(1, 2))
    extra = jnp.zeros((), jnp.float32)
    weight_sum, bias_sum, loss_sum, extra_sum = lax.psum(
        (weight_part, bias_part, loss_part, extra), ("gx", "gy")
    )
    return ((loss_sum / total).reshape(1), weight_sum / total, bias_sum / total)


def solution(mesh):
    return jax.shard_map(
        body,
        mesh=mesh,
        in_specs=(
            P(("groups", "gy"), "gx", None),
            P(),
            P(),
            P(("groups", "gy"), "gx"),
            P(("groups", "gy"), "gx"),
            P(("groups", "gy"), "gx"),
        ),
        out_specs=(P("groups"), P("groups", None), P("groups")),
        check_vma=False,
    )
```

profile of v0, /device:TPU:0, one launch (start us, length us, event | category | flops | bytes accessed | tf_op | source)
XLA Modules:
  0.0 373.8 jit_solution(10591767936966858015)
XLA Ops:
  11.0 4.9 %collective-permute-start = (f32[32,16,1]{2,0,1:T(8,128)S(1)}, f32[32,16,1]{2,0,1:T(8,128)S(1)}, u32[]{:S(2)}, u32[]{:S(2)}) collective-permute-start(f32[32,16,1]{2,0,1:T(8,128)S(1)} %get-tuple-element.198), channel_id=1, source_target_pairs={{0,2},{2,4},{4,6},{6,8},{8,10},{10,12},{12,14},{1,3},{3,5},{5,7},{... | collective-permute-start | bytes 6152 | tf_op jit(solution)/shard_map/ppermute | solution.py:15
  17.2 9.8 %collective-permute-done = f32[32,16,1]{2,0,1:T(8,128)S(1)} collective-permute-done((f32[32,16,1]{2,0,1:T(8,128)S(1)}, f32[32,16,1]{2,0,1:T(8,128)S(1)}, u32[]{:S(2)}, u32[]{:S(2)}) %collective-permute-start) | collective-permute-done | bytes 2080 | tf_op jit(solution)/shard_map/ppermute | solution.py:15
  34.7 4.4 %mul.260 = f32[32,18,64,14]{0,3,2,1:T(8,128)} broadcast(f32[32,18,64]{0,2,1:T(8,128)S(1)} %copy.29), dimensions={0,1,2} | broadcast | bytes 2211840 | tf_op jit(solution)/shard_map/mul | solution.py:39
  39.1 9.7 %mul.261 = f32[32,18,896]{0,2,1:T(8,128)} reshape(f32[32,18,64,14]{0,3,2,1:T(8,128)} %mul.260) | data formatting | bytes 4128768 | tf_op jit(solution)/shard_map/mul | solution.py:39
  50.0 4.4 %mul.267 = f32[32,18,64,14]{0,3,2,1:T(8,128)} broadcast(f32[32,18,64]{0,2,1:T(8,128)S(1)} %copy.30), dimensions={0,1,2} | broadcast | bytes 2211840 | tf_op jit(solution)/shard_map/mul | solution.py:40
  54.4 9.7 %mul.268 = f32[32,18,896]{0,2,1:T(8,128)} reshape(f32[32,18,64,14]{0,3,2,1:T(8,128)} %mul.267) | data formatting | bytes 4128768 | tf_op jit(solution)/shard_map/mul | solution.py:40
  64.3 4.4 %mul.273 = f32[32,18,64,14]{0,3,2,1:T(8,128)} broadcast(f32[32,18,64]{0,2,1:T(8,128)S(1)} %copy.31), dimensions={0,1,2} | broadcast | bytes 2211840 | tf_op jit(solution)/shard_map/mul | solution.py:41
  68.7 9.7 %mul.274 = f32[32,18,896]{0,2,1:T(8,128)} reshape(f32[32,18,64,14]{0,3,2,1:T(8,128)} %mul.273) | data formatting | bytes 4128768 | tf_op jit(solution)/shard_map/mul | solution.py:41
  78.3 12.9 %multiply_add_fusion.3 = f32[32,18,896]{0,2,1:T(8,128)} fusion(f32[32,18,896]{0,2,1:T(8,128)} %mul.274, f32[32,18,896]{0,2,1:T(8,128)} %mul.268, f32[32,18,896]{0,2,1:T(8,128)} %mul.261, f32[896]{0:T(1024)S(1)} %mul.276, f32[896]{0:T(1024)S(1)} %mul.270, f32[896]{0:T(1024)S(1)} %mul.264), kind=kLoop, calls=%fused_computation.28 | loop fusion | flops 2580480 | bytes 8268288 | tf_op jit(solution)/shard_map/add | solution.py:39
  91.2 6.4 %copy.32 = f32[32,18,896]{2,0,1:T(8,128)} copy(f32[32,18,896]{0,2,1:T(8,128)} %multiply_add_fusion.3) | data formatting | bytes 4128768
  99.6 112.4 %while.15 = (s32[]{:T(128)}, f32[32,18,896]{2,0,1:T(8,128)}, f32[]{:T(128)}, s32[4]{0:T(128)}, s32[224,896]{1,0:T(8,128)}, /*index=5*/f32[32,18,896]{2,0,1:T(8,1...) while((s32[]{:T(128)}, f32[32,18,896]{2,0,1:T(8,128)}, ...), condition=%wide.region_8.9_spmd.clone, body=%wide.region_0.8_spmd.clone.sunk | while | flops 50047156 | bytes 17863660 | solution.py:110
  102.9 2.5 fusion.28
  105.4 2.6 exponential_reduce_fusion.2
  114.4 7.6 %multiply_reduce_fusion.9 = (f32[32,4,896]{2,0,1:T(8,128)}, f32[32,4,896]{2,0,1:T(8,128)}, f32[32,4,896]{2,0,1:T(8,128)}, f32[4,14,896]{2,1,0:T(8,128)S(1)}) fusion(s32[4,14,896]{2,1,0:T(8,128)} %eq.67, f32[4,14,896]{2,1,0:T(8,128)} %log_add_fusion.2, f32[14]{0:T(128)S(1)} %broadcast_maximum_fusion.3, f32[32,4,896]{2,0,1:T(8,128)} %copy-done.1, ...), kind=kLoop, calls=%fused_computation.9.clone.1 | loop fusion | flops 28507136 | bytes 3555496 | tf_op jit(solution)/shard_map/while/body/eval_jaxpr/reduce_sum | solution.py:75
  131.0 2.5 fusion.28
  133.5 2.6 exponential_reduce_fusion.2
  142.5 7.6 %multiply_reduce_fusion.9 = (f32[32,4,896]{2,0,1:T(8,128)}, f32[32,4,896]{2,0,1:T(8,128)}, f32[32,4,896]{2,0,1:T(8,128)}, f32[4,14,896]{2,1,0:T(8,128)S(1)}) fusion(s32[4,14,896]{2,1,0:T(8,128)} %eq.67, f32[4,14,896]{2,1,0:T(8,128)} %log_add_fusion.2, f32[14]{0:T(128)S(1)} %broadcast_maximum_fusion.3, f32[32,4,896]{2,0,1:T(8,128)} %copy-done.1, ...), kind=kLoop, calls=%fused_computation.9.clone.1 | loop fusion | flops 28507136 | bytes 3555496 | tf_op jit(solution)/shard_map/while/body/eval_jaxpr/reduce_sum | solution.py:75
  159.1 2.5 fusion.28
  161.6 2.6 exponential_reduce_fusion.2
  170.6 7.6 %multiply_reduce_fusion.9 = (f32[32,4,896]{2,0,1:T(8,128)}, f32[32,4,896]{2,0,1:T(8,128)}, f32[32,4,896]{2,0,1:T(8,128)}, f32[4,14,896]{2,1,0:T(8,128)S(1)}) fusion(s32[4,14,896]{2,1,0:T(8,128)} %eq.67, f32[4,14,896]{2,1,0:T(8,128)} %log_add_fusion.2, f32[14]{0:T(128)S(1)} %broadcast_maximum_fusion.3, f32[32,4,896]{2,0,1:T(8,128)} %copy-done.1, ...), kind=kLoop, calls=%fused_computation.9.clone.1 | loop fusion | flops 28507136 | bytes 3555496 | tf_op jit(solution)/shard_map/while/body/eval_jaxpr/reduce_sum | solution.py:75
  187.2 2.5 fusion.28
  189.7 2.6 exponential_reduce_fusion.2
  198.7 7.6 %multiply_reduce_fusion.9 = (f32[32,4,896]{2,0,1:T(8,128)}, f32[32,4,896]{2,0,1:T(8,128)}, f32[32,4,896]{2,0,1:T(8,128)}, f32[4,14,896]{2,1,0:T(8,128)S(1)}) fusion(s32[4,14,896]{2,1,0:T(8,128)} %eq.67, f32[4,14,896]{2,1,0:T(8,128)} %log_add_fusion.2, f32[14]{0:T(128)S(1)} %broadcast_maximum_fusion.3, f32[32,4,896]{2,0,1:T(8,128)} %copy-done.1, ...), kind=kLoop, calls=%fused_computation.9.clone.1 | loop fusion | flops 28507136 | bytes 3555496 | tf_op jit(solution)/shard_map/while/body/eval_jaxpr/reduce_sum | solution.py:75
  209.5 2.5 add_dynamic-update-slice_fusion.2
  212.0 6.1 %copy.33 = f32[32,18,896]{0,2,1:T(8,128)} copy(f32[32,18,896]{2,0,1:T(8,128)} %get-tuple-element.108) | data formatting | bytes 4128768 | tf_op jit(solution)/shard_map/while | solution.py:110
  218.1 9.6 %reshape.155 = f32[32,18,64,14]{0,3,2,1:T(8,128)} reshape(f32[32,18,896]{0,2,1:T(8,128)} %copy.33) | data formatting | bytes 4128768 | tf_op jit(solution)/shard_map/reshape | solution.py:49
  227.8 13.2 %multiply_reduce_fusion.6 = (f32[32,18,64]{0,2,1:T(8,128)S(1)}, f32[32,18,64]{0,2,1:T(8,128)}, f32[32,18,64]{0,2,1:T(8,128)}) fusion(f32[32,18,64,14]{0,3,2,1:T(8,128)} %reshape.155, f32[14]{0:T(128)S(1)} %copy-done.3, f32[14]{0:T(128)S(1)} %copy-done.5, f32[14]{0:T(128)S(1)} %get-tuple-element.200), kind=kLoop, calls=%fused_computation.27 | loop fusion | flops 2985984 | bytes 2506920 | tf_op jit(solution)/shard_map/reduce_sum | solution.py:50
  253.3 4.4 %collective-permute-start.6 = (f32[32,16,1]{2,0,1:T(8,128)S(1)}, f32[32,16,1]{2,0,1:T(8,128)S(1)}, u32[]{:S(2)}, u32[]{:S(2)}) collective-permute-start(f32[32,16,1]{2,0,1:T(8,128)S(1)} %get-tuple-element.197), channel_id=1, source_target_pairs={{0,2},{2,4},{4,6},{6,8},{8,10},{10,12},{12,14},{1,3},{3,5},{5,7},{... | collective-permute-start | bytes 6152 | tf_op jit(solution)/shard_map/ppermute | solution.py:26
  259.4 4.2 %collective-permute-done.6 = f32[32,16,1]{2,0,1:T(8,128)S(1)} collective-permute-done((f32[32,16,1]{2,0,1:T(8,128)S(1)}, f32[32,16,1]{2,0,1:T(8,128)S(1)}, u32[]{:S(2)}, u32[]{:S(2)}) %collective-permute-start.6) | collective-permute-done | bytes 2080 | tf_op jit(solution)/shard_map/ppermute | solution.py:26
  263.6 5.4 %collective-permute-done.7 = f32[32,16,1]{2,0,1:T(8,128)S(1)} collective-permute-done((f32[32,16,1]{2,0,1:T(8,128)S(1)}, f32[32,16,1]{2,0,1:T(8,128)S(1)}, u32[]{:S(2)}, u32[]{:S(2)}) %collective-permute-start.7) | collective-permute-done | bytes 2080 | tf_op jit(solution)/shard_map/ppermute | solution.py:26
  270.7 37.0 %all-reduce.6 = (f32[]{:T(128)}, f32[]{:T(128)}, f32[32]{0:T(128)S(1)}) all-reduce(f32[]{:T(128)} %get-tuple-element.107, f32[]{:T(128)} %bitcast.2, f32[32]{0:T(128)S(1)} %add_add_fusion.2), channel_id=1, replica_groups=mesh['groups'=2,'gx'=8,'gy'=2] {'gx','gy'}, use_global_device_ids=true, to_apply=%region_9.10 | all-reduce | flops 34 | bytes 272 | tf_op jit(solution)/shard_map/psum | solution.py:180
  310.2 53.4 %all-reduce.9.cloned.1.call-done = f32[1280,32]{0,1:T(8,128)} async-done(((f32[1280,32]{0,1:T(8,128)}), f32[1280,32]{0,1:T(8,128)}) %all-reduce.9.cloned.1.call-update) | async-done | bytes 163856 | tf_op jit(solution)/shard_map/psum | solution.py:180
  (129 shorter events, 86.2 us)
Async XLA Ops:
  7.2 1.7 copy-start
  7.2 356.4 %all-reduce.9.cloned.1.call-start = ((), (), s32[]{:S(2)}) async-start(), calls=%async_computation | async-start | bytes 327680 | tf_op jit(solution)/shard_map/psum | solution.py:180
  11.0 16.1 %collective-permute-start = (f32[32,16,1]{2,0,1:T(8,128)S(1)}, f32[32,16,1]{2,0,1:T(8,128)S(1)}, u32[]{:S(2)}, u32[]{:S(2)}) collective-permute-start(f32[32,16,1]{2,0,1:T(8,128)S(1)} %get-tuple-element.198), channel_id=1, source_target_pairs={{0,2},{2,4},{4,6},{6,8},{8,10},{10,12},{12,14},{1,3},{3,5},{5,7},{... | collective-permute-start | bytes 6152 | tf_op jit(solution)/shard_map/ppermute | solution.py:15
  15.9 11.2 %collective-permute-start.1 = (f32[32,16,1]{2,0,1:T(8,128)S(1)}, f32[32,16,1]{2,0,1:T(8,128)S(1)}, u32[]{:S(2)}, u32[]{:S(2)}) collective-permute-start(f32[32,16,1]{2,0,1:T(8,128)S(1)} %get-tuple-element.199), channel_id=1, source_target_pairs={{2,0},{4,2},{6,4},{8,6},{10,8},{12,10},{14,12},{3,1},{5,3},{7,5},{... | collective-permute-start | bytes 6152 | tf_op jit(solution)/shard_map/ppermute | solution.py:18
  17.2 12.6 %copy-start.2 = (f32[14]{0:T(128)}, f32[14]{0:T(128)S(1)}, u32[]{:S(2)}) copy-start(f32[14]{0:T(128)S(1)} %get-tuple-element.201) | copy-start | bytes 172
  27.2 3.3 collective-permute-start.2
  28.5 3.1 collective-permute-start.3
  29.8 0.5 copy-start.4
  102.8 2.6 copy-start.1
  131.0 2.6 copy-start.1
  159.0 2.6 copy-start.1
  187.1 2.6 copy-start.1
  218.1 9.7 %copy-start.3 = (f32[14]{0:T(128)S(1)}, f32[14]{0:T(128)}, u32[]{:S(2)}) copy-start(f32[14]{0:T(128)} %copy-done.2) | copy-start | bytes 172
  218.1 9.7 %copy-start.5 = (f32[14]{0:T(128)S(1)}, f32[14]{0:T(128)}, u32[]{:S(2)}) copy-start(f32[14]{0:T(128)} %copy-done.4) | copy-start | bytes 172
  247.2 2.9 collective-permute-start.4
  250.1 3.1 collective-permute-start.5
  253.3 10.3 %collective-permute-start.6 = (f32[32,16,1]{2,0,1:T(8,128)S(1)}, f32[32,16,1]{2,0,1:T(8,128)S(1)}, u32[]{:S(2)}, u32[]{:S(2)}) collective-permute-start(f32[32,16,1]{2,0,1:T(8,128)S(1)} %get-tuple-element.197), channel_id=1, source_target_pairs={{0,2},{2,4},{4,6},{6,8},{8,10},{10,12},{12,14},{1,3},{3,5},{5,7},{... | collective-permute-start | bytes 6152 | tf_op jit(solution)/shard_map/ppermute | solution.py:26
  257.7 11.3 %collective-permute-start.7 = (f32[32,16,1]{2,0,1:T(8,128)S(1)}, f32[32,16,1]{2,0,1:T(8,128)S(1)}, u32[]{:S(2)}, u32[]{:S(2)}) collective-permute-start(f32[32,16,1]{2,0,1:T(8,128)S(1)} %get-tuple-element.196), channel_id=1, source_target_pairs={{2,0},{4,2},{6,4},{8,6},{10,8},{12,10},{14,12},{3,1},{5,3},{7,5},{... | collective-permute-start | bytes 6152 | tf_op jit(solution)/shard_map/ppermute | solution.py:26
Sparse Core Ops, SparseCore 0:
  270.8 92.7 all-reduce.8
where the time goes:
time: 377 us; the launch traced here: 374 us
  other arithmetic  114 us (30%)
  local copies, waits for them, and re-layouts  101 us (27%)
  waiting for transfers between devices  75.9 us (20%)
  blocking collectives  37 us (10%)
  starting transfers between devices  17.9 us (5%)
  between operations  17.5 us (5%)
  loops' own time  7.31 us (2%)
    psum x1, waiting for transfers between devices, body(): lax.psum((weight_part, bias_part, loss_part, extra), ('gx', 'gy'))  53.4 us
    psum x1, blocking collectives, body(): lax.psum((weight_part, bias_part, loss_part, extra), ('gx', 'gy'))  37 us
    reduce_sum x4, other arithmetic, narrow_rows(): mid = jnp.sum(parts * centre[:, None], axis=2)  30.2 us
    mul x4, local copies, waits for them, and re-layouts, widen_cols(): padded[:, :, :-2, None] * before  14.2 us
    mul x4, local copies, waits for them, and re-layouts, widen_cols(): padded[:, :, 1:-1, None] * centre + padded[:, :, :-2, None] * before  14.2 us
    mul x4, local copies, waits for them, and re-layouts, widen_cols(): padded[:, :, 2:, None] * after  14.2 us
    reduce_sum x1, other arithmetic, narrow_cols(): mid = jnp.sum(parts * centre, axis=3)  13.2 us
    add x1, other arithmetic, widen_cols(): padded[:, :, 1:-1, None] * centre + padded[:, :, :-2, None] * before  12.9 us
  transfers between devices with their start and end apart: 9, of which 7 were waited for; matrix products, arithmetic and copies ran while one was open for 1% of the time, Pallas kernels for 0%

commit v1 on v0

v1 whole, which is shorter than its diff:
```python
import functools
import math

import jax
import jax.numpy as jnp
import numpy as np
from jax import lax
from jax.experimental import pallas as pl
from jax.experimental.pallas import tpu as pltpu
from jax.sharding import PartitionSpec as P

PATCH = 14
HALF = PATCH // 2
STEP = 2 * PATCH
LANES = 128
SUB = 8
LOG2E = 1.0 / math.log(2.0)
LN2 = math.log(2.0)
FLOOR = -100.0
f32 = jnp.float32
bf16 = jnp.bfloat16
VMEM = pl.BlockSpec(memory_space=pltpu.VMEM)
SMEM = pl.BlockSpec(memory_space=pltpu.SMEM)


def whole(shape):
    return pl.BlockSpec(shape, lambda *ids: (0,) * len(shape))


def column_tables(cols):
    near = np.array([STEP - abs(2 * j + 1 - PATCH) for j in range(PATCH)])
    far = STEP - near
    inner = np.zeros((cols, cols * PATCH), np.float32)
    for q in range(cols * PATCH):
        i, j = divmod(q, PATCH)
        inner[i, q] += near[j]
        k = i - 1 if j < HALF else i + 1
        if 0 <= k < cols:
            inner[k, q] += far[j]
    own = np.zeros((cols, LANES), np.float32)
    halo = np.zeros((2, LANES), np.float32)
    for lane in range(4 * HALF):
        side, k = divmod(lane, HALF)
        j = k + HALF if side in (0, 2) else k
        edge = 0 if side < 2 else cols - 1
        outside = side in (0, 3)
        own[edge, lane] = far[j] if outside else near[j]
        halo[int(side > 1), lane] = near[j] if outside else far[j]
    return inner, own, halo


def split3(x):
    hi = x.astype(bf16)
    rest = x - hi.astype(f32)
    mid = rest.astype(bf16)
    return hi, mid, (rest - mid.astype(f32)).astype(bf16)


def stack3(x, cols):
    lane = lax.broadcasted_iota(jnp.int32, x.shape, 1)
    hi, mid, low = (part.astype(f32) for part in split3(jnp.where(lane < cols, x, 0.0)))
    first = jnp.where(lane < cols, hi, pltpu.roll(mid, cols, 1))
    return jnp.concatenate([first.astype(bf16), low.astype(bf16)], axis=1)


def logits_kernel(
    rows, cols, chans, slots, per, f_ref, w_ref, bias_ref, ll_ref, lr_ref, ml_ref, mr_ref, sel_ref,
    x_ref, e_ref, sa_ref, sb_ref,
):
    step = pl.program_id(0)
    steps = pl.num_programs(0)

    @pl.when(step == 0)
    def _():
        x_ref[...] = jnp.zeros_like(x_ref)

    block = f_ref[...].reshape(per * cols, f_ref.shape[2])
    score = lax.dot_general(w_ref[...], block, (((1,), (1,)), ((), ())), preferred_element_type=f32)
    score = score + bias_ref[...]
    score = (score - jnp.max(score, axis=0, keepdims=True)) * (LOG2E / STEP)
    lane = lax.broadcasted_iota(jnp.int32, (chans, LANES), 1)
    for k in range(per):
        at = k * cols
        tile = score[:, at // LANES * LANES : at // LANES * LANES + LANES]
        if at % LANES:
            tile = pltpu.roll(tile, LANES - at % LANES, 1)
        tile = jnp.where(lane < cols, tile, 0.0)
        x_ref[pl.ds(step * per + k + 1, chans, stride=slots), :] = tile
        if k == 0:

            @pl.when(step == 0)
            def _():
                e_ref[0:chans, :] = tile

        if k == per - 1:

            @pl.when(step == steps - 1)
            def _():
                e_ref[chans : 2 * chans, :] = tile

    @pl.when(step == steps - 1)
    def _():
        edges = lax.dot_general(
            sel_ref[...], stack3(x_ref[...], cols), (((1,), (1,)), ((), ())), preferred_element_type=f32
        )
        at = lax.broadcasted_iota(jnp.int32, (SUB, LANES), 1)
        even = lax.rem(lax.axis_index("gx"), 2) == 0
        n = chans * slots // LANES
        for b in range(rows // SUB):
            left = jnp.full((SUB, LANES), -1.0, f32)
            right = left
            for j in range(PATCH):
                pick = pl.ds(b * SUB * PATCH + j, SUB, stride=PATCH)
                here = (at >= j * HALF) & (at < j * HALF + HALF)
                lab = jnp.where(ml_ref[pick, :] != 0, ll_ref[pick, :], -1).astype(f32)
                shift = j * HALF
                left = jnp.where(here, pltpu.roll(lab, shift, 1) if shift else lab, left)
                lab = jnp.where(mr_ref[pick, :] != 0, lr_ref[pick, :], -1).astype(f32)
                right = jnp.where(here, pltpu.roll(lab, (shift + HALF) % LANES, 1), right)
            sa_ref[b * SUB : b * SUB + SUB, :] = jnp.where(even, right, left)
            sb_ref[b * SUB : b * SUB + SUB, :] = jnp.where(even, left, right)
        for r in range(n):
            part = edges[:, r * LANES : r * LANES + LANES]
            sa_ref[rows + r : rows + r + 1, :] = jnp.where(even, part[1:2], part[0:1])
            sb_ref[rows + r : rows + r + 1, :] = jnp.where(even, part[0:1], part[1:2])
        pad = sa_ref.shape[0] - rows - n
        if pad:
            sa_ref[rows + n :, :] = jnp.zeros((pad, LANES), f32)
            sb_ref[rows + n :, :] = jnp.zeros((pad, LANES), f32)


def softmax_fast(groups, chans, slots, up, w_ref, p_ref):
    sums = [None] * (groups * HALF)
    for c in range(chans):
        for b in range(groups):
            row = c * slots + SUB * b
            centre = w_ref[pl.ds(row + 1, SUB), :]
            beyond = w_ref[pl.ds(row + (2 if up else 0), SUB), :]
            slope = (beyond - centre) * (1.0 / STEP)
            p = jnp.exp2(centre + slope)
            ratio = jnp.exp2(slope + slope)
            for m in range(HALF):
                k = b * HALF + m
                if m:
                    p = p * ratio
                p_ref[c * groups * HALF + k] = p
                sums[k] = p if sums[k] is None else sums[k] + p
    return sums


def softmax_slow(groups, chans, slots, up, w_ref, p_ref, labels, weights):
    sums, losses = [], jnp.zeros((SUB, LANES), f32)
    for b in range(groups):
        for m in range(HALF):
            k = b * HALF + m

            def score(c, b=b, m=m):
                row = c * slots + SUB * b
                centre = w_ref[pl.ds(row + 1, SUB), :]
                beyond = w_ref[pl.ds(row + (2 if up else 0), SUB), :]
                return centre + (beyond - centre) * ((2 * m + 1.0) / STEP)

            top = lax.fori_loop(1, chans, lambda c, t: jnp.maximum(t, score(c)), score(0))

            def take(c, carry, k=k, top=top, score=score):
                total, picked = carry
                shifted = score(c) - top
                p = jnp.exp2(shifted)
                p_ref[c * groups * HALF + k] = p
                return total + p, jnp.where(labels[k] == c, shifted, picked)

            zero = jnp.zeros((SUB, LANES), f32)
            total, picked = lax.fori_loop(0, chans, take, (zero, zero))
            sums.append(total)
            losses = losses - weights[k] * picked
    return sums, losses


def pixels(groups, chans, slots, load_labels, fast, w_ref, p_ref, g_ref, s_ref):
    count = groups * HALF
    g_ref[...] = jnp.zeros_like(g_ref)
    loss = jnp.zeros((SUB, LANES), f32)
    for up in (False, True):
        labels = [None] * count
        for m in range(HALF):
            for b in range(groups):
                labels[b * HALF + m] = load_labels(b, HALF + m if up else HALF - 1 - m)
        weights = [jnp.where(lab >= 0, 1.0, 0.0) for lab in labels]
        packed = [
            jnp.concatenate([labels[b * HALF + m] for b in range(groups)], axis=0).astype(jnp.int16)
            for m in range(HALF)
        ]

        @pl.when(fast)
        def _():
            sums = softmax_fast(groups, chans, slots, up, w_ref, p_ref)
            for k in range(count):
                s_ref[k] = sums[k]
            s_ref[count] = jnp.zeros((SUB, LANES), f32)

        @pl.when(jnp.logical_not(fast))
        def _():
            sums, losses = softmax_slow(groups, chans, slots, up, w_ref, p_ref, labels, weights)
            for k in range(count):
                s_ref[k] = sums[k]
            s_ref[count] = losses

        sums = [s_ref[k] for k in range(count)]
        extra = s_ref[count]
        scale = []
        for k in range(count):
            loss = loss + weights[k] * jnp.log(sums[k])
            scale.append(weights[k] / sums[k])
        picked = jnp.zeros((SUB, LANES), f32)
        for c in range(chans):
            tally = None
            for m in range(HALF):
                hit = jnp.where(packed[m] == jnp.int16(c), jnp.int16(1 + SUB * (2 * m + 1)), jnp.int16(0))
                tally = hit if tally is None else tally + hit
            tally = tally.astype(jnp.int32)
            for b in range(groups):
                total = run = None
                for m in reversed(range(HALF)):
                    g = p_ref[c * count + b * HALF + m] * scale[b * HALF + m]
                    total = g if total is None else total + g
                    run = total if run is None else run + total
                part = tally[b * SUB : b * SUB + SUB]
                ones = (part & (SUB - 1)).astype(f32)
                far = lax.shift_right_logical(part, 3).astype(f32) * (1.0 / STEP)
                centre = pl.ds(c * slots + 1 + SUB * b, SUB)
                beyond = pl.ds(c * slots + (2 if up else 0) + SUB * b, SUB)
                picked = picked + (ones - far) * w_ref[centre, :] + far * w_ref[beyond, :]
                out = (run + run - total) * (1.0 / STEP) - far
                g_ref[centre, :] += (total - ones) - out
                g_ref[beyond, :] += out
        loss = loss + LN2 * jnp.where(fast, -picked, extra)
    return loss


def narrow(g_ref, table):
    g = g_ref[...]
    hi = g.astype(bf16)
    low = (g - hi.astype(f32)).astype(bf16)
    return jnp.dot(jnp.concatenate([hi, low], axis=1), table, preferred_element_type=f32)


def inner_kernel(
    cols, chans, slots, groups, x_ref, own_ref, got_ref, table_ref, back_ref, lab_ref, mask_ref,
    acc_ref, loss_ref, stack_ref, floor_ref, w_ref, p_ref, g_ref, s_ref, h_ref,
):
    step = pl.program_id(0)

    @pl.when(step == 0)
    def _():
        h_ref[...] = x_ref[...]
        row = lax.axis_index("gy")
        top = jnp.where(row == 0, own_ref[0:chans, :], got_ref[chans : 2 * chans, :])
        last = row == lax.axis_size("gy") - 1
        bottom = jnp.where(last, own_ref[chans : 2 * chans, :], got_ref[0:chans, :])
        h_ref[pl.ds(0, chans, stride=slots), :] = top
        h_ref[pl.ds(groups * SUB + 1, chans, stride=slots), :] = bottom
        full = h_ref[...]
        floor_ref[0] = jnp.min(full) * STEP
        stack_ref[...] = stack3(full, cols)
        acc_ref[...] = jnp.zeros_like(acc_ref)
        loss_ref[...] = jnp.zeros_like(loss_ref)

    w_ref[...] = jnp.dot(stack_ref[...], table_ref[...], preferred_element_type=f32)
    lane = lax.broadcasted_iota(jnp.int32, (SUB, LANES), 1) + step * LANES
    inside = (lane >= HALF) & (lane < cols * PATCH - HALF)

    def load_labels(b, j):
        pick = pl.ds(b * SUB * PATCH + j, SUB, stride=PATCH)
        return jnp.where((mask_ref[pick, :] != 0) & inside, lab_ref[pick, :], -1)

    fast = floor_ref[0] >= FLOOR
    loss_ref[...] += pixels(groups, chans, slots, load_labels, fast, w_ref, p_ref, g_ref, s_ref)
    acc_ref[...] += narrow(g_ref, back_ref[...])


def edge_kernel(
    rows, cols, chans, slots, groups, floor_ref, stack_ref, acc_ref, loss_in_ref, sa_ref, sb_ref, ra_ref, rb_ref,
    va_ref, vb_ref, table_ref, fold_ref, back_ref, halo_ref, out_ref, v_ref, loss_ref, w_ref, p_ref, g_ref, s_ref,
):
    col = lax.axis_index("gx")
    row = lax.axis_index("gy")
    even = lax.rem(col, 2) == 0
    first, last = col == 0, col == lax.axis_size("gx") - 1
    n = chans * slots // LANES
    width = n * LANES

    def line(ref):
        return jnp.concatenate([ref[rows + r : rows + r + 1, :] for r in range(n)], axis=1)

    slot = lax.rem(lax.broadcasted_iota(jnp.int32, (1, width), 1), slots)

    def with_ends(mine, partner):
        top = jnp.where(row == 0, pltpu.roll(mine, width - 1, 1), pltpu.roll(partner, width - rows, 1))
        bottom = jnp.where(row == lax.axis_size("gy") - 1, pltpu.roll(mine, 1, 1), pltpu.roll(partner, rows, 1))
        return jnp.where(slot == 0, top, jnp.where(slot == rows + 1, bottom, mine))

    a = with_ends(line(ra_ref), line(va_ref))
    b = with_ends(line(rb_ref), line(vb_ref))
    sides = [jnp.where(even, b, a), jnp.where(even, a, b)]
    absent = [first, last]
    lows = jnp.float32(0.0)
    parts = []
    for side, gone in zip(sides, absent):
        side = jnp.where(gone, 0.0, side)
        lows = jnp.minimum(lows, jnp.min(side))
        parts += [part.astype(f32) for part in split3(side)]
    parts.append(jnp.zeros((16 - len(parts), width), f32))
    halo = jnp.concatenate(parts, axis=0).astype(bf16)
    table = table_ref[...]
    back = back_ref[...]
    depth = table.shape[0]
    zero = jnp.zeros_like(table)
    table = table + jnp.where(first, fold_ref[0:depth, :], zero) + jnp.where(last, fold_ref[depth : 2 * depth, :], zero)
    back = back + jnp.where(first, fold_ref[2 * depth : 3 * depth, :], zero)
    back = back + jnp.where(last, fold_ref[3 * depth : 4 * depth, :], zero)
    w_ref[...] = jnp.dot(stack_ref[...], table, preferred_element_type=f32) + lax.dot_general(
        halo, halo_ref[...], (((0,), (0,)), ((), ())), preferred_element_type=f32
    )
    lane = lax.broadcasted_iota(jnp.int32, (SUB, LANES), 1)

    def load_labels(b, j):
        pick = slice(b * SUB, b * SUB + SUB)
        strips = [
            jnp.where(first, -1.0, jnp.where(even, rb_ref[pick, :], ra_ref[pick, :])),
            jnp.where(even, sb_ref[pick, :], sa_ref[pick, :]),
            jnp.where(even, sa_ref[pick, :], sb_ref[pick, :]),
            jnp.where(last, -1.0, jnp.where(even, ra_ref[pick, :], rb_ref[pick, :])),
        ]
        out = jnp.full((SUB, LANES), -1.0, f32)
        for k, strip in enumerate(strips):
            shift = (k * HALF - j * HALF) % LANES
            moved = pltpu.roll(strip, shift, 1) if shift else strip
            out = jnp.where((lane >= k * HALF) & (lane < k * HALF + HALF), moved, out)
        return out.astype(jnp.int32)

    fast = jnp.minimum(lows * STEP, floor_ref[0]) >= FLOOR
    outside = (lane < HALF) | (lane >= 3 * HALF)
    loss = pixels(groups, chans, slots, load_labels, fast, w_ref, p_ref, g_ref, s_ref)
    loss_ref[...] = loss_in_ref[...] + jnp.where(outside, 0.0, loss)
    out_ref[...] = (acc_ref[...] + narrow(g_ref, back)) * (1.0 / STEP)
    v_ref[0:chans, :] = out_ref[pl.ds(0, chans, stride=slots), :]
    v_ref[chans : 2 * chans, :] = out_ref[pl.ds(rows + 1, chans, stride=slots), :]


def grad_kernel(
    rows, cols, chans, slots, per, f_ref, g_ref, own_ref, got_ref, loss_ref, count_ref,
    mine_ref, other_ref, sum_ref, acc_ref,
):
    step = pl.program_id(0)
    row = lax.axis_index("gy")

    @pl.when(step == 0)
    def _():
        sum_ref[...] = g_ref[...]
        last = row == lax.axis_size("gy") - 1
        top = jnp.where(row == 0, own_ref[0:chans, :], got_ref[chans : 2 * chans, :])
        bottom = jnp.where(last, own_ref[chans : 2 * chans, :], got_ref[0:chans, :])
        sum_ref[pl.ds(1, chans, stride=slots), :] += top
        sum_ref[pl.ds(rows, chans, stride=slots), :] += bottom
        acc_ref[...] = jnp.zeros_like(acc_ref)

    lane = lax.broadcasted_iota(jnp.int32, (chans, LANES), 1)
    share = LANES // cols
    tiles = []
    for k in range(0, per, share):
        tile = None
        for r in range(share):
            piece = sum_ref[pl.ds(step * per + k + r + 1, chans, stride=slots), :]
            if r:
                piece = pltpu.roll(piece, r * cols, 1)
            tile = piece if tile is None else jnp.where(lane < r * cols, tile, piece)
        tiles.append(tile.astype(bf16))
    block = f_ref[...].reshape(per * cols, f_ref.shape[2])
    acc_ref[...] += jnp.dot(jnp.concatenate(tiles, axis=1), block, preferred_element_type=f32)

    @pl.when(step == pl.num_programs(0) - 1)
    def _():
        total = sum_ref[pl.ds(1, chans, stride=slots), :]
        for i in range(2, rows + 1):
            total = total + sum_ref[pl.ds(i, chans, stride=slots), :]
        total = jnp.where(lane < cols, total, 0.0)
        square = jnp.concatenate([total, jnp.zeros((LANES - chans, LANES), f32)], axis=0)
        bias = jnp.sum(square.T, axis=0, keepdims=True)
        at = lax.broadcasted_iota(jnp.int32, (SUB, LANES), 0)
        rest = jnp.where(at == 1, jnp.sum(loss_ref[...]), count_ref[0, 0].astype(f32))
        stats = jnp.where(at == 0, bias, jnp.where(at < 3, rest, 0.0))
        half = acc_ref.shape[1] // 2
        low, high = acc_ref[:, 0:half], acc_ref[:, half:]
        mine_ref[:, 0:half] = jnp.where(row == 0, low, high)
        other_ref[:, 0:half] = jnp.where(row == 0, high, low)
        for ref in (mine_ref, other_ref):
            ref[0:SUB, half:] = stats
            ref[SUB:, half:] = jnp.zeros((chans - SUB, LANES), f32)


def final_kernel(y_ref, z_ref, loss_ref, weight_ref, bias_ref):
    chans = y_ref.shape[0]
    half = y_ref.shape[1] - LANES
    lower = lax.axis_index("gy") == 0
    y, z = y_ref[:, 0:half], z_ref[:, 0:half]
    stats = y_ref[0:SUB, half:]
    total = stats[2:3, 0:1]
    weight_ref[:, 0:half] = jnp.where(lower, y, z) / total
    weight_ref[:, half:] = jnp.where(lower, z, y) / total
    loss_ref[...] = stats[1:2, 0:1] / total
    bias_ref[...] = stats[0:1, 0:chans] / total


def body(features, probe_weight, probe_bias, labels, valid_mask, valid_count):
    rows, cols, width = features.shape
    chans = probe_weight.shape[1]
    gx, gy = lax.axis_size("gx"), lax.axis_size("gy")
    if gy != 2 or rows % SUB or cols * PATCH % LANES or gx & (gx - 1):
        raise ValueError("unsupported tile")
    groups = rows // SUB
    slots = rows + SUB
    count = groups * HALF
    tiles = cols * PATCH // LANES
    tall = rows * PATCH
    depth = 2 * LANES
    inner, own, halo = column_tables(cols)

    def forward(table):
        out = np.zeros((depth, table.shape[1]), np.float32)
        for k in range(3):
            out[k * cols : k * cols + cols] = table
        return out

    def backward(table):
        out = np.zeros((table.shape[1] // LANES, 2, LANES, LANES), np.float32)
        out[:, :, :, :cols] = table.T.reshape(-1, 1, LANES, cols)
        return out.reshape(-1, LANES)

    lift, back = forward(inner), backward(inner)
    left, right = np.zeros_like(own), np.zeros_like(own)
    left[0], right[cols - 1] = halo
    fold = np.concatenate([forward(left), forward(right), backward(left), backward(right)])
    sides = np.zeros((16, LANES), np.float32)
    sides[0:3], sides[3:6] = halo[0], halo[1]
    ends = np.zeros((SUB, depth), np.float32)
    for k in range(3):
        ends[0, k * cols] = 1.0
        ends[1, k * cols + cols - 1] = 1.0
    lift, back, own_f, own_b, fold, sides, ends = (
        jnp.asarray(t, bf16) for t in (lift, back, forward(own), backward(own), fold, sides, ends)
    )

    per = 4
    shape = lambda *dims: jax.ShapeDtypeStruct(dims, f32)
    strip = -(-(rows + chans * slots // LANES) // SUB) * SUB
    block = pl.BlockSpec((per, cols, width), lambda i: (i, 0, 0))
    tail = pl.BlockSpec((tall, LANES), lambda i: (0, tiles - 1))
    head = pl.BlockSpec((tall, LANES), lambda i: (0, 0))
    x, edge, send_a, send_b = pl.pallas_call(
        functools.partial(logits_kernel, rows, cols, chans, slots, per),
        grid=(rows // per,),
        in_specs=[block, whole((chans, width)), whole((chans, 1)), head, tail, head, tail, whole((SUB, depth))],
        out_specs=[whole((chans * slots, LANES)), whole((2 * chans, LANES)), whole((strip, LANES)), whole((strip, LANES))],
        out_shape=[shape(chans * slots, LANES), shape(2 * chans, LANES), shape(strip, LANES), shape(strip, LANES)],
        name="logits",
    )(features, probe_weight.T, probe_bias.reshape(chans, 1), labels, labels, valid_mask, valid_mask, ends)

    swap = lambda v: lax.ppermute(v, "gy", [(0, 1), (1, 0)])
    pairs = lambda at: [p for i in range(at, gx - 1, 2) for p in ((i, i + 1), (i + 1, i))]
    got = swap(edge)
    got_a = lax.ppermute(send_a, "gx", pairs(0))
    got_b = lax.ppermute(send_b, "gx", pairs(1))

    scratch = [
        pltpu.VMEM((chans * slots, LANES), f32),
        pltpu.VMEM((chans * count, SUB, LANES), f32),
        pltpu.VMEM((chans * slots, LANES), f32),
        pltpu.VMEM((count + 1, SUB, LANES), f32),
    ]
    column = pl.BlockSpec((tall, LANES), lambda t: (0, t))
    acc, loss, stack, floor = pl.pallas_call(
        functools.partial(inner_kernel, cols, chans, slots, groups),
        grid=(tiles,),
        in_specs=[
            whole((chans * slots, LANES)), whole((2 * chans, LANES)), whole((2 * chans, LANES)),
            pl.BlockSpec((depth, LANES), lambda t: (0, t)), pl.BlockSpec((depth, LANES), lambda t: (t, 0)),
            column, column,
        ],
        out_specs=[whole((chans * slots, LANES)), whole((SUB, LANES)), whole((chans * slots, depth)), SMEM],
        out_shape=[
            shape(chans * slots, LANES), shape(SUB, LANES),
            jax.ShapeDtypeStruct((chans * slots, depth), bf16), shape(1),
        ],
        scratch_shapes=scratch + [pltpu.VMEM((chans * slots, LANES), f32)],
        cost_estimate=pl.CostEstimate(flops=2 * 10**9, bytes_accessed=4 * 10**6, transcendentals=10**6),
        name="inner",
    )(x, edge, got, lift, back, labels, valid_mask)

    far_a, far_b = swap(got_a), swap(got_b)
    grad, spill, loss = pl.pallas_call(
        functools.partial(edge_kernel, rows, cols, chans, slots, groups),
        in_specs=[SMEM] + [VMEM] * 13,
        out_specs=[VMEM] * 3,
        out_shape=[shape(chans * slots, LANES), shape(2 * chans, LANES), shape(SUB, LANES)],
        scratch_shapes=scratch,
        name="edge",
    )(floor, stack, acc, loss, send_a, send_b, got_a, got_b, far_a, far_b, own_f, fold, own_b, sides)

    got = swap(spill)
    half = width // 2
    part = whole((chans, half + LANES))
    mine, other = pl.pallas_call(
        functools.partial(grad_kernel, rows, cols, chans, slots, per),
        grid=(rows // per,),
        in_specs=[
            block, whole((chans * slots, LANES)), whole((2 * chans, LANES)), whole((2 * chans, LANES)),
            whole((SUB, LANES)), SMEM,
        ],
        out_specs=[part, part],
        out_shape=[shape(chans, half + LANES)] * 2,
        scratch_shapes=[pltpu.VMEM((chans * slots, LANES), f32), pltpu.VMEM((chans, width), f32)],
        name="grad",
    )(features, grad, spill, got, loss, valid_count)

    total = mine + swap(other)
    step = 1
    while step < gx:
        total = total + lax.ppermute(total, "gx", [(i, i ^ step) for i in range(gx)])
        step *= 2
    loss, weight, bias = pl.pallas_call(
        final_kernel,
        in_specs=[VMEM] * 2,
        out_specs=[VMEM] * 3,
        out_shape=[shape(1, 1), shape(chans, width), shape(1, chans)],
        name="final",
    )(total, swap(total))
    return loss.reshape(1), weight.T, bias.reshape(chans)


def solution(mesh):
    return jax.shard_map(
        body,
        mesh=mesh,
        in_specs=(
            P(("groups", "gy"), "gx", None),
            P(),
            P(),
            P(("groups", "gy"), "gx"),
            P(("groups", "gy"), "gx"),
            P(("groups", "gy"), "gx"),
        ),
        out_specs=(P("groups"), P("groups", None), P("groups")),
        check_vma=False,
    )
```

time: 377 us -> 215 us (0.57)
  Pallas kernels: 0 us -> 180 us
  other arithmetic: 114 us -> 0.94 us
  local copies, waits for them, and re-layouts: 101 us -> 3.78 us
  waiting for transfers between devices: 75.9 us -> 13.1 us
  blocking collectives: 37 us -> 0 us
  between operations: 17.5 us -> 1.4 us
  loops' own time: 7.31 us -> 0 us
    pallas_call x0 -> x5, Pallas kernels: none -> 180 us  [the longest x1 146 us: body(): pl.pallas_call(functools.partial(inner_kernel, cols, chans, slots, groups...]
    reduce_sum x16 -> x0, other arithmetic: 60.9 us -> none  [the longest x4 30.2 us: narrow_rows(): mid = jnp.sum(parts * centre[:, None], axis=2)]
    psum x1 -> x0, waiting for transfers between devices: 53.4 us -> none  [body(): lax.psum((weight_part, bias_part, loss_part, extra), ('gx', 'gy'))]
    mul x16 -> x0, local copies, waits for them, and re-layouts: 49 us -> none  [the longest x4 14.2 us: widen_cols(): padded[:, :, :-2, None] * before]
    psum x1 -> x0, blocking collectives: 37 us -> none  [body(): lax.psum((weight_part, bias_part, loss_part, extra), ('gx', 'gy'))]
    add x8 -> x4, other arithmetic: 16 us -> 0.94 us  [the longest x1 0.91 us: body(): total = mine + swap(other)]
    reduce_max x4 -> x0, other arithmetic: 10.1 us -> none  [step(): top = jnp.max(scores, axis=0)]
    slice x16 -> x0, local copies, waits for them, and re-layouts: 9.92 us -> none  [the longest x4 5.68 us: widen_rows(): slab[:, 1:-1, None, :] * centre[:, None]]
  transfers between devices with their start and end apart: 9 -> 11, of which waited for: 7 -> 7; matrix products, arithmetic and copies ran while one was open for 1% -> 0% of each run, Pallas kernels for 0% -> 68%
where the time goes in v1:
time: 215 us; the launch traced here: 214 us
  Pallas kernels  180 us (84%)
  starting transfers between devices  15.5 us (7%)
  waiting for transfers between devices  13.1 us (6%)
  local copies, waits for them, and re-layouts  3.78 us (2%)
    pallas_call x1, Pallas kernels, body(): pl.pallas_call(functools.partial(inner_kernel, cols, chans, slots, groups...  146 us
    pallas_call x1, Pallas kernels, body(): pl.pallas_call(functools.partial(edge_kernel, rows, cols, chans, slots, g...  23.4 us
    ppermute x3, starting transfers between devices, body(): lax.ppermute(total, 'gx', [(i, i ^ step) for i in range(gx)])  11 us
    ppermute x3, waiting for transfers between devices, body(): lax.ppermute(total, 'gx', [(i, i ^ step) for i in range(gx)])  8.5 us
    pallas_call x1, Pallas kernels, body(): pl.pallas_call(functools.partial(logits_kernel, rows, cols, chans, slots,...  4.8 us
  transfers between devices with their start and end apart: 11, of which 7 were waited for; matrix products, arithmetic and copies ran while one was open for 0% of the time, Pallas kernels for 68%

profile of v1, /device:TPU:0, one launch (start us, length us, event | category | flops | bytes accessed | tf_op | source)
XLA Modules:
  0.0 214.3 jit_solution(14388649269942351330)
XLA Ops:
  0.6 1.3 copy.16.bias_ref
  2.0 4.8 %logits.1 = (f32[768,128]{1,0:T(8,128)}, f32[64,128]{1,0:T(8,128)}, f32[24,128]{1,0:T(8,128)}, f32[24,128]{1,0:T(8,128)}) custom-call(bf16[16,64,1280]{2,1,0:T(8,128)(2,1)} %f_ref.3, bf16[32,1280]{1,0:T(8,128)(2,1)} %bitcast.5, f32[32,1]{1,0:T(8,128)} %copy.16.bias_ref, s32[224,896]{1,0:T(8,128)} %lab_ref.1, s32[224,896]{1,0:T(8,128)} %lab_ref.1, ...), custom_call_target="tpu_custom_call" | custom-call | tf_op jit(solution)/shard_map/logits/pallas_call | solution.py:459
  6.8 0.5 collective-permute-start
  7.3 2.6 %collective-permute-start.1 = (f32[24,128]{1,0:T(8,128)}, f32[24,128]{1,0:T(8,128)S(1)}, u32[]{:S(2)}, u32[]{:S(2)}) collective-permute-start(f32[24,128]{1,0:T(8,128)} %get-tuple-element.25.sa_ref), channel_id=1, source_target_pairs={{0,2},{2,0},{4,6},{6,4},{8,10},{10,8},{12,14},{14,12},{1,3},{3,1},... | collective-permute-start | bytes 36872 | tf_op jit(solution)/shard_map/ppermute | solution.py:471
  9.8 0.7 collective-permute-start.2
  10.5 1.2 collective-permute-done.1.ra_ref
  11.7 0.0 collective-permute-start.3
  11.7 0.0 collective-permute-done.2.rb_ref
  11.7 0.5 collective-permute-start.4
  12.3 0.6 copy-done.7
  12.8 145.6 %inner.1 = (f32[768,128]{1,0:T(8,128)}, f32[8,128]{1,0:T(8,128)}, bf16[768,256]{1,0:T(8,128)(2,1)}, f32[1]{0:T(128)}) custom-call(f32[768,128]{1,0:T(8,128)} %get-tuple-element.19.x_ref, f32[64,128]{1,0:T(8,128)} %get-tuple-element.20.own_ref, f32[64,128]{1,0:T(8,128)} %copy-done.7, bf16[256,896]{1,0:T(8,128)(2,1)} %constant.14.clone.table_ref, ...), custom_call_target="tpu_custom_call" | custom-call | flops 2000000000 | bytes 4000000 | tf_op jit(solution)/shard_map/inner/pallas_call | solution.py:481
  158.5 0.0 copy-start.5
  158.6 0.6 copy-done.5
  159.1 0.0 copy-done.6
  159.2 23.4 %edge.1 = (f32[768,128]{1,0:T(8,128)}, f32[64,128]{1,0:T(8,128)}, f32[8,128]{1,0:T(8,128)}) custom-call(f32[1]{0:T(128)} %get-tuple-element.21.floor_ref, bf16[768,256]{1,0:T(8,128)(2,1)} %get-tuple-element.22.stack_ref, f32[768,128]{1,0:T(8,128)} %get-tuple-element.23.acc_ref, f32[8,128]{1,0:T(8,128)} %get-tuple-element.24.loss_in_ref, ...), custom_call_target="tpu_custom_call" | custom-call | tf_op jit(solution)/shard_map/edge/pallas_call | solution.py:500
  182.6 0.1 collective-permute-start.5
  183.3 0.7 collective-permute-done.5.got_ref
  184.0 0.6 copy-done.2
  184.6 4.1 %grad.1 = (f32[32,768]{1,0:T(8,128)}, f32[32,768]{1,0:T(8,128)}) custom-call(bf16[16,64,1280]{2,1,0:T(8,128)(2,1)} %f_ref.3, f32[768,128]{1,0:T(8,128)} %get-tuple-element.27.g_ref, f32[64,128]{1,0:T(8,128)} %get-tuple-element.28.own_ref, f32[64,128]{1,0:T(8,128)} %copy-done.2, f32[8,128]{1,0:T(8,128)} %get-tuple-element.29.loss_ref, s32[1,1]{1,0:T(1,128)S(6)} %copy.17.count_ref), custom_call_target="tpu_custom_call" | custom-call | tf_op jit(solution)/shard_map/grad/pallas_call | solution.py:512
  188.6 0.2 collective-permute-start.6
  188.8 1.4 collective-permute-done.6
  190.2 0.9 add.12
  191.1 4.6 %collective-permute-start.7 = (f32[32,768]{1,0:T(8,128)S(1)}, f32[32,768]{1,0:T(8,128)S(1)}, u32[]{:S(2)}, u32[]{:S(2)}) collective-permute-start(f32[32,768]{1,0:T(8,128)S(1)} %add.12), channel_id=1, source_target_pairs={{0,2},{2,0},{4,6},{6,4},{8,10},{10,8},{12,14},{14,12},{1,3},{3,1},... | collective-permute-start | bytes 294920 | tf_op jit(solution)/shard_map/ppermute | solution.py:528
  195.7 3.3 %collective-permute-done.7 = f32[32,768]{1,0:T(8,128)S(1)} collective-permute-done((f32[32,768]{1,0:T(8,128)S(1)}, f32[32,768]{1,0:T(8,128)S(1)}, u32[]{:S(2)}, u32[]{:S(2)}) %collective-permute-start.7) | collective-permute-done | bytes 98336 | tf_op jit(solution)/shard_map/ppermute | solution.py:528
  199.0 3.3 %collective-permute-start.8 = (f32[32,768]{1,0:T(8,128)S(1)}, f32[32,768]{1,0:T(8,128)S(1)}, u32[]{:S(2)}, u32[]{:S(2)}) collective-permute-start(f32[32,768]{1,0:T(8,128)S(1)} %add.13), channel_id=1, source_target_pairs={{0,4},{2,6},{4,0},{6,2},{8,12},{10,14},{12,8},{14,10},{1,5},{3,7},... | collective-permute-start | bytes 294920 | tf_op jit(solution)/shard_map/ppermute | solution.py:528
  202.3 2.6 %collective-permute-done.8 = f32[32,768]{1,0:T(8,128)S(1)} collective-permute-done((f32[32,768]{1,0:T(8,128)S(1)}, f32[32,768]{1,0:T(8,128)S(1)}, u32[]{:S(2)}, u32[]{:S(2)}) %collective-permute-start.8) | collective-permute-done | bytes 98336 | tf_op jit(solution)/shard_map/ppermute | solution.py:528
  204.9 3.1 %collective-permute-start.9 = (f32[32,768]{1,0:T(8,128)S(1)}, f32[32,768]{1,0:T(8,128)S(1)}, u32[]{:S(2)}, u32[]{:S(2)}) collective-permute-start(f32[32,768]{1,0:T(8,128)S(1)} %add.14), channel_id=1, source_target_pairs={{0,8},{2,10},{4,12},{6,14},{8,0},{10,2},{12,4},{14,6},{1,9},{3,11}... | collective-permute-start | bytes 294920 | tf_op jit(solution)/shard_map/ppermute | solution.py:528
  208.0 2.6 %collective-permute-done.9 = f32[32,768]{1,0:T(8,128)S(1)} collective-permute-done((f32[32,768]{1,0:T(8,128)S(1)}, f32[32,768]{1,0:T(8,128)S(1)}, u32[]{:S(2)}, u32[]{:S(2)}) %collective-permute-start.9) | collective-permute-done | bytes 98336 | tf_op jit(solution)/shard_map/ppermute | solution.py:528
  210.6 0.1 collective-permute-start.10
  210.7 1.3 collective-permute-done.10.z_ref
  212.0 0.6 copy-done.1
  212.6 1.7 final.1
  (16 shorter events, 0.1 us)
Async XLA Ops:
  6.8 5.5 %collective-permute-start = (f32[64,128]{1,0:T(8,128)}, f32[64,128]{1,0:T(8,128)S(1)}, u32[]{:S(2)}, u32[]{:S(2)}) collective-permute-start(f32[64,128]{1,0:T(8,128)} %get-tuple-element.20.own_ref), channel_id=1, source_target_pairs={{0,1},{1,0},{2,3},{3,2},{4,5},{5,4},{6,7},{7,6},{8,9},{9,8},{10,11... | collective-permute-start | bytes 98312 | tf_op jit(solution)/shard_map/ppermute | solution.py:468
  7.3 4.5 %collective-permute-start.1 = (f32[24,128]{1,0:T(8,128)}, f32[24,128]{1,0:T(8,128)S(1)}, u32[]{:S(2)}, u32[]{:S(2)}) collective-permute-start(f32[24,128]{1,0:T(8,128)} %get-tuple-element.25.sa_ref), channel_id=1, source_target_pairs={{0,2},{2,0},{4,6},{6,4},{8,10},{10,8},{12,14},{14,12},{1,3},{3,1},... | collective-permute-start | bytes 36872 | tf_op jit(solution)/shard_map/ppermute | solution.py:471
  9.8 1.9 collective-permute-start.2
  11.7 146.8 %copy-start.3 = (f32[24,128]{1,0:T(8,128)}, f32[24,128]{1,0:T(8,128)S(1)}, u32[]{:S(2)}) copy-start(f32[24,128]{1,0:T(8,128)S(1)} %collective-permute-done.1.ra_ref) | copy-start | bytes 36868
  11.7 146.8 %collective-permute-start.3 = (f32[24,128]{1,0:T(8,128)S(1)}, f32[24,128]{1,0:T(8,128)S(1)}, u32[]{:S(2)}, u32[]{:S(2)}) collective-permute-start(f32[24,128]{1,0:T(8,128)S(1)} %collective-permute-done.1.ra_ref), channel_id=1, source_target_pairs={{0,1},{1,0},{2,3},{3,2},{4,5},{5,4},{6,7},{7,6},{8,9},{9,8},{10,11... | collective-permute-start | bytes 36872 | tf_op jit(solution)/shard_map/ppermute | solution.py:468
  11.7 146.8 %copy-start.4 = (f32[24,128]{1,0:T(8,128)}, f32[24,128]{1,0:T(8,128)S(1)}, u32[]{:S(2)}) copy-start(f32[24,128]{1,0:T(8,128)S(1)} %collective-permute-done.2.rb_ref) | copy-start | bytes 36868
  11.7 146.8 %collective-permute-start.4 = (f32[24,128]{1,0:T(8,128)S(1)}, f32[24,128]{1,0:T(8,128)S(1)}, u32[]{:S(2)}, u32[]{:S(2)}) collective-permute-start(f32[24,128]{1,0:T(8,128)S(1)} %collective-permute-done.2.rb_ref), channel_id=1, source_target_pairs={{0,1},{1,0},{2,3},{3,2},{4,5},{5,4},{6,7},{7,6},{8,9},{9,8},{10,11... | collective-permute-start | bytes 36872 | tf_op jit(solution)/shard_map/ppermute | solution.py:468
  12.2 0.6 copy-start.7
  158.5 0.6 copy-start.5
  158.6 0.6 copy-start.6
  182.6 1.4 collective-permute-start.5
  184.0 0.6 copy-start.2
  188.6 1.5 collective-permute-start.6
  191.1 8.0 %collective-permute-start.7 = (f32[32,768]{1,0:T(8,128)S(1)}, f32[32,768]{1,0:T(8,128)S(1)}, u32[]{:S(2)}, u32[]{:S(2)}) collective-permute-start(f32[32,768]{1,0:T(8,128)S(1)} %add.12), channel_id=1, source_target_pairs={{0,2},{2,0},{4,6},{6,4},{8,10},{10,8},{12,14},{14,12},{1,3},{3,1},... | collective-permute-start | bytes 294920 | tf_op jit(solution)/shard_map/ppermute | solution.py:528
  199.0 5.9 %collective-permute-start.8 = (f32[32,768]{1,0:T(8,128)S(1)}, f32[32,768]{1,0:T(8,128)S(1)}, u32[]{:S(2)}, u32[]{:S(2)}) collective-permute-start(f32[32,768]{1,0:T(8,128)S(1)} %add.13), channel_id=1, source_target_pairs={{0,4},{2,6},{4,0},{6,2},{8,12},{10,14},{12,8},{14,10},{1,5},{3,7},... | collective-permute-start | bytes 294920 | tf_op jit(solution)/shard_map/ppermute | solution.py:528
  204.9 5.7 %collective-permute-start.9 = (f32[32,768]{1,0:T(8,128)S(1)}, f32[32,768]{1,0:T(8,128)S(1)}, u32[]{:S(2)}, u32[]{:S(2)}) collective-permute-start(f32[32,768]{1,0:T(8,128)S(1)} %add.14), channel_id=1, source_target_pairs={{0,8},{2,10},{4,12},{6,14},{8,0},{10,2},{12,4},{14,6},{1,9},{3,11}... | collective-permute-start | bytes 294920 | tf_op jit(solution)/shard_map/ppermute | solution.py:528
  210.6 1.4 copy-start
  210.6 1.4 collective-permute-start.10
  212.0 0.6 copy-start.1

commit v2 on v1

--- a/solution.py
+++ b/solution.py
@@ -20,6 +20,8 @@
 f32 = jnp.float32
 bf16 = jnp.bfloat16
 VMEM = pl.BlockSpec(memory_space=pltpu.VMEM)
+ANY = pl.BlockSpec(memory_space=pl.ANY)
+ROOM = pltpu.CompilerParams(vmem_limit_bytes=16 * 2**20)
 SMEM = pl.BlockSpec(memory_space=pltpu.SMEM)
 
 
@@ -64,69 +66,72 @@
 
 
 def logits_kernel(
-    rows, cols, chans, slots, per, f_ref, w_ref, bias_ref, ll_ref, lr_ref, ml_ref, mr_ref, sel_ref,
-    x_ref, e_ref, sa_ref, sb_ref,
+    rows, cols, chans, slots, per, f_ref, w_ref, bias_ref, lab_ref, mask_ref, sel_ref,
+    x_ref, e_ref, sa_ref, sb_ref, keep_ref, strip_ref, f_sem, s_sem,
 ):
-    step = pl.program_id(0)
-    steps = pl.num_programs(0)
-
-    @pl.when(step == 0)
-    def _():
-        x_ref[...] = jnp.zeros_like(x_ref)
-
-    block = f_ref[...].reshape(per * cols, f_ref.shape[2])
-    score = lax.dot_general(w_ref[...], block, (((1,), (1,)), ((), ())), preferred_element_type=f32)
-    score = score + bias_ref[...]
-    score = (score - jnp.max(score, axis=0, keepdims=True)) * (LOG2E / STEP)
+    steps = rows // per
+    tail = lab_ref.shape[1] - LANES
+    loads = [
+        pltpu.make_async_copy(f_ref.at[pl.ds(k * per, per)], keep_ref.at[pl.ds(k * per, per)], f_sem.at[k])
+        for k in range(steps)
+    ]
+    strips = [
+        pltpu.make_async_copy(ref.at[:, pl.ds(at, LANES)], strip_ref.at[k], s_sem.at[k])
+        for k, (ref, at) in enumerate(((lab_ref, 0), (mask_ref, 0), (lab_ref, tail), (mask_ref, tail)))
+    ]
+    for copy in strips + loads:
+        copy.start()
+    x_ref[...] = jnp.zeros_like(x_ref)
+    bias = jnp.concatenate([bias_ref[...], jnp.zeros((1, LANES - chans), f32)], axis=1)
+    bias = jnp.broadcast_to(bias, (LANES, LANES)).T[0:chans, :]
+    bias = jnp.concatenate([bias] * (per * cols // LANES), axis=1)
+    at = lax.broadcasted_iota(jnp.int32, (SUB, LANES), 1)
+    even = lax.rem(lax.axis_index("gx"), 2) == 0
+    for copy in strips:
+        copy.wait()
+    for b in range(rows // SUB):
+        left = jnp.full((SUB, LANES), -1.0, f32)
+        right = left
+        for j in range(PATCH):
+            pick = pl.ds(b * SUB * PATCH + j, SUB, stride=PATCH)
+            here = (at >= j * HALF) & (at < j * HALF + HALF)
+            lab = jnp.where(strip_ref[1, pick, :] != 0, strip_ref[0, pick, :], -1).astype(f32)
+            shift = j * HALF
+            left = jnp.where(here, pltpu.roll(lab, shift, 1) if shift else lab, left)
+            lab = jnp.where(strip_ref[3, pick, :] != 0, strip_ref[2, pick, :], -1).astype(f32)
+            right = jnp.where(here, pltpu.roll(lab, (shift + HALF) % LANES, 1), right)
+        sa_ref[b * SUB : b * SUB + SUB, :] = jnp.where(even, right, left)
+        sb_ref[b * SUB : b * SUB + SUB, :] = jnp.where(even, left, right)
     lane = lax.broadcasted_iota(jnp.int32, (chans, LANES), 1)
-    for k in range(per):
-        at = k * cols
-        tile = score[:, at // LANES * LANES : at // LANES * LANES + LANES]
-        if at % LANES:
-            tile = pltpu.roll(tile, LANES - at % LANES, 1)
-        tile = jnp.where(lane < cols, tile, 0.0)
-        x_ref[pl.ds(step * per + k + 1, chans, stride=slots), :] = tile
-        if k == 0:
-
-            @pl.when(step == 0)
-            def _():
+    for step in range(steps):
+        loads[step].wait()
+        block = keep_ref[step * per : step * per + per].reshape(per * cols, f_ref.shape[2])
+        score = lax.dot_general(w_ref[...], block, (((1,), (1,)), ((), ())), preferred_element_type=f32)
+        score = score + bias
+        score = (score - jnp.max(score, axis=0, keepdims=True)) * (LOG2E / STEP)
+        for k in range(per):
+            off = k * cols
+            tile = score[:, off // LANES * LANES : off // LANES * LANES + LANES]
+            if off % LANES:
+                tile = pltpu.roll(tile, LANES - off % LANES, 1)
+            tile = jnp.where(lane < cols, tile, 0.0)
+            x_ref[pl.ds(step * per + k + 1, chans, stride=slots), :] = tile
+            if step == 0 and k == 0:
                 e_ref[0:chans, :] = tile
-
-        if k == per - 1:
-
-            @pl.when(step == steps - 1)
-            def _():
+            if step == steps - 1 and k == per - 1:
                 e_ref[chans : 2 * chans, :] = tile
-
-    @pl.when(step == steps - 1)
-    def _():
-        edges = lax.dot_general(
-            sel_ref[...], stack3(x_ref[...], cols), (((1,), (1,)), ((), ())), preferred_element_type=f32
-        )
-        at = lax.broadcasted_iota(jnp.int32, (SUB, LANES), 1)
-        even = lax.rem(lax.axis_index("gx"), 2) == 0
-        n = chans * slots // LANES
-        for b in range(rows // SUB):
-            left = jnp.full((SUB, LANES), -1.0, f32)
-            right = left
-            for j in range(PATCH):
-                pick = pl.ds(b * SUB * PATCH + j, SUB, stride=PATCH)
-                here = (at >= j * HALF) & (at < j * HALF + HALF)
-                lab = jnp.where(ml_ref[pick, :] != 0, ll_ref[pick, :], -1).astype(f32)
-                shift = j * HALF
-                left = jnp.where(here, pltpu.roll(lab, shift, 1) if shift else lab, left)
-                lab = jnp.where(mr_ref[pick, :] != 0, lr_ref[pick, :], -1).astype(f32)
-                right = jnp.where(here, pltpu.roll(lab, (shift + HALF) % LANES, 1), right)
-            sa_ref[b * SUB : b * SUB + SUB, :] = jnp.where(even, right, left)
-            sb_ref[b * SUB : b * SUB + SUB, :] = jnp.where(even, left, right)
-        for r in range(n):
-            part = edges[:, r * LANES : r * LANES + LANES]
-            sa_ref[rows + r : rows + r + 1, :] = jnp.where(even, part[1:2], part[0:1])
-            sb_ref[rows + r : rows + r + 1, :] = jnp.where(even, part[0:1], part[1:2])
-        pad = sa_ref.shape[0] - rows - n
-        if pad:
-            sa_ref[rows + n :, :] = jnp.zeros((pad, LANES), f32)
-            sb_ref[rows + n :, :] = jnp.zeros((pad, LANES), f32)
+    edges = lax.dot_general(
+        sel_ref[...], stack3(x_ref[...], cols), (((1,), (1,)), ((), ())), preferred_element_type=f32
+    )
+    n = chans * slots // LANES
+    for r in range(n):
+        part = edges[:, r * LANES : r * LANES + LANES]
+        sa_ref[rows + r : rows + r + 1, :] = jnp.where(even, part[1:2], part[0:1])
+        sb_ref[rows + r : rows + r + 1, :] = jnp.where(even, part[0:1], part[1:2])
+    pad = sa_ref.shape[0] - rows - n
+    if pad:
+        sa_ref[rows + n :, :] = jnp.zeros((pad, LANES), f32)
+        sb_ref[rows + n :, :] = jnp.zeros((pad, LANES), f32)
 
 
 def softmax_fast(groups, chans, slots, up, w_ref, p_ref):
@@ -348,65 +353,56 @@
 
 
 def grad_kernel(
-    rows, cols, chans, slots, per, f_ref, g_ref, own_ref, got_ref, loss_ref, count_ref,
-    mine_ref, other_ref, sum_ref, acc_ref,
+    rows, cols, chans, slots, f_ref, g_ref, own_ref, got_ref, loss_ref, count_ref, mine_ref, other_ref, sum_ref,
 ):
-    step = pl.program_id(0)
     row = lax.axis_index("gy")
-
-    @pl.when(step == 0)
-    def _():
-        sum_ref[...] = g_ref[...]
-        last = row == lax.axis_size("gy") - 1
-        top = jnp.where(row == 0, own_ref[0:chans, :], got_ref[chans : 2 * chans, :])
-        bottom = jnp.where(last, own_ref[chans : 2 * chans, :], got_ref[0:chans, :])
-        sum_ref[pl.ds(1, chans, stride=slots), :] += top
-        sum_ref[pl.ds(rows, chans, stride=slots), :] += bottom
-        acc_ref[...] = jnp.zeros_like(acc_ref)
-
+    sum_ref[...] = g_ref[...]
+    last = row == lax.axis_size("gy") - 1
+    top = jnp.where(row == 0, own_ref[0:chans, :], got_ref[chans : 2 * chans, :])
+    bottom = jnp.where(last, own_ref[chans : 2 * chans, :], got_ref[0:chans, :])
+    sum_ref[pl.ds(1, chans, stride=slots), :] += top
+    sum_ref[pl.ds(rows, chans, stride=slots), :] += bottom
     lane = lax.broadcasted_iota(jnp.int32, (chans, LANES), 1)
     share = LANES // cols
     tiles = []
-    for k in range(0, per, share):
+    total = jnp.zeros((chans, LANES), f32)
+    for k in range(0, rows, share):
         tile = None
         for r in range(share):
-            piece = sum_ref[pl.ds(step * per + k + r + 1, chans, stride=slots), :]
+            piece = sum_ref[pl.ds(k + r + 1, chans, stride=slots), :]
+            total = total + piece
             if r:
                 piece = pltpu.roll(piece, r * cols, 1)
             tile = piece if tile is None else jnp.where(lane < r * cols, tile, piece)
         tiles.append(tile.astype(bf16))
-    block = f_ref[...].reshape(per * cols, f_ref.shape[2])
-    acc_ref[...] += jnp.dot(jnp.concatenate(tiles, axis=1), block, preferred_element_type=f32)
-
-    @pl.when(step == pl.num_programs(0) - 1)
-    def _():
-        total = sum_ref[pl.ds(1, chans, stride=slots), :]
-        for i in range(2, rows + 1):
-            total = total + sum_ref[pl.ds(i, chans, stride=slots), :]
-        total = jnp.where(lane < cols, total, 0.0)
-        square = jnp.concatenate([total, jnp.zeros((LANES - chans, LANES), f32)], axis=0)
-        bias = jnp.sum(square.T, axis=0, keepdims=True)
-        at = lax.broadcasted_iota(jnp.int32, (SUB, LANES), 0)
-        rest = jnp.where(at == 1, jnp.sum(loss_ref[...]), count_ref[0, 0].astype(f32))
-        stats = jnp.where(at == 0, bias, jnp.where(at < 3, rest, 0.0))
-        half = acc_ref.shape[1] // 2
-        low, high = acc_ref[:, 0:half], acc_ref[:, half:]
-        mine_ref[:, 0:half] = jnp.where(row == 0, low, high)
-        other_ref[:, 0:half] = jnp.where(row == 0, high, low)
-        for ref in (mine_ref, other_ref):
-            ref[0:SUB, half:] = stats
-            ref[SUB:, half:] = jnp.zeros((chans - SUB, LANES), f32)
-
-
-def final_kernel(y_ref, z_ref, loss_ref, weight_ref, bias_ref):
-    chans = y_ref.shape[0]
-    half = y_ref.shape[1] - LANES
+    block = f_ref[...].reshape(rows * cols, f_ref.shape[2])
+    out = jnp.dot(jnp.concatenate(tiles, axis=1), block, preferred_element_type=f32)
+    total = jnp.where(lane < cols, total, 0.0)
+    square = jnp.concatenate([total, jnp.zeros((LANES - chans, LANES), f32)], axis=0)
+    bias = jnp.sum(square.T, axis=0, keepdims=True)
+    at = lax.broadcasted_iota(jnp.int32, (SUB, LANES), 0)
+    rest = jnp.where(at == 1, jnp.sum(loss_ref[...]), count_ref[0, 0].astype(f32))
+    stats = jnp.where(at == 0, bias, jnp.where(at < 3, rest, 0.0))
+    pieces = out.shape[1] // LANES // 2
+    for k in range(pieces):
+        low = out[:, k * LANES : k * LANES + LANES]
+        high = out[:, (pieces + k) * LANES : (pieces + k + 1) * LANES]
+        mine_ref[k * chans : k * chans + chans, :] = jnp.where(row == 0, low, high)
+        other_ref[k * chans : k * chans + chans, :] = jnp.where(row == 0, high, low)
+    mine_ref[pieces * chans :, :] = stats
+    other_ref[pieces * chans :, :] = stats
+
+
+def final_kernel(chans, y_ref, z_ref, loss_ref, weight_ref, bias_ref):
+    pieces = y_ref.shape[0] // chans
     lower = lax.axis_index("gy") == 0
-    y, z = y_ref[:, 0:half], z_ref[:, 0:half]
-    stats = y_ref[0:SUB, half:]
+    stats = y_ref[pieces * chans :, :]
     total = stats[2:3, 0:1]
-    weight_ref[:, 0:half] = jnp.where(lower, y, z) / total
-    weight_ref[:, half:] = jnp.where(lower, z, y) / total
+    for k in range(pieces):
+        y = y_ref[k * chans : k * chans + chans, :]
+        z = z_ref[k * chans : k * chans + chans, :]
+        weight_ref[:, k * LANES : k * LANES + LANES] = jnp.where(lower, y, z) / total
+        weight_ref[:, (pieces + k) * LANES : (pieces + k + 1) * LANES] = jnp.where(lower, z, y) / total
     loss_ref[...] = stats[1:2, 0:1] / total
     bias_ref[...] = stats[0:1, 0:chans] / total
 
@@ -452,18 +448,26 @@
 
     per = 4
     shape = lambda *dims: jax.ShapeDtypeStruct(dims, f32)
+    held = lambda *dims, kind=f32: pltpu.VMEM(dims, kind)
+    here = lambda v: pltpu.with_memory_space_constraint(v, pltpu.VMEM)
     strip = -(-(rows + chans * slots // LANES) // SUB) * SUB
-    block = pl.BlockSpec((per, cols, width), lambda i: (i, 0, 0))
-    tail = pl.BlockSpec((tall, LANES), lambda i: (0, tiles - 1))
-    head = pl.BlockSpec((tall, LANES), lambda i: (0, 0))
-    x, edge, send_a, send_b = pl.pallas_call(
+    tall_x = chans * slots
+    x, edge, send_a, send_b, kept = pl.pallas_call(
         functools.partial(logits_kernel, rows, cols, chans, slots, per),
-        grid=(rows // per,),
-        in_specs=[block, whole((chans, width)), whole((chans, 1)), head, tail, head, tail, whole((SUB, depth))],
-        out_specs=[whole((chans * slots, LANES)), whole((2 * chans, LANES)), whole((strip, LANES)), whole((strip, LANES))],
-        out_shape=[shape(chans * slots, LANES), shape(2 * chans, LANES), shape(strip, LANES), shape(strip, LANES)],
+        in_specs=[ANY, VMEM, VMEM, ANY, ANY, VMEM],
+        out_specs=[VMEM] * 5,
+        out_shape=[
+            held(tall_x, LANES), held(2 * chans, LANES), held(strip, LANES), held(strip, LANES),
+            held(rows, cols, width, kind=bf16),
+        ],
+        scratch_shapes=[
+            pltpu.VMEM((4, tall, LANES), jnp.int32),
+            pltpu.SemaphoreType.DMA((rows // per,)),
+            pltpu.SemaphoreType.DMA((4,)),
+        ],
+        compiler_params=ROOM,
         name="logits",
-    )(features, probe_weight.T, probe_bias.reshape(chans, 1), labels, labels, valid_mask, valid_mask, ends)
+    )(features, probe_weight.T, probe_bias.reshape(1, chans), labels, valid_mask, ends)
 
     swap = lambda v: lax.ppermute(v, "gy", [(0, 1), (1, 0)])
     pairs = lambda at: [p for i in range(at, gx - 1, 2) for p in ((i, i + 1), (i + 1, i))]
@@ -472,9 +476,9 @@
     got_b = lax.ppermute(send_b, "gx", pairs(1))
 
     scratch = [
-        pltpu.VMEM((chans * slots, LANES), f32),
+        pltpu.VMEM((tall_x, LANES), f32),
         pltpu.VMEM((chans * count, SUB, LANES), f32),
-        pltpu.VMEM((chans * slots, LANES), f32),
+        pltpu.VMEM((tall_x, LANES), f32),
         pltpu.VMEM((count + 1, SUB, LANES), f32),
     ]
     column = pl.BlockSpec((tall, LANES), lambda t: (0, t))
@@ -482,45 +486,43 @@
         functools.partial(inner_kernel, cols, chans, slots, groups),
         grid=(tiles,),
         in_specs=[
-            whole((chans * slots, LANES)), whole((2 * chans, LANES)), whole((2 * chans, LANES)),
+            VMEM, VMEM, VMEM,
             pl.BlockSpec((depth, LANES), lambda t: (0, t)), pl.BlockSpec((depth, LANES), lambda t: (t, 0)),
             column, column,
         ],
-        out_specs=[whole((chans * slots, LANES)), whole((SUB, LANES)), whole((chans * slots, depth)), SMEM],
-        out_shape=[
-            shape(chans * slots, LANES), shape(SUB, LANES),
-            jax.ShapeDtypeStruct((chans * slots, depth), bf16), shape(1),
-        ],
-        scratch_shapes=scratch + [pltpu.VMEM((chans * slots, LANES), f32)],
+        out_specs=[VMEM, VMEM, VMEM, SMEM],
+        out_shape=[held(tall_x, LANES), held(SUB, LANES), held(tall_x, depth, kind=bf16), shape(1)],
+        scratch_shapes=scratch + [pltpu.VMEM((tall_x, LANES), f32)],
         cost_estimate=pl.CostEstimate(flops=2 * 10**9, bytes_accessed=4 * 10**6, transcendentals=10**6),
+        compiler_params=ROOM,
         name="inner",
-    )(x, edge, got, lift, back, labels, valid_mask)
+    )(here(x), here(edge), here(got), lift, back, labels, valid_mask)
 
     far_a, far_b = swap(got_a), swap(got_b)
     grad, spill, loss = pl.pallas_call(
         functools.partial(edge_kernel, rows, cols, chans, slots, groups),
         in_specs=[SMEM] + [VMEM] * 13,
         out_specs=[VMEM] * 3,
-        out_shape=[shape(chans * slots, LANES), shape(2 * chans, LANES), shape(SUB, LANES)],
+        out_shape=[held(tall_x, LANES), held(2 * chans, LANES), held(SUB, LANES)],
         scratch_shapes=scratch,
+        compiler_params=ROOM,
         name="edge",
-    )(floor, stack, acc, loss, send_a, send_b, got_a, got_b, far_a, far_b, own_f, fold, own_b, sides)
+    )(
+        floor, *(here(v) for v in (stack, acc, loss, send_a, send_b, got_a, got_b, far_a, far_b)),
+        own_f, fold, own_b, sides,
+    )
 
     got = swap(spill)
-    half = width // 2
-    part = whole((chans, half + LANES))
+    pack = (chans * width // 2 // LANES + SUB, LANES)
     mine, other = pl.pallas_call(
-        functools.partial(grad_kernel, rows, cols, chans, slots, per),
-        grid=(rows // per,),
-        in_specs=[
-            block, whole((chans * slots, LANES)), whole((2 * chans, LANES)), whole((2 * chans, LANES)),
-            whole((SUB, LANES)), SMEM,
-        ],
-        out_specs=[part, part],
-        out_shape=[shape(chans, half + LANES)] * 2,
-        scratch_shapes=[pltpu.VMEM((chans * slots, LANES), f32), pltpu.VMEM((chans, width), f32)],
+        functools.partial(grad_kernel, rows, cols, chans, slots),
+        in_specs=[VMEM] * 5 + [SMEM],
+        out_specs=[VMEM] * 2,
+        out_shape=[held(*pack)] * 2,
+        scratch_shapes=[pltpu.VMEM((tall_x, LANES), f32)],
+        compiler_params=ROOM,
         name="grad",
-    )(features, grad, spill, got, loss, valid_count)
+    )(*(here(v) for v in (kept, grad, spill, got, loss)), valid_count)
 
     total = mine + swap(other)
     step = 1
@@ -528,12 +530,13 @@
         total = total + lax.ppermute(total, "gx", [(i, i ^ step) for i in range(gx)])
         step *= 2
     loss, weight, bias = pl.pallas_call(
-        final_kernel,
+        functools.partial(final_kernel, chans),
         in_specs=[VMEM] * 2,
         out_specs=[VMEM] * 3,
         out_shape=[shape(1, 1), shape(chans, width), shape(1, chans)],
+        compiler_params=ROOM,
         name="final",
-    )(total, swap(total))
+    )(here(total), here(swap(total)))
     return loss.reshape(1), weight.T, bias.reshape(chans)
 
 

time: 215 us -> 206 us (0.958)
  Pallas kernels: 180 us -> 170 us
  local copies, waits for them, and re-layouts: 3.78 us -> 6.28 us
    pallas_call x2, Pallas kernels: 5.71 us -> 1.3 us  [the longest x1 0.72 us: body(): pl.pallas_call(functools.partial(final_kernel, chans), in_specs=[VMEM] *...]
    unnamed x16 -> x28, local copies, waits for them, and re-layouts: 2.44 us -> 6.28 us
  transfers between devices with their start and end apart: 11 -> 11, of which waited for: 7 -> 7; matrix products, arithmetic and copies ran while one was open for 0% -> 0% of each run, Pallas kernels for 68% -> 70%
where the time goes in v2:
time: 206 us; the launch traced here: 205 us
  Pallas kernels  170 us (83%)
  starting transfers between devices  15.7 us (8%)
  waiting for transfers between devices  11.9 us (6%)
  local copies, waits for them, and re-layouts  6.28 us (3%)
    pallas_call x1, Pallas kernels, body(): pl.pallas_call(functools.partial(inner_kernel, cols, chans, slots, groups...  144 us
    pallas_call x1, Pallas kernels, body(): pl.pallas_call(functools.partial(edge_kernel, rows, cols, chans, slots, g...  21.3 us
    ppermute x3, starting transfers between devices, body(): lax.ppermute(total, 'gx', [(i, i ^ step) for i in range(gx)])  11 us
    ppermute x3, waiting for transfers between devices, body(): lax.ppermute(total, 'gx', [(i, i ^ step) for i in range(gx)])  7.97 us
    unnamed x28, local copies, waits for them, and re-layouts  6.28 us
  transfers between devices with their start and end apart: 11, of which 7 were waited for; matrix products, arithmetic and copies ran while one was open for 0% of the time, Pallas kernels for 70%

profile of v2, /device:TPU:0, one launch (start us, length us, event | category | flops | bytes accessed | tf_op | source)
XLA Modules:
  0.0 205.4 jit_solution(4970205238752348120)
XLA Ops:
  0.6 1.7 copy-done
  2.4 1.1 copy-done.1
  3.5 1.1 copy-done.3
  4.7 0.9 copy-done.6
  5.5 0.7 copy-done.10
  6.2 0.7 copy-done.11
  6.9 3.7 %logits.1 = (f32[768,128]{1,0:T(8,128)S(1)}, f32[64,128]{1,0:T(8,128)S(1)}, f32[24,128]{1,0:T(8,128)S(1)}, f32[24,128]{1,0:T(8,128)S(1)}, bf16[16,64,1280]{2,1,0:T(8,128)(2,1)S(1)}) custom-call(bf16[16,64,1280]{2,1,0:T(8,128)(2,1)S(1)} %copy-done, bf16[32,1280]{1,0:T(8,128)(2,1)S(1)} %bitcast.5, f32[1,32]{1,0:T(1,128)S(1)} %bitcast.6, ...), custom_call_target="tpu_custom_call" | custom-call | tf_op jit(solution)/shard_map/logits/pallas_call | solution.py:455
  10.6 0.6 collective-permute-start
  11.1 2.6 %collective-permute-start.1 = (f32[24,128]{1,0:T(8,128)S(1)}, f32[24,128]{1,0:T(8,128)S(1)}, u32[]{:S(2)}, u32[]{:S(2)}) collective-permute-start(f32[24,128]{1,0:T(8,128)S(1)} %get-tuple-element.27.sa_ref), channel_id=1, source_target_pairs={{0,2},{2,0},{4,6},{6,4},{8,10},{10,8},{12,14},{14,12},{1,3},{3,1},... | collective-permute-start | bytes 36872 | tf_op jit(solution)/shard_map/ppermute | solution.py:475
  13.7 0.7 collective-permute-start.2
  14.4 1.0 collective-permute-done.1.ra_ref
  15.4 0.5 collective-permute-start.4
  15.9 0.0 copy-start.5
  15.9 0.0 copy-start.7
  16.0 0.0 copy-start.8
  16.0 0.0 copy-start.9
  16.0 143.7 %inner.1 = (f32[768,128]{1,0:T(8,128)S(1)}, f32[8,128]{1,0:T(8,128)S(1)}, bf16[768,256]{1,0:T(8,128)(2,1)S(1)}, f32[1]{0:T(128)}) custom-call(f32[768,128]{1,0:T(8,128)S(1)} %get-tuple-element.21.x_ref, f32[64,128]{1,0:T(8,128)S(1)} %get-tuple-element.22.own_ref, f32[64,128]{1,0:T(8,128)S(1)} %collective-permute-done.got_ref, ...), custom_call_target="tpu_custom_call" | custom-call | flops 2000000000 | bytes 4000000 | tf_op jit(solution)/shard_map/inner/pallas_call | solution.py:485
  159.8 21.3 %edge.1 = (f32[768,128]{1,0:T(8,128)S(1)}, f32[64,128]{1,0:T(8,128)S(1)}, f32[8,128]{1,0:T(8,128)S(1)}) custom-call(f32[1]{0:T(128)} %get-tuple-element.23.floor_ref, bf16[768,256]{1,0:T(8,128)(2,1)S(1)} %get-tuple-element.24.stack_ref, f32[768,128]{1,0:T(8,128)S(1)} %get-tuple-element.25.acc_ref, f32[8,128]{1,0:T(8,128)S(1)} %get-tuple-element.26.loss_in_ref, ...), custom_call_target="tpu_custom_call" | custom-call | tf_op jit(solution)/shard_map/edge/pallas_call | solution.py:502
  181.1 0.1 collective-permute-start.5
  181.8 0.5 collective-permute-done.5.got_ref
  182.3 0.6 grad.1
  182.9 0.2 collective-permute-start.6
  183.2 1.1 collective-permute-done.6
  184.3 4.6 %collective-permute-start.7 = (f32[168,128]{1,0:T(8,128)S(1)}, f32[168,128]{1,0:T(8,128)S(1)}, u32[]{:S(2)}, u32[]{:S(2)}) collective-permute-start(f32[168,128]{1,0:T(8,128)S(1)} %add.12), channel_id=1, source_target_pairs={{0,2},{2,0},{4,6},{6,4},{8,10},{10,8},{12,14},{14,12},{1,3},{3,1},... | collective-permute-start | bytes 258056 | tf_op jit(solution)/shard_map/ppermute | solution.py:530
  188.9 3.0 %collective-permute-done.7 = f32[168,128]{1,0:T(8,128)S(1)} collective-permute-done((f32[168,128]{1,0:T(8,128)S(1)}, f32[168,128]{1,0:T(8,128)S(1)}, u32[]{:S(2)}, u32[]{:S(2)}) %collective-permute-start.7) | collective-permute-done | bytes 86048 | tf_op jit(solution)/shard_map/ppermute | solution.py:530
  192.0 3.3 %collective-permute-start.8 = (f32[168,128]{1,0:T(8,128)S(1)}, f32[168,128]{1,0:T(8,128)S(1)}, u32[]{:S(2)}, u32[]{:S(2)}) collective-permute-start(f32[168,128]{1,0:T(8,128)S(1)} %add.13), channel_id=1, source_target_pairs={{0,4},{2,6},{4,0},{6,2},{8,12},{10,14},{12,8},{14,10},{1,5},{3,7},... | collective-permute-start | bytes 258056 | tf_op jit(solution)/shard_map/ppermute | solution.py:530
  195.2 2.5 %collective-permute-done.8 = f32[168,128]{1,0:T(8,128)S(1)} collective-permute-done((f32[168,128]{1,0:T(8,128)S(1)}, f32[168,128]{1,0:T(8,128)S(1)}, u32[]{:S(2)}, u32[]{:S(2)}) %collective-permute-start.8) | collective-permute-done | bytes 86048 | tf_op jit(solution)/shard_map/ppermute | solution.py:530
  197.7 3.1 %collective-permute-start.9 = (f32[168,128]{1,0:T(8,128)S(1)}, f32[168,128]{1,0:T(8,128)S(1)}, u32[]{:S(2)}, u32[]{:S(2)}) collective-permute-start(f32[168,128]{1,0:T(8,128)S(1)} %add.14), channel_id=1, source_target_pairs={{0,8},{2,10},{4,12},{6,14},{8,0},{10,2},{12,4},{14,6},{1,9},{3,11}... | collective-permute-start | bytes 258056 | tf_op jit(solution)/shard_map/ppermute | solution.py:530
  200.8 2.5 %collective-permute-done.9 = f32[168,128]{1,0:T(8,128)S(1)} collective-permute-done((f32[168,128]{1,0:T(8,128)S(1)}, f32[168,128]{1,0:T(8,128)S(1)}, u32[]{:S(2)}, u32[]{:S(2)}) %collective-permute-start.9) | collective-permute-done | bytes 86048 | tf_op jit(solution)/shard_map/ppermute | solution.py:530
  203.3 0.1 collective-permute-start.10
  203.4 1.3 collective-permute-done.10.z_ref
  204.7 0.7 final.1
  (27 shorter events, 0.1 us)
Async XLA Ops:
  0.6 1.7 copy-start
  2.4 1.1 copy-start.1
  3.5 1.1 copy-start.3
  4.7 0.9 copy-start.6
  5.5 0.7 copy-start.10
  6.2 0.7 copy-start.11
  6.9 9.0 %copy-start.2 = (s32[224,896]{1,0:T(8,128)S(1)}, s32[224,896]{1,0:T(8,128)}, u32[]{:S(2)}) copy-start(s32[224,896]{1,0:T(8,128)} %lab_ref.3) | copy-start | bytes 2408452
  6.9 9.0 %copy-start.4 = (s32[224,896]{1,0:T(8,128)S(1)}, s32[224,896]{1,0:T(8,128)}, u32[]{:S(2)}) copy-start(s32[224,896]{1,0:T(8,128)} %mask_ref.3) | copy-start | bytes 2408452
  6.9 9.0 %copy-start.12 = (bf16[256,896]{1,0:T(8,128)(2,1)S(1)}, bf16[256,896]{1,0:T(8,128)(2,1)}, u32[]{:S(2)}) copy-start(bf16[256,896]{1,0:T(8,128)(2,1)} %constant.14.clone.table_ref) | copy-start | bytes 1376260
  6.9 9.0 %copy-start.13 = (bf16[1792,128]{1,0:T(8,128)(2,1)S(1)}, bf16[1792,128]{1,0:T(8,128)(2,1)}, u32[]{:S(2)}) copy-start(bf16[1792,128]{1,0:T(8,128)(2,1)} %constant.15.clone.back_ref) | copy-start | bytes 1376260
  10.6 5.3 %collective-permute-start = (f32[64,128]{1,0:T(8,128)S(1)}, f32[64,128]{1,0:T(8,128)S(1)}, u32[]{:S(2)}, u32[]{:S(2)}) collective-permute-start(f32[64,128]{1,0:T(8,128)S(1)} %get-tuple-element.22.own_ref), channel_id=1, source_target_pairs={{0,1},{1,0},{2,3},{3,2},{4,5},{5,4},{6,7},{7,6},{8,9},{9,8},{10,11... | collective-permute-start | bytes 98312 | tf_op jit(solution)/shard_map/ppermute | solution.py:472
  11.1 4.3 %collective-permute-start.1 = (f32[24,128]{1,0:T(8,128)S(1)}, f32[24,128]{1,0:T(8,128)S(1)}, u32[]{:S(2)}, u32[]{:S(2)}) collective-permute-start(f32[24,128]{1,0:T(8,128)S(1)} %get-tuple-element.27.sa_ref), channel_id=1, source_target_pairs={{0,2},{2,0},{4,6},{6,4},{8,10},{10,8},{12,14},{14,12},{1,3},{3,1},... | collective-permute-start | bytes 36872 | tf_op jit(solution)/shard_map/ppermute | solution.py:475
  13.7 1.7 collective-permute-start.2
  15.4 144.3 %collective-permute-start.3 = (f32[24,128]{1,0:T(8,128)S(1)}, f32[24,128]{1,0:T(8,128)S(1)}, u32[]{:S(2)}, u32[]{:S(2)}) collective-permute-start(f32[24,128]{1,0:T(8,128)S(1)} %collective-permute-done.1.ra_ref), channel_id=1, source_target_pairs={{0,1},{1,0},{2,3},{3,2},{4,5},{5,4},{6,7},{7,6},{8,9},{9,8},{10,11... | collective-permute-start | bytes 36872 | tf_op jit(solution)/shard_map/ppermute | solution.py:472
  15.4 144.3 %collective-permute-start.4 = (f32[24,128]{1,0:T(8,128)S(1)}, f32[24,128]{1,0:T(8,128)S(1)}, u32[]{:S(2)}, u32[]{:S(2)}) collective-permute-start(f32[24,128]{1,0:T(8,128)S(1)} %collective-permute-done.2.rb_ref), channel_id=1, source_target_pairs={{0,1},{1,0},{2,3},{3,2},{4,5},{5,4},{6,7},{7,6},{8,9},{9,8},{10,11... | collective-permute-start | bytes 36872 | tf_op jit(solution)/shard_map/ppermute | solution.py:472
  15.9 143.8 %copy-start.5 = (bf16[1024,128]{1,0:T(8,128)(2,1)S(1)}, bf16[1024,128]{1,0:T(8,128)(2,1)}, u32[]{:S(2)}) copy-start(bf16[1024,128]{1,0:T(8,128)(2,1)} %constant.18.clone.fold_ref) | copy-start | bytes 786436
  15.9 143.8 %copy-start.7 = (bf16[256,128]{1,0:T(8,128)(2,1)S(1)}, bf16[256,128]{1,0:T(8,128)(2,1)}, u32[]{:S(2)}) copy-start(bf16[256,128]{1,0:T(8,128)(2,1)} %constant.16.clone.table_ref) | copy-start | bytes 196612
  16.0 143.8 %copy-start.8 = (bf16[256,128]{1,0:T(8,128)(2,1)S(1)}, bf16[256,128]{1,0:T(8,128)(2,1)}, u32[]{:S(2)}) copy-start(bf16[256,128]{1,0:T(8,128)(2,1)} %constant.17.clone.back_ref) | copy-start | bytes 196612
  16.0 143.8 %copy-start.9 = (bf16[16,128]{1,0:T(8,128)(2,1)S(1)}, bf16[16,128]{1,0:T(8,128)(2,1)}, u32[]{:S(2)}) copy-start(bf16[16,128]{1,0:T(8,128)(2,1)} %constant.19.clone.halo_ref) | copy-start | bytes 12292
  181.1 1.3 collective-permute-start.5
  182.9 1.3 collective-permute-start.6
  184.3 7.7 %collective-permute-start.7 = (f32[168,128]{1,0:T(8,128)S(1)}, f32[168,128]{1,0:T(8,128)S(1)}, u32[]{:S(2)}, u32[]{:S(2)}) collective-permute-start(f32[168,128]{1,0:T(8,128)S(1)} %add.12), channel_id=1, source_target_pairs={{0,2},{2,0},{4,6},{6,4},{8,10},{10,8},{12,14},{14,12},{1,3},{3,1},... | collective-permute-start | bytes 258056 | tf_op jit(solution)/shard_map/ppermute | solution.py:530
  192.0 5.7 %collective-permute-start.8 = (f32[168,128]{1,0:T(8,128)S(1)}, f32[168,128]{1,0:T(8,128)S(1)}, u32[]{:S(2)}, u32[]{:S(2)}) collective-permute-start(f32[168,128]{1,0:T(8,128)S(1)} %add.13), channel_id=1, source_target_pairs={{0,4},{2,6},{4,0},{6,2},{8,12},{10,14},{12,8},{14,10},{1,5},{3,7},... | collective-permute-start | bytes 258056 | tf_op jit(solution)/shard_map/ppermute | solution.py:530
  197.7 5.6 %collective-permute-start.9 = (f32[168,128]{1,0:T(8,128)S(1)}, f32[168,128]{1,0:T(8,128)S(1)}, u32[]{:S(2)}, u32[]{:S(2)}) collective-permute-start(f32[168,128]{1,0:T(8,128)S(1)} %add.14), channel_id=1, source_target_pairs={{0,8},{2,10},{4,12},{6,14},{8,0},{10,2},{12,4},{14,6},{1,9},{3,11}... | collective-permute-start | bytes 258056 | tf_op jit(solution)/shard_map/ppermute | solution.py:530
  203.3 1.3 collective-permute-start.10

commit v3 on v2

--- a/solution.py
+++ b/solution.py
@@ -67,7 +67,7 @@
 
 def logits_kernel(
     rows, cols, chans, slots, per, f_ref, w_ref, bias_ref, lab_ref, mask_ref, sel_ref,
-    x_ref, e_ref, sa_ref, sb_ref, keep_ref, strip_ref, f_sem, s_sem,
+    x_ref, e_ref, sa_ref, sb_ref, keep_ref, strip_ref, wv_ref, bv_ref, selv_ref, f_sem, s_sem,
 ):
     steps = rows // per
     tail = lab_ref.shape[1] - LANES
@@ -79,10 +79,16 @@
         pltpu.make_async_copy(ref.at[:, pl.ds(at, LANES)], strip_ref.at[k], s_sem.at[k])
         for k, (ref, at) in enumerate(((lab_ref, 0), (mask_ref, 0), (lab_ref, tail), (mask_ref, tail)))
     ]
-    for copy in strips + loads:
+    small = [
+        pltpu.make_async_copy(a, b, s_sem.at[len(strips) + k])
+        for k, (a, b) in enumerate(((w_ref, wv_ref), (bias_ref, bv_ref), (sel_ref, selv_ref)))
+    ]
+    for copy in strips + small + loads:
         copy.start()
     x_ref[...] = jnp.zeros_like(x_ref)
-    bias = jnp.concatenate([bias_ref[...], jnp.zeros((1, LANES - chans), f32)], axis=1)
+    for copy in small:
+        copy.wait()
+    bias = jnp.concatenate([bv_ref[...], jnp.zeros((1, LANES - chans), f32)], axis=1)
     bias = jnp.broadcast_to(bias, (LANES, LANES)).T[0:chans, :]
     bias = jnp.concatenate([bias] * (per * cols // LANES), axis=1)
     at = lax.broadcasted_iota(jnp.int32, (SUB, LANES), 1)
@@ -106,7 +112,7 @@
     for step in range(steps):
         loads[step].wait()
         block = keep_ref[step * per : step * per + per].reshape(per * cols, f_ref.shape[2])
-        score = lax.dot_general(w_ref[...], block, (((1,), (1,)), ((), ())), preferred_element_type=f32)
+        score = lax.dot_general(wv_ref[...], block, (((1,), (1,)), ((), ())), preferred_element_type=f32)
         score = score + bias
         score = (score - jnp.max(score, axis=0, keepdims=True)) * (LOG2E / STEP)
         for k in range(per):
@@ -121,7 +127,7 @@
             if step == steps - 1 and k == per - 1:
                 e_ref[chans : 2 * chans, :] = tile
     edges = lax.dot_general(
-        sel_ref[...], stack3(x_ref[...], cols), (((1,), (1,)), ((), ())), preferred_element_type=f32
+        selv_ref[...], stack3(x_ref[...], cols), (((1,), (1,)), ((), ())), preferred_element_type=f32
     )
     n = chans * slots // LANES
     for r in range(n):
@@ -134,144 +140,184 @@
         sb_ref[rows + n :, :] = jnp.zeros((pad, LANES), f32)
 
 
-def softmax_fast(groups, chans, slots, up, w_ref, p_ref):
-    sums = [None] * (groups * HALF)
+def softmax_fast(groups, chans, slots, w_ref, p_ref):
+    sums = [None] * (2 * groups * HALF)
     for c in range(chans):
         for b in range(groups):
             row = c * slots + SUB * b
+            centre = w_ref[row + 1 : row + 1 + SUB, :]
+            for up in range(2):
+                beyond = w_ref[row + 2 * up : row + 2 * up + SUB, :]
+                slope = (beyond - centre) * (1.0 / STEP)
+                p = jnp.exp2(centre + slope)
+                ratio = jnp.exp2(slope + slope)
+                for m in range(HALF):
+                    k = (up * groups + b) * HALF + m
+                    if m:
+                        p = p * ratio
+                    p_ref[c * len(sums) + k] = p
+                    sums[k] = p if sums[k] is None else sums[k] + p
+    return sums
+
+
+def softmax_slow(groups, chans, slots, w_ref, p_ref, labels, weights):
+    count = len(labels)
+    sums, losses = [], jnp.zeros((SUB, LANES), f32)
+    for k in range(count):
+        up, b, m = k // (groups * HALF), k // HALF % groups, k % HALF
+
+        def score(c, up=up, b=b, m=m):
+            row = c * slots + SUB * b
             centre = w_ref[pl.ds(row + 1, SUB), :]
-            beyond = w_ref[pl.ds(row + (2 if up else 0), SUB), :]
-            slope = (beyond - centre) * (1.0 / STEP)
-            p = jnp.exp2(centre + slope)
-            ratio = jnp.exp2(slope + slope)
-            for m in range(HALF):
-                k = b * HALF + m
+            beyond = w_ref[pl.ds(row + 2 * up, SUB), :]
+            return centre + (beyond - centre) * ((2 * m + 1.0) / STEP)
+
+        top = lax.fori_loop(1, chans, lambda c, t, score=score: jnp.maximum(t, score(c)), score(0))
+
+        def take(c, carry, k=k, top=top, score=score):
+            total, picked = carry
+            shifted = score(c) - top
+            p = jnp.exp2(shifted)
+            p_ref[c * count + k] = p
+            return total + p, jnp.where(labels[k] == c, shifted, picked)
+
+        zero = jnp.zeros((SUB, LANES), f32)
+        total, picked = lax.fori_loop(0, chans, take, (zero, zero))
+        sums.append(total)
+        losses = losses - weights[k] * picked
+    return sums, losses
+
+
+def pixels(groups, chans, slots, load_labels, fast, w_ref, p_ref, s_ref, lhs_ref):
+    count = 2 * groups * HALF
+    labels = []
+    for up in range(2):
+        for b in range(groups):
+            labels += [load_labels(b, HALF + m if up else HALF - 1 - m) for m in range(HALF)]
+    weights = [jnp.where(lab >= 0, 1.0, 0.0) for lab in labels]
+
+    @pl.when(fast)
+    def _():
+        sums = softmax_fast(groups, chans, slots, w_ref, p_ref)
+        for k in range(count):
+            s_ref[k] = sums[k]
+        s_ref[count] = jnp.zeros((SUB, LANES), f32)
+
+    @pl.when(jnp.logical_not(fast))
+    def _():
+        sums, losses = softmax_slow(groups, chans, slots, w_ref, p_ref, labels, weights)
+        for k in range(count):
+            s_ref[k] = sums[k]
+        s_ref[count] = losses
+
+    loss = jnp.zeros((SUB, LANES), f32)
+    scale = []
+    for k in range(count):
+        total = s_ref[k]
+        loss = loss + weights[k] * jnp.log(total)
+        scale.append(weights[k] / total)
+    packed = [
+        jnp.concatenate([labels[(up * groups + b) * HALF + m] for b in range(groups)], axis=0).astype(f32).astype(bf16)
+        for up in range(2)
+        for m in range(HALF)
+    ]
+    half = jnp.asarray(0.5, bf16)
+    near = jnp.zeros((SUB, LANES), f32)
+    away = jnp.zeros((SUB, LANES), f32)
+    tall = groups * SUB
+    for c in range(chans):
+        tally, hits = None, []
+        for up in range(2):
+            total = run = None
+            for m in reversed(range(HALF)):
+                hit = jnp.where(packed[up * HALF + m] == jnp.asarray(c, bf16), jnp.asarray(1, bf16), jnp.asarray(0, bf16))
+                total = hit if total is None else total + hit
                 if m:
-                    p = p * ratio
-                p_ref[c * groups * HALF + k] = p
-                sums[k] = p if sums[k] is None else sums[k] + p
-    return sums
-
-
-def softmax_slow(groups, chans, slots, up, w_ref, p_ref, labels, weights):
-    sums, losses = [], jnp.zeros((SUB, LANES), f32)
-    for b in range(groups):
-        for m in range(HALF):
-            k = b * HALF + m
-
-            def score(c, b=b, m=m):
-                row = c * slots + SUB * b
-                centre = w_ref[pl.ds(row + 1, SUB), :]
-                beyond = w_ref[pl.ds(row + (2 if up else 0), SUB), :]
-                return centre + (beyond - centre) * ((2 * m + 1.0) / STEP)
-
-            top = lax.fori_loop(1, chans, lambda c, t: jnp.maximum(t, score(c)), score(0))
-
-            def take(c, carry, k=k, top=top, score=score):
-                total, picked = carry
-                shifted = score(c) - top
-                p = jnp.exp2(shifted)
-                p_ref[c * groups * HALF + k] = p
-                return total + p, jnp.where(labels[k] == c, shifted, picked)
-
-            zero = jnp.zeros((SUB, LANES), f32)
-            total, picked = lax.fori_loop(0, chans, take, (zero, zero))
-            sums.append(total)
-            losses = losses - weights[k] * picked
-    return sums, losses
-
-
-def pixels(groups, chans, slots, load_labels, fast, w_ref, p_ref, g_ref, s_ref):
-    count = groups * HALF
-    g_ref[...] = jnp.zeros_like(g_ref)
-    loss = jnp.zeros((SUB, LANES), f32)
-    for up in (False, True):
-        labels = [None] * count
-        for m in range(HALF):
-            for b in range(groups):
-                labels[b * HALF + m] = load_labels(b, HALF + m if up else HALF - 1 - m)
-        weights = [jnp.where(lab >= 0, 1.0, 0.0) for lab in labels]
-        packed = [
-            jnp.concatenate([labels[b * HALF + m] for b in range(groups)], axis=0).astype(jnp.int16)
-            for m in range(HALF)
-        ]
-
-        @pl.when(fast)
-        def _():
-            sums = softmax_fast(groups, chans, slots, up, w_ref, p_ref)
-            for k in range(count):
-                s_ref[k] = sums[k]
-            s_ref[count] = jnp.zeros((SUB, LANES), f32)
-
-        @pl.when(jnp.logical_not(fast))
-        def _():
-            sums, losses = softmax_slow(groups, chans, slots, up, w_ref, p_ref, labels, weights)
-            for k in range(count):
-                s_ref[k] = sums[k]
-            s_ref[count] = losses
-
-        sums = [s_ref[k] for k in range(count)]
-        extra = s_ref[count]
-        scale = []
-        for k in range(count):
-            loss = loss + weights[k] * jnp.log(sums[k])
-            scale.append(weights[k] / sums[k])
-        picked = jnp.zeros((SUB, LANES), f32)
-        for c in range(chans):
-            tally = None
-            for m in range(HALF):
-                hit = jnp.where(packed[m] == jnp.int16(c), jnp.int16(1 + SUB * (2 * m + 1)), jnp.int16(0))
-                tally = hit if tally is None else tally + hit
-            tally = tally.astype(jnp.int32)
-            for b in range(groups):
+                    run = total if run is None else run + total
+            hits.append(run + total * half)
+            tally = total if tally is None else tally + total
+        hits = [v.astype(f32) for v in [tally] + hits]
+        parts = [[], [], []]
+        for b in range(groups):
+            whole_sum = None
+            for up in range(2):
                 total = run = None
                 for m in reversed(range(HALF)):
-                    g = p_ref[c * count + b * HALF + m] * scale[b * HALF + m]
+                    k = (up * groups + b) * HALF + m
+                    g = p_ref[c * count + k] * scale[k]
                     total = g if total is None else total + g
-                    run = total if run is None else run + total
-                part = tally[b * SUB : b * SUB + SUB]
-                ones = (part & (SUB - 1)).astype(f32)
-                far = lax.shift_right_logical(part, 3).astype(f32) * (1.0 / STEP)
-                centre = pl.ds(c * slots + 1 + SUB * b, SUB)
-                beyond = pl.ds(c * slots + (2 if up else 0) + SUB * b, SUB)
-                picked = picked + (ones - far) * w_ref[centre, :] + far * w_ref[beyond, :]
-                out = (run + run - total) * (1.0 / STEP) - far
-                g_ref[centre, :] += (total - ones) - out
-                g_ref[beyond, :] += out
-        loss = loss + LN2 * jnp.where(fast, -picked, extra)
-    return loss
-
-
-def narrow(g_ref, table):
-    g = g_ref[...]
-    hi = g.astype(bf16)
-    low = (g - hi.astype(f32)).astype(bf16)
-    return jnp.dot(jnp.concatenate([hi, low], axis=1), table, preferred_element_type=f32)
+                    if m:
+                        run = total if run is None else run + total
+                parts[up + 1].append(run + total * 0.5)
+                whole_sum = total if whole_sum is None else whole_sum + total
+            parts[0].append(whole_sum)
+            row = c * slots + SUB * b
+            centre = w_ref[row + 1 : row + 1 + SUB, :]
+            mine = [v[b * SUB : b * SUB + SUB] for v in hits]
+            near = near + mine[0] * centre
+            away = away + mine[1] * (w_ref[row : row + SUB, :] - centre)
+            away = away + mine[2] * (w_ref[row + 2 : row + 2 + SUB, :] - centre)
+        for kind in range(3):
+            g = jnp.concatenate(parts[kind], axis=0) - hits[kind]
+            hi = g.astype(bf16)
+            at = (kind * chans + c) * tall
+            lhs_ref[at : at + tall, 0:LANES] = hi
+            lhs_ref[at : at + tall, LANES:] = (g - hi.astype(f32)).astype(bf16)
+    picked = near + away * (1.0 / PATCH)
+    return loss + LN2 * jnp.where(fast, -picked, s_ref[count])
+
+
+def to_slots(groups, chans, slots, sums_ref, out_ref):
+    out_ref[...] = jnp.zeros_like(out_ref)
+    for c in range(chans):
+        for b in range(groups):
+            total, low, high = (
+                sums_ref[((kind * chans + c) * groups + b) * SUB : ((kind * chans + c) * groups + b + 1) * SUB, :]
+                for kind in range(3)
+            )
+            low = low * (1.0 / PATCH)
+            high = high * (1.0 / PATCH)
+            row = c * slots + SUB * b
+            out_ref[row : row + SUB, :] += low
+            out_ref[row + 1 : row + 1 + SUB, :] += total - low - high
+            out_ref[row + 2 : row + 2 + SUB, :] += high
 
 
 def inner_kernel(
-    cols, chans, slots, groups, x_ref, own_ref, got_ref, table_ref, back_ref, lab_ref, mask_ref,
-    acc_ref, loss_ref, stack_ref, floor_ref, w_ref, p_ref, g_ref, s_ref, h_ref,
+    cols, chans, slots, groups, first, tiles, x_ref, own_ref, got_ref, table_ref, next_ref, back_ref, lab_ref, mask_ref,
+    *rest,
 ):
+    if first:
+        acc_ref, loss_ref, stack_ref, floor_ref, w_ref, p_ref, s_ref, lhs_ref = rest
+        begin = 0
+    else:
+        acc_in_ref, loss_in_ref, stack_ref, floor_ref, acc_ref, loss_ref, w_ref, p_ref, s_ref, lhs_ref, sum_ref = rest
+        begin = tiles - pl.num_programs(0)
     step = pl.program_id(0)
+    now = lax.rem(step, 2)
 
     @pl.when(step == 0)
     def _():
-        h_ref[...] = x_ref[...]
-        row = lax.axis_index("gy")
-        top = jnp.where(row == 0, own_ref[0:chans, :], got_ref[chans : 2 * chans, :])
-        last = row == lax.axis_size("gy") - 1
-        bottom = jnp.where(last, own_ref[chans : 2 * chans, :], got_ref[0:chans, :])
-        h_ref[pl.ds(0, chans, stride=slots), :] = top
-        h_ref[pl.ds(groups * SUB + 1, chans, stride=slots), :] = bottom
-        full = h_ref[...]
-        floor_ref[0] = jnp.min(full) * STEP
-        stack_ref[...] = stack3(full, cols)
-        acc_ref[...] = jnp.zeros_like(acc_ref)
-        loss_ref[...] = jnp.zeros_like(loss_ref)
-
-    w_ref[...] = jnp.dot(stack_ref[...], table_ref[...], preferred_element_type=f32)
-    lane = lax.broadcasted_iota(jnp.int32, (SUB, LANES), 1) + step * LANES
+        if first:
+            w_ref[0] = x_ref[...]
+            row = lax.axis_index("gy")
+            top = jnp.where(row == 0, own_ref[0:chans, :], got_ref[chans : 2 * chans, :])
+            last = row == lax.axis_size("gy") - 1
+            bottom = jnp.where(last, own_ref[chans : 2 * chans, :], got_ref[0:chans, :])
+            w_ref[0, pl.ds(0, chans, stride=slots), :] = top
+            w_ref[0, pl.ds(groups * SUB + 1, chans, stride=slots), :] = bottom
+            full = w_ref[0]
+            floor_ref[0] = jnp.min(full) * STEP
+            stack_ref[...] = stack3(full, cols)
+            acc_ref[...] = jnp.zeros_like(acc_ref)
+            loss_ref[...] = jnp.zeros_like(loss_ref)
+        else:
+            sum_ref[...] = acc_in_ref[...]
+            loss_ref[...] = loss_in_ref[...]
+        w_ref[0] = jnp.dot(stack_ref[...], table_ref[...], preferred_element_type=f32)
+
+    sums = acc_ref if first else sum_ref
+    lane = lax.broadcasted_iota(jnp.int32, (SUB, LANES), 1) + (step + begin) * LANES
     inside = (lane >= HALF) & (lane < cols * PATCH - HALF)
 
     def load_labels(b, j):
@@ -279,13 +325,19 @@
         return jnp.where((mask_ref[pick, :] != 0) & inside, lab_ref[pick, :], -1)
 
     fast = floor_ref[0] >= FLOOR
-    loss_ref[...] += pixels(groups, chans, slots, load_labels, fast, w_ref, p_ref, g_ref, s_ref)
-    acc_ref[...] += narrow(g_ref, back_ref[...])
+    loss_ref[...] += pixels(groups, chans, slots, load_labels, fast, w_ref.at[now], p_ref, s_ref, lhs_ref)
+    w_ref[1 - now] = jnp.dot(stack_ref[...], next_ref[...], preferred_element_type=f32)
+    sums[...] += jnp.dot(lhs_ref[...], back_ref[...], preferred_element_type=f32)
+    if not first:
+
+        @pl.when(step == pl.num_programs(0) - 1)
+        def _():
+            to_slots(groups, chans, slots, sum_ref, acc_ref)
 
 
 def edge_kernel(
     rows, cols, chans, slots, groups, floor_ref, stack_ref, acc_ref, loss_in_ref, sa_ref, sb_ref, ra_ref, rb_ref,
-    va_ref, vb_ref, table_ref, fold_ref, back_ref, halo_ref, out_ref, v_ref, loss_ref, w_ref, p_ref, g_ref, s_ref,
+    v_in_ref, table_ref, fold_ref, back_ref, halo_ref, out_ref, v_ref, loss_ref, w_ref, p_ref, s_ref, lhs_ref, sum_ref, more_ref,
 ):
     col = lax.axis_index("gx")
     row = lax.axis_index("gy")
@@ -294,8 +346,8 @@
     n = chans * slots // LANES
     width = n * LANES
 
-    def line(ref):
-        return jnp.concatenate([ref[rows + r : rows + r + 1, :] for r in range(n)], axis=1)
+    def line(ref, at=0):
+        return jnp.concatenate([ref[at + rows + r : at + rows + r + 1, :] for r in range(n)], axis=1)
 
     slot = lax.rem(lax.broadcasted_iota(jnp.int32, (1, width), 1), slots)
 
@@ -304,8 +356,8 @@
         bottom = jnp.where(row == lax.axis_size("gy") - 1, pltpu.roll(mine, 1, 1), pltpu.roll(partner, rows, 1))
         return jnp.where(slot == 0, top, jnp.where(slot == rows + 1, bottom, mine))
 
-    a = with_ends(line(ra_ref), line(va_ref))
-    b = with_ends(line(rb_ref), line(vb_ref))
+    a = with_ends(line(ra_ref), line(v_in_ref))
+    b = with_ends(line(rb_ref), line(v_in_ref, ra_ref.shape[0]))
     sides = [jnp.where(even, b, a), jnp.where(even, a, b)]
     absent = [first, last]
     lows = jnp.float32(0.0)
@@ -345,9 +397,11 @@
 
     fast = jnp.minimum(lows * STEP, floor_ref[0]) >= FLOOR
     outside = (lane < HALF) | (lane >= 3 * HALF)
-    loss = pixels(groups, chans, slots, load_labels, fast, w_ref, p_ref, g_ref, s_ref)
+    loss = pixels(groups, chans, slots, load_labels, fast, w_ref, p_ref, s_ref, lhs_ref)
     loss_ref[...] = loss_in_ref[...] + jnp.where(outside, 0.0, loss)
-    out_ref[...] = (acc_ref[...] + narrow(g_ref, back)) * (1.0 / STEP)
+    sum_ref[...] = jnp.dot(lhs_ref[...], back, preferred_element_type=f32)
+    to_slots(groups, chans, slots, sum_ref, more_ref)
+    out_ref[...] = (acc_ref[...] + more_ref[...]) * (1.0 / STEP)
     v_ref[0:chans, :] = out_ref[pl.ds(0, chans, stride=slots), :]
     v_ref[chans : 2 * chans, :] = out_ref[pl.ds(rows + 1, chans, stride=slots), :]
 
@@ -449,12 +503,13 @@
     per = 4
     shape = lambda *dims: jax.ShapeDtypeStruct(dims, f32)
     held = lambda *dims, kind=f32: pltpu.VMEM(dims, kind)
+    far = lambda v: pltpu.with_memory_space_constraint(v, pltpu.HBM)
     here = lambda v: pltpu.with_memory_space_constraint(v, pltpu.VMEM)
     strip = -(-(rows + chans * slots // LANES) // SUB) * SUB
     tall_x = chans * slots
     x, edge, send_a, send_b, kept = pl.pallas_call(
         functools.partial(logits_kernel, rows, cols, chans, slots, per),
-        in_specs=[ANY, VMEM, VMEM, ANY, ANY, VMEM],
+        in_specs=[ANY] * 6,
         out_specs=[VMEM] * 5,
         out_shape=[
             held(tall_x, LANES), held(2 * chans, LANES), held(strip, LANES), held(strip, LANES),
@@ -462,12 +517,15 @@
         ],
         scratch_shapes=[
             pltpu.VMEM((4, tall, LANES), jnp.int32),
+            pltpu.VMEM((chans, width), bf16),
+            pltpu.VMEM((1, chans), f32),
+            pltpu.VMEM((SUB, depth), bf16),
             pltpu.SemaphoreType.DMA((rows // per,)),
-            pltpu.SemaphoreType.DMA((4,)),
+            pltpu.SemaphoreType.DMA((7,)),
         ],
         compiler_params=ROOM,
         name="logits",
-    )(features, probe_weight.T, probe_bias.reshape(1, chans), labels, valid_mask, ends)
+    )(*(far(v) for v in (features, probe_weight.T, probe_bias.reshape(1, chans), labels, valid_mask, ends)))
 
     swap = lambda v: lax.ppermute(v, "gy", [(0, 1), (1, 0)])
     pairs = lambda at: [p for i in range(at, gx - 1, 2) for p in ((i, i + 1), (i + 1, i))]
@@ -476,39 +534,53 @@
     got_b = lax.ppermute(send_b, "gx", pairs(1))
 
     scratch = [
-        pltpu.VMEM((tall_x, LANES), f32),
-        pltpu.VMEM((chans * count, SUB, LANES), f32),
-        pltpu.VMEM((tall_x, LANES), f32),
-        pltpu.VMEM((count + 1, SUB, LANES), f32),
+        pltpu.VMEM((2 * chans * count, SUB, LANES), f32),
+        pltpu.VMEM((2 * count + 1, SUB, LANES), f32),
+        pltpu.VMEM((3 * chans * rows, 2 * LANES), bf16),
     ]
-    column = pl.BlockSpec((tall, LANES), lambda t: (0, t))
-    acc, loss, stack, floor = pl.pallas_call(
-        functools.partial(inner_kernel, cols, chans, slots, groups),
-        grid=(tiles,),
-        in_specs=[
-            VMEM, VMEM, VMEM,
-            pl.BlockSpec((depth, LANES), lambda t: (0, t)), pl.BlockSpec((depth, LANES), lambda t: (t, 0)),
-            column, column,
-        ],
-        out_specs=[VMEM, VMEM, VMEM, SMEM],
-        out_shape=[held(tall_x, LANES), held(SUB, LANES), held(tall_x, depth, kind=bf16), shape(1)],
-        scratch_shapes=scratch + [pltpu.VMEM((tall_x, LANES), f32)],
-        cost_estimate=pl.CostEstimate(flops=2 * 10**9, bytes_accessed=4 * 10**6, transcendentals=10**6),
-        compiler_params=ROOM,
-        name="inner",
-    )(here(x), here(edge), here(got), lift, back, labels, valid_mask)
-
-    far_a, far_b = swap(got_a), swap(got_b)
+    sums = (3 * chans * rows, LANES)
+
+    def inner_call(first, *args):
+        begin, steps = (0, tiles // 2 + 1) if first else (tiles // 2 + 1, tiles - tiles // 2 - 1)
+        column = pl.BlockSpec((tall, LANES), lambda t: (0, t + begin))
+        outs = [held(*sums), held(SUB, LANES)]
+        if first:
+            outs += [held(tall_x, depth, kind=bf16), shape(1)]
+        else:
+            outs[0] = held(tall_x, LANES)
+        return pl.pallas_call(
+            functools.partial(inner_kernel, cols, chans, slots, groups, first, tiles),
+            grid=(steps,),
+            in_specs=[
+                VMEM, VMEM, VMEM,
+                pl.BlockSpec((depth, LANES), lambda t: (0, t + begin)),
+                pl.BlockSpec((depth, LANES), lambda t: (0, jnp.minimum(t + begin + 1, tiles - 1))),
+                pl.BlockSpec((depth, LANES), lambda t: (t + begin, 0)),
+                column, column,
+            ] + ([] if first else [VMEM, VMEM, VMEM, SMEM]),
+            out_specs=[VMEM, VMEM, VMEM, SMEM] if first else [VMEM, VMEM],
+            out_shape=outs,
+            scratch_shapes=[pltpu.VMEM((2, tall_x, LANES), f32)] + scratch + ([] if first else [pltpu.VMEM(sums, f32)]),
+            cost_estimate=pl.CostEstimate(flops=2 * 10**9, bytes_accessed=4 * 10**6, transcendentals=10**6),
+            compiler_params=ROOM,
+            name="inner_head" if first else "inner_tail",
+        )(*args)
+
+    base = (here(x), here(edge), here(got), lift, lift, back, labels, valid_mask)
+    acc, loss, stack, floor = inner_call(True, *base)
+    got_a, got_b, acc = lax.optimization_barrier((got_a, got_b, acc))
+    corners = swap(jnp.concatenate([got_a, got_b]))
+    acc, loss = inner_call(False, *base, here(acc), here(loss), here(stack), floor)
     grad, spill, loss = pl.pallas_call(
         functools.partial(edge_kernel, rows, cols, chans, slots, groups),
-        in_specs=[SMEM] + [VMEM] * 13,
+        in_specs=[SMEM] + [VMEM] * 12,
         out_specs=[VMEM] * 3,
         out_shape=[held(tall_x, LANES), held(2 * chans, LANES), held(SUB, LANES)],
-        scratch_shapes=scratch,
+        scratch_shapes=[pltpu.VMEM((tall_x, LANES), f32)] + scratch + [pltpu.VMEM(sums, f32), pltpu.VMEM((tall_x, LANES), f32)],
         compiler_params=ROOM,
         name="edge",
     )(
-        floor, *(here(v) for v in (stack, acc, loss, send_a, send_b, got_a, got_b, far_a, far_b)),
+        floor, *(here(v) for v in (stack, acc, loss, send_a, send_b, got_a, got_b, corners)),
         own_f, fold, own_b, sides,
     )
 

time: 206 us -> 197 us (0.956)
  local copies, waits for them, and re-layouts: 6.28 us -> 0.04 us
  starting transfers between devices: 15.7 us -> 13.6 us
    unnamed x28 -> x16, local copies, waits for them, and re-layouts: 6.28 us -> 0.04 us
    ppermute x3, starting transfers between devices: 11 us -> 8.64 us  [body(): lax.ppermute(total, 'gx', [(i, i ^ step) for i in range(gx)])]
    pallas_call x1 -> x2, Pallas kernels: 144 us -> 143 us  [inner_call(): pl.pallas_call(functools.partial(inner_kernel, cols, chans, slots, groups...]
  transfers between devices with their start and end apart: 11 -> 10, of which waited for: 7 -> 6; matrix products, arithmetic and copies ran while one was open for 0% -> 0% of each run, Pallas kernels for 70% -> 73%
where the time goes in v3:
time: 197 us; the launch traced here: 196 us
  Pallas kernels  170 us (86%)
  starting transfers between devices  13.6 us (7%)
  waiting for transfers between devices  11.2 us (6%)
    pallas_call x2, Pallas kernels, inner_call(): pl.pallas_call(functools.partial(inner_kernel, cols, chans, slots, groups...  143 us
    pallas_call x1, Pallas kernels, body(): pl.pallas_call(functools.partial(edge_kernel, rows, cols, chans, slots, g...  21.2 us
    ppermute x3, waiting for transfers between devices, body(): lax.ppermute(total, 'gx', [(i, i ^ step) for i in range(gx)])  8.74 us
    ppermute x3, starting transfers between devices, body(): lax.ppermute(total, 'gx', [(i, i ^ step) for i in range(gx)])  8.64 us
    pallas_call x1, Pallas kernels, body(): pl.pallas_call(functools.partial(logits_kernel, rows, cols, chans, slots,...  4.54 us
  transfers between devices with their start and end apart: 10, of which 6 were waited for; matrix products, arithmetic and copies ran while one was open for 0% of the time, Pallas kernels for 73%

profile of v3, /device:TPU:0, one launch (start us, length us, event | category | flops | bytes accessed | tf_op | source)
XLA Modules:
  0.0 196.4 jit_solution(183703072202169537)
XLA Ops:
  0.6 0.0 copy-start.6
  0.6 0.0 copy-start.7
  0.7 0.0 copy-start
  0.7 0.0 copy-start.1
  0.7 4.5 %logits.1 = (f32[768,128]{1,0:T(8,128)S(1)}, f32[64,128]{1,0:T(8,128)S(1)}, f32[24,128]{1,0:T(8,128)S(1)}, f32[24,128]{1,0:T(8,128)S(1)}, bf16[16,64,1280]{2,1,0:T(8,128)(2,1)S(1)}) custom-call(bf16[16,64,1280]{2,1,0:T(8,128)(2,1)} %f_ref.1, bf16[32,1280]{1,0:T(8,128)(2,1)} %bitcast.5, f32[1,32]{1,0:T(1,128)} %bitcast.6, s32[224,896]{1,0:T(8,128)} %lab_ref.5, ...), custom_call_target="tpu_custom_call" | custom-call | tf_op jit(solution)/shard_map/logits/pallas_call | solution.py:510
  5.2 0.6 collective-permute-start
  5.8 2.6 %collective-permute-start.1 = (f32[24,128]{1,0:T(8,128)S(1)}, f32[24,128]{1,0:T(8,128)S(1)}, u32[]{:S(2)}, u32[]{:S(2)}) collective-permute-start(f32[24,128]{1,0:T(8,128)S(1)} %get-tuple-element.30.sa_ref), channel_id=1, source_target_pairs={{0,2},{2,0},{4,6},{6,4},{8,10},{10,8},{12,14},{14,12},{1,3},{3,1},... | collective-permute-start | bytes 36872 | tf_op jit(solution)/shard_map/ppermute | solution.py:533
  8.4 0.7 collective-permute-start.2
  9.0 0.0 collective-permute-done.got_ref
  9.0 0.0 copy-done.6
  9.0 0.0 copy-done.7
  9.1 81.5 %inner_head.1 = (f32[1536,128]{1,0:T(8,128)S(1)}, f32[8,128]{1,0:T(8,128)S(1)}, bf16[768,256]{1,0:T(8,128)(2,1)S(1)}, f32[1]{0:T(128)}) custom-call(f32[768,128]{1,0:T(8,128)S(1)} %get-tuple-element.26.x_ref, f32[64,128]{1,0:T(8,128)S(1)} %get-tuple-element.27.own_ref, f32[64,128]{1,0:T(8,128)S(1)} %collective-permute-done.got_ref, ...), custom_call_target="tpu_custom_call" | custom-call | flops 2000000000 | bytes 4000000 | tf_op jit(solution)/shard_map/inner_head/pallas_call | solution.py:551
  90.6 0.0 collective-permute-done.1.ra_ref
  90.6 0.0 collective-permute-done.2.rb_ref
  90.6 0.2 collective-permute-start.3
  90.8 61.6 %inner_tail.1 = (f32[768,128]{1,0:T(8,128)S(1)}, f32[8,128]{1,0:T(8,128)S(1)}) custom-call(f32[768,128]{1,0:T(8,128)S(1)} %get-tuple-element.26.x_ref, f32[64,128]{1,0:T(8,128)S(1)} %get-tuple-element.27.own_ref, f32[64,128]{1,0:T(8,128)S(1)} %collective-permute-done.got_ref, bf16[256,896]{1,0:T(8,128)(2,1)S(1)} %copy-done.6, ...), custom_call_target="tpu_custom_call" | custom-call | flops 2000000000 | bytes 4000000 | tf_op jit(solution)/shard_map/inner_tail/pallas_call | solution.py:551
  152.4 0.0 collective-permute-done.3.v_in_ref
  152.5 21.2 %edge.1 = (f32[768,128]{1,0:T(8,128)S(1)}, f32[64,128]{1,0:T(8,128)S(1)}, f32[8,128]{1,0:T(8,128)S(1)}) custom-call(f32[1]{0:T(128)} %get-tuple-element.28.rest_3_.floor_ref, bf16[768,256]{1,0:T(8,128)(2,1)S(1)} %get-tuple-element.29.rest_2_.stack_ref, f32[768,128]{1,0:T(8,128)S(1)} %get-tuple-element.35.acc_ref, ...), custom_call_target="tpu_custom_call" | custom-call | tf_op jit(solution)/shard_map/edge/pallas_call | solution.py:574
  173.7 0.4 collective-permute-start.4
  174.8 0.2 collective-permute-done.4.got_ref
  175.0 0.6 grad.1
  175.5 0.4 collective-permute-start.5
  176.0 0.9 collective-permute-done.5
  176.9 4.3 %collective-permute-start.6 = (f32[168,128]{1,0:T(8,128)S(1)}, f32[168,128]{1,0:T(8,128)S(1)}, u32[]{:S(2)}, u32[]{:S(2)}) collective-permute-start(f32[168,128]{1,0:T(8,128)S(1)} %add.12), channel_id=1, source_target_pairs={{0,2},{2,0},{4,6},{6,4},{8,10},{10,8},{12,14},{14,12},{1,3},{3,1},... | collective-permute-start | bytes 258056 | tf_op jit(solution)/shard_map/ppermute | solution.py:602
  181.3 3.0 %collective-permute-done.6 = f32[168,128]{1,0:T(8,128)S(1)} collective-permute-done((f32[168,128]{1,0:T(8,128)S(1)}, f32[168,128]{1,0:T(8,128)S(1)}, u32[]{:S(2)}, u32[]{:S(2)}) %collective-permute-start.6) | collective-permute-done | bytes 86048 | tf_op jit(solution)/shard_map/ppermute | solution.py:602
  184.3 1.6 collective-permute-start.7
  186.0 2.9 %collective-permute-done.7 = f32[168,128]{1,0:T(8,128)S(1)} collective-permute-done((f32[168,128]{1,0:T(8,128)S(1)}, f32[168,128]{1,0:T(8,128)S(1)}, u32[]{:S(2)}, u32[]{:S(2)}) %collective-permute-start.7) | collective-permute-done | bytes 86048 | tf_op jit(solution)/shard_map/ppermute | solution.py:602
  188.9 2.7 %collective-permute-start.8 = (f32[168,128]{1,0:T(8,128)S(1)}, f32[168,128]{1,0:T(8,128)S(1)}, u32[]{:S(2)}, u32[]{:S(2)}) collective-permute-start(f32[168,128]{1,0:T(8,128)S(1)} %add.14), channel_id=1, source_target_pairs={{0,8},{2,10},{4,12},{6,14},{8,0},{10,2},{12,4},{14,6},{1,9},{3,11}... | collective-permute-start | bytes 258056 | tf_op jit(solution)/shard_map/ppermute | solution.py:602
  191.5 2.8 %collective-permute-done.8 = f32[168,128]{1,0:T(8,128)S(1)} collective-permute-done((f32[168,128]{1,0:T(8,128)S(1)}, f32[168,128]{1,0:T(8,128)S(1)}, u32[]{:S(2)}, u32[]{:S(2)}) %collective-permute-start.8) | collective-permute-done | bytes 86048 | tf_op jit(solution)/shard_map/ppermute | solution.py:602
  194.3 0.1 collective-permute-start.9
  194.4 1.3 collective-permute-done.9.z_ref
  195.7 0.7 final.1
  (15 shorter events, 0.1 us)
Async XLA Ops:
  0.6 8.4 %copy-start.6 = (bf16[256,896]{1,0:T(8,128)(2,1)S(1)}, bf16[256,896]{1,0:T(8,128)(2,1)}, u32[]{:S(2)}) copy-start(bf16[256,896]{1,0:T(8,128)(2,1)} %constant.14.clone.table_ref.next_ref) | copy-start | bytes 1376260
  0.6 8.4 %copy-start.7 = (bf16[1792,128]{1,0:T(8,128)(2,1)S(1)}, bf16[1792,128]{1,0:T(8,128)(2,1)}, u32[]{:S(2)}) copy-start(bf16[1792,128]{1,0:T(8,128)(2,1)} %constant.15.clone.back_ref) | copy-start | bytes 1376260
  0.7 8.4 %copy-start = (s32[224,896]{1,0:T(8,128)S(1)}, s32[224,896]{1,0:T(8,128)}, u32[]{:S(2)}) copy-start(s32[224,896]{1,0:T(8,128)} %lab_ref.5) | copy-start | bytes 2408452
  0.7 8.4 %copy-start.1 = (s32[224,896]{1,0:T(8,128)S(1)}, s32[224,896]{1,0:T(8,128)}, u32[]{:S(2)}) copy-start(s32[224,896]{1,0:T(8,128)} %mask_ref.5) | copy-start | bytes 2408452
  5.2 3.8 %collective-permute-start = (f32[64,128]{1,0:T(8,128)S(1)}, f32[64,128]{1,0:T(8,128)S(1)}, u32[]{:S(2)}, u32[]{:S(2)}) collective-permute-start(f32[64,128]{1,0:T(8,128)S(1)} %get-tuple-element.27.own_ref), channel_id=1, source_target_pairs={{0,1},{1,0},{2,3},{3,2},{4,5},{5,4},{6,7},{7,6},{8,9},{9,8},{10,11... | collective-permute-start | bytes 98312 | tf_op jit(solution)/shard_map/ppermute | solution.py:530
  5.8 84.8 %collective-permute-start.1 = (f32[24,128]{1,0:T(8,128)S(1)}, f32[24,128]{1,0:T(8,128)S(1)}, u32[]{:S(2)}, u32[]{:S(2)}) collective-permute-start(f32[24,128]{1,0:T(8,128)S(1)} %get-tuple-element.30.sa_ref), channel_id=1, source_target_pairs={{0,2},{2,0},{4,6},{6,4},{8,10},{10,8},{12,14},{14,12},{1,3},{3,1},... | collective-permute-start | bytes 36872 | tf_op jit(solution)/shard_map/ppermute | solution.py:533
  8.4 82.2 %collective-permute-start.2 = (f32[24,128]{1,0:T(8,128)S(1)}, f32[24,128]{1,0:T(8,128)S(1)}, u32[]{:S(2)}, u32[]{:S(2)}) collective-permute-start(f32[24,128]{1,0:T(8,128)S(1)} %get-tuple-element.31.sb_ref), channel_id=1, source_target_pairs={{2,4},{4,2},{6,8},{8,6},{10,12},{12,10},{3,5},{5,3},{7,9},{9,7},{1... | collective-permute-start | bytes 36872 | tf_op jit(solution)/shard_map/ppermute | solution.py:534
  90.6 61.8 %collective-permute-start.3 = (f32[48,128]{1,0:T(8,128)S(1)}, f32[48,128]{1,0:T(8,128)S(1)}, u32[]{:S(2)}, u32[]{:S(2)}) collective-permute-start(f32[48,128]{1,0:T(8,128)S(1)} %pad_maximum_fusion), channel_id=1, source_target_pairs={{0,1},{1,0},{2,3},{3,2},{4,5},{5,4},{6,7},{7,6},{8,9},{9,8},{10,11... | collective-permute-start | bytes 73736 | tf_op jit(solution)/shard_map/ppermute | solution.py:530
  90.8 61.6 %copy-start.2 = (bf16[1024,128]{1,0:T(8,128)(2,1)S(1)}, bf16[1024,128]{1,0:T(8,128)(2,1)}, u32[]{:S(2)}) copy-start(bf16[1024,128]{1,0:T(8,128)(2,1)} %constant.18.clone.fold_ref) | copy-start | bytes 786436
  90.8 61.6 %copy-start.3 = (bf16[256,128]{1,0:T(8,128)(2,1)S(1)}, bf16[256,128]{1,0:T(8,128)(2,1)}, u32[]{:S(2)}) copy-start(bf16[256,128]{1,0:T(8,128)(2,1)} %constant.16.clone.table_ref) | copy-start | bytes 196612
  90.8 61.6 %copy-start.4 = (bf16[256,128]{1,0:T(8,128)(2,1)S(1)}, bf16[256,128]{1,0:T(8,128)(2,1)}, u32[]{:S(2)}) copy-start(bf16[256,128]{1,0:T(8,128)(2,1)} %constant.17.clone.back_ref) | copy-start | bytes 196612
  90.8 61.6 %copy-start.5 = (bf16[16,128]{1,0:T(8,128)(2,1)S(1)}, bf16[16,128]{1,0:T(8,128)(2,1)}, u32[]{:S(2)}) copy-start(bf16[16,128]{1,0:T(8,128)(2,1)} %constant.19.clone.halo_ref) | copy-start | bytes 12292
  173.7 1.3 collective-permute-start.4
  175.5 1.3 collective-permute-start.5
  176.9 7.4 %collective-permute-start.6 = (f32[168,128]{1,0:T(8,128)S(1)}, f32[168,128]{1,0:T(8,128)S(1)}, u32[]{:S(2)}, u32[]{:S(2)}) collective-permute-start(f32[168,128]{1,0:T(8,128)S(1)} %add.12), channel_id=1, source_target_pairs={{0,2},{2,0},{4,6},{6,4},{8,10},{10,8},{12,14},{14,12},{1,3},{3,1},... | collective-permute-start | bytes 258056 | tf_op jit(solution)/shard_map/ppermute | solution.py:602
  184.3 4.6 %collective-permute-start.7 = (f32[168,128]{1,0:T(8,128)S(1)}, f32[168,128]{1,0:T(8,128)S(1)}, u32[]{:S(2)}, u32[]{:S(2)}) collective-permute-start(f32[168,128]{1,0:T(8,128)S(1)} %add.13), channel_id=1, source_target_pairs={{0,4},{2,6},{4,0},{6,2},{8,12},{10,14},{12,8},{14,10},{1,5},{3,7},... | collective-permute-start | bytes 258056 | tf_op jit(solution)/shard_map/ppermute | solution.py:602
  188.9 5.4 %collective-permute-start.8 = (f32[168,128]{1,0:T(8,128)S(1)}, f32[168,128]{1,0:T(8,128)S(1)}, u32[]{:S(2)}, u32[]{:S(2)}) collective-permute-start(f32[168,128]{1,0:T(8,128)S(1)} %add.14), channel_id=1, source_target_pairs={{0,8},{2,10},{4,12},{6,14},{8,0},{10,2},{12,4},{14,6},{1,9},{3,11}... | collective-permute-start | bytes 258056 | tf_op jit(solution)/shard_map/ppermute | solution.py:602
  194.3 1.3 collective-permute-start.9

commit v4 on v3

v4 whole, which is shorter than its diff:
```python
import functools
import math

import jax
import jax.numpy as jnp
import numpy as np
from jax import lax
from jax.experimental import pallas as pl
from jax.experimental.pallas import tpu as pltpu
from jax.sharding import PartitionSpec as P

PATCH = 14
HALF = PATCH // 2
STEP = 2 * PATCH
LANES = 128
SUB = 8
LOG2E = 1.0 / math.log(2.0)
LN2 = math.log(2.0)
FLOOR = -100.0
f32 = jnp.float32
bf16 = jnp.bfloat16
VMEM = pl.BlockSpec(memory_space=pltpu.VMEM)
ANY = pl.BlockSpec(memory_space=pl.ANY)
ROOM = pltpu.CompilerParams(vmem_limit_bytes=16 * 2**20)
SMEM = pl.BlockSpec(memory_space=pltpu.SMEM)


def whole(shape):
    return pl.BlockSpec(shape, lambda *ids: (0,) * len(shape))


def column_tables(cols):
    tables = np.zeros((2, cols + 1, cols * PATCH), np.float32)
    for q in range(cols * PATCH):
        i, k = divmod((q if q >= HALF else q + cols * PATCH) - HALF, PATCH)
        far = 2 * k + 1
        for end in range(2):
            if end and i == cols - 1:
                tables[end, i + (k >= HALF), q] = STEP
            else:
                tables[end, i, q] = STEP - far
                tables[end, i + 1, q] = far
    return tables


def split3(x):
    hi = x.astype(bf16)
    rest = x - hi.astype(f32)
    mid = rest.astype(bf16)
    return hi, mid, (rest - mid.astype(f32)).astype(bf16)


def stack3(x):
    cols = LANES // 2
    lane = lax.broadcasted_iota(jnp.int32, x.shape, 1)
    hi, mid, low = (part.astype(f32) for part in split3(x))
    first = jnp.where(lane < cols, hi, pltpu.roll(mid, cols, 1))
    second = jnp.where(lane == cols + 1, pltpu.roll(mid, 1, 1), pltpu.roll(low, 2, 1))
    second = jnp.where(lane == cols, hi, jnp.where(lane < cols + 3, second, 0.0))
    second = jnp.where(lane < cols, low, second)
    return jnp.concatenate([first.astype(bf16), second.astype(bf16)], axis=1)


def pack_kernel(rows, f_ref, lab_ref, mask_ref, out_ref, head_ref, f_vmem, l_vmem, h_vmem, sem):
    width = f_vmem.shape[2]
    tiles = head_ref.shape[0] // SUB
    copies = [
        pltpu.make_async_copy(lab_ref.at[:, pl.ds(0, LANES)], l_vmem.at[0], sem.at[0]),
        pltpu.make_async_copy(mask_ref.at[:, pl.ds(0, LANES)], l_vmem.at[1], sem.at[1]),
        pltpu.make_async_copy(f_ref.at[:, pl.ds(0, SUB)], f_vmem, sem.at[2]),
        pltpu.make_async_copy(lab_ref.at[pl.ds(0, SUB)], h_vmem.at[0], sem.at[3]),
        pltpu.make_async_copy(mask_ref.at[pl.ds(0, SUB)], h_vmem.at[1], sem.at[4]),
    ]
    for copy in copies:
        copy.start()
    at = lax.broadcasted_iota(jnp.int32, (SUB, LANES), 1)
    for copy in copies:
        copy.wait()
    for b in range(rows // SUB):
        strip = jnp.full((SUB, LANES), -1.0, f32)
        for j in range(PATCH):
            pick = pl.ds(b * SUB * PATCH + j, SUB, stride=PATCH)
            lab = jnp.where(l_vmem[1, pick, :] != 0, l_vmem[0, pick, :], -1).astype(f32)
            here = (at >= j * HALF) & (at < j * HALF + HALF)
            strip = jnp.where(here, pltpu.roll(lab, j * HALF, 1) if j else lab, strip)
        out_ref[b * SUB : b * SUB + SUB, :] = strip
    for i in range(rows):
        line = f_vmem[i].astype(f32)
        for k in range(width // LANES):
            out_ref[rows + k * rows + i : rows + k * rows + i + 1, :] = line[0:1, k * LANES : k * LANES + LANES]
    for t in range(tiles):
        lanes = slice(t * LANES, t * LANES + LANES)
        head_ref[t * SUB : t * SUB + SUB, :] = jnp.where(h_vmem[1, :, lanes] != 0, h_vmem[0, :, lanes], -1).astype(f32)


def logits_kernel(
    rows, cols, chans, slots, per, f_ref, w_ref, bias_ref, side_ref, head_ref, x_ref, e_ref, beside_ref,
):
    x_ref[...] = jnp.zeros_like(x_ref)
    bias = jnp.concatenate([bias_ref[...], jnp.zeros((1, LANES - chans), f32)], axis=1)
    bias = jnp.broadcast_to(bias, (LANES, LANES)).T[0:chans, :]
    width = f_ref.shape[2]

    def score_of(block):
        score = lax.dot_general(w_ref[...], block, (((1,), (1,)), ((), ())), preferred_element_type=f32)
        score = score + jnp.concatenate([bias] * (block.shape[0] // LANES), axis=1)
        return (score - jnp.max(score, axis=0, keepdims=True)) * (LOG2E / STEP)

    side = jnp.concatenate(
        [side_ref[rows + k * rows : rows + k * rows + rows, :] for k in range(width // LANES)], axis=1
    ).astype(bf16)
    beside_ref[...] = side
    beyond = score_of(jnp.concatenate([side, jnp.zeros((LANES - rows, width), bf16)], axis=0))
    lane = lax.broadcasted_iota(jnp.int32, (chans, LANES), 1)
    for step in range(rows // per):
        block = f_ref[step * per : step * per + per].reshape(per * cols, width)
        score = score_of(block)
        for k in range(per):
            i, off = step * per + k, k * cols
            tile = score[:, off // LANES * LANES : off // LANES * LANES + LANES]
            if off % LANES:
                tile = pltpu.roll(tile, LANES - off % LANES, 1)
            tile = jnp.where(lane < cols, tile, jnp.where(lane == cols, pltpu.roll(beyond, cols - i, 1), 0.0))
            x_ref[pl.ds(i, chans, stride=slots), :] = tile
            if i == 0:
                e_ref[0:chans, :] = tile
    e_ref[chans : chans + head_ref.shape[0], :] = head_ref[...]
    e_ref[chans + head_ref.shape[0] :, :] = side_ref[0:SUB, :]


def softmax_fast(groups, chans, slots, fold, w_ref, p_ref):
    sums = [None] * (2 * groups * HALF)
    for c in range(chans):
        for b in range(groups):
            row = c * slots + SUB * b
            upper = w_ref[row : row + SUB, :]
            lower = w_ref[row + 1 : row + 1 + SUB, :]
            slope = (lower - upper) * fold[b]
            twice = slope + slope
            for half, (p, ratio) in enumerate(((upper + slope, twice), (lower - slope, -twice))):
                p, ratio = jnp.exp2(p), jnp.exp2(ratio)
                for m in range(HALF):
                    k = (half * groups + b) * HALF + m
                    if m:
                        p = p * ratio
                    p_ref[c * len(sums) + k] = p
                    sums[k] = p if sums[k] is None else sums[k] + p
    return sums


def softmax_slow(groups, chans, slots, fold, w_ref, p_ref, labels, weights):
    count = len(labels)
    sums, losses = [], jnp.zeros((SUB, LANES), f32)
    for k in range(count):
        half, b, m = k // (groups * HALF), k // HALF % groups, k % HALF

        def score(c, half=half, b=b, m=m):
            row = c * slots + SUB * b
            near = w_ref[pl.ds(row + half, SUB), :]
            away = w_ref[pl.ds(row + 1 - half, SUB), :]
            return near + (away - near) * fold[b] * (2 * m + 1.0)

        top = lax.fori_loop(1, chans, lambda c, t, score=score: jnp.maximum(t, score(c)), score(0))

        def take(c, carry, k=k, top=top, score=score):
            total, picked = carry
            shifted = score(c) - top
            p = jnp.exp2(shifted)
            p_ref[c * count + k] = p
            return total + p, jnp.where(labels[k] == c, shifted, picked)

        zero = jnp.zeros((SUB, LANES), f32)
        total, picked = lax.fori_loop(0, chans, take, (zero, zero))
        sums.append(total)
        losses = losses - weights[k] * picked
    return sums, losses


def pixels(groups, chans, slots, fold, lab_ref, fast, w_ref, p_ref, s_ref, lhs_ref):
    count = 2 * groups * HALF
    labels = []
    for half in range(2):
        for b in range(groups):
            for m in range(HALF):
                k = PATCH - 1 - m if half else m
                labels.append(lab_ref[pl.ds(b * SUB * PATCH + HALF + k, SUB, stride=PATCH), :])
    weights = [jnp.where(lab >= 0, 1.0, 0.0) for lab in labels]

    @pl.when(fast)
    def _():
        sums = softmax_fast(groups, chans, slots, fold, w_ref, p_ref)
        for k in range(count):
            s_ref[k] = sums[k]
        s_ref[count] = jnp.zeros((SUB, LANES), f32)

    @pl.when(jnp.logical_not(fast))
    def _():
        sums, losses = softmax_slow(groups, chans, slots, fold, w_ref, p_ref, labels, weights)
        for k in range(count):
            s_ref[k] = sums[k]
        s_ref[count] = losses

    loss = jnp.zeros((SUB, LANES), f32)
    scale = []
    for k in range(count):
        total = s_ref[k]
        loss = loss + weights[k] * jnp.log(total)
        scale.append(weights[k] / total)
    packed = [
        jnp.concatenate([labels[(half * groups + b) * HALF + m] for b in range(groups)], axis=0).astype(f32).astype(bf16)
        for half in range(2)
        for m in range(HALF)
    ]
    one, none, mid = (jnp.asarray(v, bf16) for v in (1, 0, 0.5))
    picked = jnp.zeros((SUB, LANES), f32)
    tall = groups * SUB

    def two_sums(item):
        totals, runs = [], []
        for half in range(2):
            total = run = None
            for m in reversed(range(HALF)):
                v = item(half, m)
                total = v if total is None else total + v
                if m:
                    run = total if run is None else run + total
            totals.append(total)
            runs.append(run)
        return totals[0], totals[1], runs[0] - runs[1], totals[0] - totals[1]

    for c in range(chans):
        mark = jnp.asarray(c, bf16)
        up, down, run, lean = two_sums(lambda half, m: jnp.where(packed[half * HALF + m] == mark, one, none))
        hits = [v.astype(f32) for v in (up, down, run + lean * mid)]
        parts = [[], []]
        for b in range(groups):
            row = c * slots + SUB * b
            up, down, lean = (v[b * SUB : b * SUB + SUB] for v in hits)
            lean = lean * (fold[b] * 2.0)
            up, down = up - lean, down + lean
            picked = picked + up * w_ref[row : row + SUB, :] + down * w_ref[row + 1 : row + 1 + SUB, :]
            above, below, run, lean = two_sums(
                lambda half, m: p_ref[c * count + (half * groups + b) * HALF + m] * scale[(half * groups + b) * HALF + m]
            )
            lean = (run + lean * 0.5) * (fold[b] * 2.0)
            parts[0].append((above - up) - lean)
            parts[1].append((below - down) + lean)
        for kind in range(2):
            g = jnp.concatenate(parts[kind], axis=0)
            hi = g.astype(bf16)
            at = (kind * chans + c) * tall
            lhs_ref[at : at + tall, 0:LANES] = hi
            lhs_ref[at : at + tall, LANES:] = (g - hi.astype(f32)).astype(bf16)
    return loss + LN2 * jnp.where(fast, -picked, s_ref[count])


def inner_kernel(
    rows, cols, chans, slots, groups, x_ref, got_ref, strip_ref, lift_ref, lift_end_ref, next_ref, next_end_ref,
    back_ref, back_end_ref, lab_ref, mask_ref, out_ref, spill_ref, loss_ref,
    w_ref, p_ref, s_ref, lhs_ref, sum_ref, stack_ref, tile_ref, floor_ref,
):
    step = pl.program_id(0)
    steps = pl.num_programs(0)
    now = lax.rem(step, 2)
    last_col = lax.axis_index("gx") == lax.axis_size("gx") - 1
    last_row = lax.axis_index("gy") == lax.axis_size("gy") - 1
    tall = rows * PATCH
    lane = lax.broadcasted_iota(jnp.int32, (SUB, LANES), 1)

    @pl.when(step == 0)
    def _():
        w_ref[0] = x_ref[...]
        w_ref[0, pl.ds(rows, chans, stride=slots), :] = got_ref[0:chans, :]
        full = w_ref[0]
        floor_ref[0] = jnp.min(full) * STEP
        stack_ref[...] = stack3(full)
        sum_ref[...] = jnp.zeros_like(sum_ref)
        loss_ref[...] = jnp.zeros_like(loss_ref)
        table = jnp.where(last_col, lift_end_ref[...], lift_ref[...])
        w_ref[0] = jnp.dot(stack_ref[...], table, preferred_element_type=f32)

    tile_ref[0:tall, :] = jnp.where(mask_ref[...] != 0, lab_ref[...], -1)
    tile_ref[tall : tall + SUB, :] = got_ref[pl.ds(pl.multiple_of(chans + step * SUB, SUB), SUB), :].astype(jnp.int32)

    @pl.when(step == 0)
    def _():
        for j in range(PATCH):
            for b in range(groups):
                pick = pl.ds(b * SUB * PATCH + j, SUB, stride=PATCH)
                strip = strip_ref[b * SUB : b * SUB + SUB, :]
                strip = pltpu.roll(strip, LANES - j * HALF, 1) if j else strip
                tile_ref[pick, :] = jnp.where(lane < HALF, strip.astype(jnp.int32), tile_ref[pick, :])
        at = chans + steps * SUB
        for j in range(HALF):
            strip = got_ref[at : at + 1, :]
            strip = pltpu.roll(strip, LANES - j * HALF, 1) if j else strip
            row = tile_ref[tall + j : tall + j + 1, :]
            tile_ref[tall + j : tall + j + 1, :] = jnp.where(lane[0:1] < HALF, strip.astype(jnp.int32), row)

    flat = jnp.full((SUB, LANES), 1.0 / STEP, f32)
    sub = lax.broadcasted_iota(jnp.int32, (SUB, LANES), 0)
    fold = [flat] * (groups - 1) + [jnp.where(last_row & (sub == SUB - 1), 0.0, flat)]
    fast = floor_ref[0] >= FLOOR
    loss_ref[...] += pixels(groups, chans, slots, fold, tile_ref, fast, w_ref.at[now], p_ref, s_ref, lhs_ref)
    table = jnp.where(last_col, next_end_ref[...], next_ref[...])
    w_ref[1 - now] = jnp.dot(stack_ref[...], table, preferred_element_type=f32)
    table = jnp.where(last_col, back_end_ref[...], back_ref[...])
    sum_ref[...] += jnp.dot(lhs_ref[...], table, preferred_element_type=f32)

    @pl.when(step == steps - 1)
    def _():
        w_ref[0] = jnp.zeros_like(w_ref[0])
        high = groups * SUB
        for c in range(chans):
            for kind in range(2):
                at = (kind * chans + c) * high
                row = c * slots + kind
                w_ref[0, row : row + high, :] += sum_ref[at : at + high, :]
        out_ref[...] = w_ref[0] * (1.0 / STEP)
        spill_ref[...] = out_ref[pl.ds(rows, chans, stride=slots), :]


def grad_kernel(
    rows, cols, chans, slots, f_ref, beside_ref, g_ref, got_ref, loss_ref, count_ref, mine_ref, other_ref, sum_ref,
):
    row = lax.axis_index("gy")
    sum_ref[...] = g_ref[...]
    sum_ref[pl.ds(0, chans, stride=slots), :] += got_ref[...]
    lane = lax.broadcasted_iota(jnp.int32, (chans, LANES), 1)
    share = LANES // cols
    edge = jnp.zeros((chans, LANES), f32)
    tiles = []
    total = jnp.zeros((chans, LANES), f32)
    for k in range(0, rows, share):
        tile = None
        for r in range(share):
            piece = sum_ref[pl.ds(k + r, chans, stride=slots), :]
            total = total + piece
            edge = jnp.where(lane == k + r, pltpu.roll(piece, (k + r - cols) % LANES, 1), edge)
            if r:
                piece = pltpu.roll(piece, r * cols, 1)
            tile = piece if tile is None else jnp.where(lane < r * cols, tile, piece)
        tiles.append(tile.astype(bf16))
    block = f_ref[...].reshape(rows * cols, f_ref.shape[2])
    out = jnp.dot(jnp.concatenate(tiles, axis=1), block, preferred_element_type=f32)
    beside = jnp.concatenate([beside_ref[...], jnp.zeros((LANES - rows, f_ref.shape[2]), bf16)], axis=0)
    out = out + jnp.dot(edge.astype(bf16), beside, preferred_element_type=f32)
    total = jnp.where(lane <= cols, total, 0.0)
    square = jnp.concatenate([total, jnp.zeros((LANES - chans, LANES), f32)], axis=0)
    bias = jnp.sum(square.T, axis=0, keepdims=True)
    at = lax.broadcasted_iota(jnp.int32, (SUB, LANES), 0)
    rest = jnp.where(at == 1, jnp.sum(loss_ref[...]), count_ref[0, 0].astype(f32))
    stats = jnp.where(at == 0, bias, jnp.where(at < 3, rest, 0.0))
    pieces = out.shape[1] // LANES // 2
    for k in range(pieces):
        low = out[:, k * LANES : k * LANES + LANES]
        high = out[:, (pieces + k) * LANES : (pieces + k + 1) * LANES]
        mine_ref[k * chans : k * chans + chans, :] = jnp.where(row == 0, low, high)
        other_ref[k * chans : k * chans + chans, :] = jnp.where(row == 0, high, low)
    mine_ref[pieces * chans :, :] = stats
    other_ref[pieces * chans :, :] = stats


def final_kernel(chans, y_ref, z_ref, loss_ref, weight_ref, bias_ref):
    pieces = y_ref.shape[0] // chans
    lower = lax.axis_index("gy") == 0
    stats = y_ref[pieces * chans :, :]
    total = stats[2:3, 0:1]
    for k in range(pieces):
        y = y_ref[k * chans : k * chans + chans, :]
        z = z_ref[k * chans : k * chans + chans, :]
        weight_ref[:, k * LANES : k * LANES + LANES] = jnp.where(lower, y, z) / total
        weight_ref[:, (pieces + k) * LANES : (pieces + k + 1) * LANES] = jnp.where(lower, z, y) / total
    loss_ref[...] = stats[1:2, 0:1] / total
    bias_ref[...] = stats[0:1, 0:chans] / total


def body(features, probe_weight, probe_bias, labels, valid_mask, valid_count):
    rows, cols, width = features.shape
    chans = probe_weight.shape[1]
    gx, gy = lax.axis_size("gx"), lax.axis_size("gy")
    if gy != 2 or rows % SUB or 2 * cols != LANES or cols * PATCH % LANES or width % (2 * LANES) or gx & (gx - 1):
        raise ValueError("unsupported tile")
    groups = rows // SUB
    slots = rows + SUB
    count = groups * HALF
    tiles = cols * PATCH // LANES
    tall = rows * PATCH
    depth = 2 * LANES

    def forward(table):
        out = np.zeros((depth, table.shape[1]), np.float32)
        for k in range(3):
            out[k * cols : k * cols + cols] = table[:cols]
            out[3 * cols + k] = table[cols]
        return out

    def backward(table):
        out = np.zeros((table.shape[1] // LANES, 2, LANES, LANES), np.float32)
        out[:, :, :, : cols + 1] = table.T.reshape(-1, 1, LANES, cols + 1)
        return out.reshape(-1, LANES)

    inside, ending = column_tables(cols)
    lift, lift_end, back, back_end = (
        jnp.asarray(t, bf16) for t in (forward(inside), forward(ending), backward(inside), backward(ending))
    )

    shape = lambda *dims: jax.ShapeDtypeStruct(dims, f32)
    held = lambda *dims, kind=f32: pltpu.VMEM(dims, kind)
    far = lambda v: pltpu.with_memory_space_constraint(v, pltpu.HBM)
    here = lambda v: pltpu.with_memory_space_constraint(v, pltpu.VMEM)
    ring = lambda v, axis: lax.ppermute(v, axis, [(i, (i - 1) % lax.axis_size(axis)) for i in range(lax.axis_size(axis))])
    swap = lambda v: lax.ppermute(v, "gy", [(0, 1), (1, 0)])
    tall_x = chans * slots

    side, head = pl.pallas_call(
        functools.partial(pack_kernel, rows),
        in_specs=[ANY] * 3,
        out_specs=[VMEM] * 2,
        out_shape=[held(rows + rows * width // LANES, LANES), held(tiles * SUB, LANES)],
        scratch_shapes=[
            pltpu.VMEM((rows, SUB, width), bf16),
            pltpu.VMEM((2, tall, LANES), jnp.int32),
            pltpu.VMEM((2, SUB, tiles * LANES), jnp.int32),
            pltpu.SemaphoreType.DMA((5,)),
        ],
        compiler_params=ROOM,
        name="pack",
    )(far(features), far(labels), far(valid_mask))
    side = ring(side, "gx")
    x, edge, beside = pl.pallas_call(
        functools.partial(logits_kernel, rows, cols, chans, slots, 4),
        in_specs=[VMEM] * 5,
        out_specs=[VMEM] * 3,
        out_shape=[
            held(tall_x, LANES), held(chans + tiles * SUB + SUB, LANES), held(rows, width, kind=bf16),
        ],
        compiler_params=ROOM,
        name="logits",
    )(*(here(v) for v in (features, probe_weight.T, probe_bias.reshape(1, chans), side, head)))
    got = ring(edge, "gy")
    column = pl.BlockSpec((tall, LANES), lambda t: (0, t))
    block = pl.BlockSpec((depth, LANES), lambda t: (0, t))
    ahead = pl.BlockSpec((depth, LANES), lambda t: (0, jnp.minimum(t + 1, tiles - 1)))
    rear = pl.BlockSpec((depth, LANES), lambda t: (t, 0))
    grad, spill, loss = pl.pallas_call(
        functools.partial(inner_kernel, rows, cols, chans, slots, groups),
        grid=(tiles,),
        in_specs=[VMEM] * 3 + [block, block, ahead, ahead, rear, rear, column, column],
        out_specs=[VMEM] * 3,
        out_shape=[held(tall_x, LANES), held(chans, LANES), held(SUB, LANES)],
        scratch_shapes=[
            pltpu.VMEM((2, tall_x, LANES), f32),
            pltpu.VMEM((2 * chans * count, SUB, LANES), f32),
            pltpu.VMEM((2 * count + 1, SUB, LANES), f32),
            pltpu.VMEM((2 * chans * rows, depth), bf16),
            pltpu.VMEM((2 * chans * rows, LANES), f32),
            pltpu.VMEM((tall_x, depth), bf16),
            pltpu.VMEM((tall + SUB, LANES), jnp.int32),
            pltpu.SMEM((1,), f32),
        ],
        compiler_params=ROOM,
        name="inner",
    )(here(x), here(got), here(side), lift, lift_end, lift, lift_end, back, back_end, labels, valid_mask)
    got = lax.ppermute(spill, "gy", [(i, (i + 1) % gy) for i in range(gy)])
    pack = (chans * width // 2 // LANES + SUB, LANES)
    mine, other = pl.pallas_call(
        functools.partial(grad_kernel, rows, cols, chans, slots),
        in_specs=[VMEM] * 5 + [SMEM],
        out_specs=[VMEM] * 2,
        out_shape=[held(*pack)] * 2,
        scratch_shapes=[pltpu.VMEM((tall_x, LANES), f32)],
        compiler_params=ROOM,
        name="grad",
    )(*(here(v) for v in (features, beside, grad, got, loss)), valid_count)

    total = mine + swap(other)
    step = 1
    while step < gx:
        total = total + lax.ppermute(total, "gx", [(i, i ^ step) for i in range(gx)])
        step *= 2
    loss, weight, bias = pl.pallas_call(
        functools.partial(final_kernel, chans),
        in_specs=[VMEM] * 2,
        out_specs=[VMEM] * 3,
        out_shape=[shape(1, 1), shape(chans, width), shape(1, chans)],
        compiler_params=ROOM,
        name="final",
    )(here(total), here(swap(total)))
    return loss.reshape(1), weight.T, bias.reshape(chans)


def solution(mesh):
    return jax.shard_map(
        body,
        mesh=mesh,
        in_specs=(
            P(("groups", "gy"), "gx", None),
            P(),
            P(),
            P(("groups", "gy"), "gx"),
            P(("groups", "gy"), "gx"),
            P(("groups", "gy"), "gx"),
        ),
        out_specs=(P("groups"), P("groups", None), P("groups")),
        check_vma=False,
    )
```

time: 197 us -> 186 us (0.944)
  Pallas kernels: 170 us -> 156 us
  waiting for transfers between devices: 11.2 us -> 17.8 us
  starting transfers between devices: 13.6 us -> 9.66 us
    pallas_call x3 -> x2, Pallas kernels: 164 us -> 153 us  [the longest x1 152 us: body(): pl.pallas_call(functools.partial(inner_kernel, rows, cols, chans, slots,...]
    ppermute x3, starting transfers between devices: 8.64 us -> 2.99 us  [body(): lax.ppermute(total, 'gx', [(i, i ^ step) for i in range(gx)])]
    ppermute x2 -> x3, waiting for transfers between devices: 0.01 us -> 3.74 us  [the longest x2 3.35 us: body(): lax.ppermute(v, axis, [(i, (i - 1) % lax.axis_size(axis)) for i in range(...]
    pallas_call x1, Pallas kernels: 4.54 us -> 0.94 us  [body(): pl.pallas_call(functools.partial(logits_kernel, rows, cols, chans, slots,...]
    ppermute x2 -> x3, starting transfers between devices: 3.23 us -> 6.37 us  [the longest x2 6.16 us: body(): lax.ppermute(v, axis, [(i, (i - 1) % lax.axis_size(axis)) for i in range(...]
    ppermute x3, waiting for transfers between devices: 8.74 us -> 11.7 us  [body(): lax.ppermute(total, 'gx', [(i, i ^ step) for i in range(gx)])]
  transfers between devices with their start and end apart: 10 -> 8, of which waited for: 6 -> 8; matrix products, arithmetic and copies ran while one was open for 0% -> 0% of each run, Pallas kernels for 73% -> 0%
where the time goes in v4:
time: 186 us
  Pallas kernels  156 us (84%)
  waiting for transfers between devices  17.8 us (10%)
  starting transfers between devices  9.66 us (5%)
    pallas_call x1, Pallas kernels, body(): pl.pallas_call(functools.partial(inner_kernel, rows, cols, chans, slots,...  152 us
    ppermute x3, waiting for transfers between devices, body(): lax.ppermute(total, 'gx', [(i, i ^ step) for i in range(gx)])  11.7 us
    ppermute x2, starting transfers between devices, body(): lax.ppermute(v, axis, [(i, (i - 1) % lax.axis_size(axis)) for i in range(...  6.16 us
  transfers between devices with their start and end apart: 8, of which 8 were waited for; matrix products, arithmetic and copies ran while one was open for 0% of the time, Pallas kernels for 0%

profile of v4, /device:TPU:0, one launch (start us, length us, event | category | flops | bytes accessed | tf_op | source)
XLA Modules:
  0.0 186.1 jit_solution(4347224528789444123)
XLA Ops:
  0.6 0.0 copy-start.3
  0.6 0.0 copy-start.4
  0.7 0.0 copy-start.5
  0.7 0.0 copy-start
  0.7 0.0 copy-start.6
  0.7 0.0 copy-start.1
  0.7 0.0 copy-start.2
  0.7 1.4 pack.1
  2.1 6.1 %collective-permute-start = (f32[176,128]{1,0:T(8,128)S(1)}, f32[176,128]{1,0:T(8,128)S(1)}, u32[]{:S(2)}, u32[]{:S(2)}) collective-permute-start(f32[176,128]{1,0:T(8,128)S(1)} %get-tuple-element.16), channel_id=1, source_target_pairs={{0,14},{2,0},{4,2},{6,4},{8,6},{10,8},{12,10},{14,12},{1,15},{3,1}... | collective-permute-start | bytes 270344 | tf_op jit(solution)/shard_map/ppermute | solution.py:412
  8.2 2.1 %collective-permute-done.side_ref.strip_ref = f32[176,128]{1,0:T(8,128)S(1)} collective-permute-done((f32[176,128]{1,0:T(8,128)S(1)}, f32[176,128]{1,0:T(8,128)S(1)}, u32[]{:S(2)}, u32[]{:S(2)}) %collective-permute-start) | collective-permute-done | bytes 90144 | tf_op jit(solution)/shard_map/ppermute | solution.py:412
  10.4 0.0 copy-done
  10.4 0.9 copy-done.7
  11.3 0.7 copy-done.8
  11.9 0.9 logits.1
  12.9 0.1 collective-permute-start.1
  12.9 1.2 collective-permute-done.1.got_ref
  14.1 0.0 copy-done.3
  14.2 151.8 %inner.1 = (f32[768,128]{1,0:T(8,128)S(1)}, f32[32,128]{1,0:T(8,128)S(1)}, f32[8,128]{1,0:T(8,128)S(1)}) custom-call(f32[768,128]{1,0:T(8,128)S(1)} %get-tuple-element.19.x_ref, f32[96,128]{1,0:T(8,128)S(1)} %collective-permute-done.1.got_ref, f32[176,128]{1,0:T(8,128)S(1)} %collective-permute-done.side_ref.strip_ref, bf16[256,896]{1,0:T(8,128)(2,1)S(1)} %copy-done.3, ...), custom_call_target="tpu_custom_call" | custom-call | tf_op jit(solution)/shard_map/inner/pallas_call | solution.py:446
  166.0 0.2 collective-permute-start.2
  166.9 0.4 collective-permute-done.2.got_ref
  167.3 0.7 grad.1
  168.0 0.2 collective-permute-start.3
  168.2 1.1 collective-permute-done.3
  169.4 0.3 collective-permute-start.4
  169.7 4.3 %collective-permute-done.4 = f32[168,128]{1,0:T(8,128)S(1)} collective-permute-done((f32[168,128]{1,0:T(8,128)S(1)}, f32[168,128]{1,0:T(8,128)S(1)}, u32[]{:S(2)}, u32[]{:S(2)}) %collective-permute-start.4) | collective-permute-done | bytes 86048 | tf_op jit(solution)/shard_map/ppermute | solution.py:480
  174.0 0.1 collective-permute-start.5
  174.2 4.4 %collective-permute-done.5 = f32[168,128]{1,0:T(8,128)S(1)} collective-permute-done((f32[168,128]{1,0:T(8,128)S(1)}, f32[168,128]{1,0:T(8,128)S(1)}, u32[]{:S(2)}, u32[]{:S(2)}) %collective-permute-start.5) | collective-permute-done | bytes 86048 | tf_op jit(solution)/shard_map/ppermute | solution.py:480
  178.6 2.5 %collective-permute-start.6 = (f32[168,128]{1,0:T(8,128)S(1)}, f32[168,128]{1,0:T(8,128)S(1)}, u32[]{:S(2)}, u32[]{:S(2)}) collective-permute-start(f32[168,128]{1,0:T(8,128)S(1)} %add.14), channel_id=1, source_target_pairs={{0,8},{2,10},{4,12},{6,14},{8,0},{10,2},{12,4},{14,6},{1,9},{3,11}... | collective-permute-start | bytes 258056 | tf_op jit(solution)/shard_map/ppermute | solution.py:480
  181.1 2.9 %collective-permute-done.6 = f32[168,128]{1,0:T(8,128)S(1)} collective-permute-done((f32[168,128]{1,0:T(8,128)S(1)}, f32[168,128]{1,0:T(8,128)S(1)}, u32[]{:S(2)}, u32[]{:S(2)}) %collective-permute-start.6) | collective-permute-done | bytes 86048 | tf_op jit(solution)/shard_map/ppermute | solution.py:480
  184.1 0.1 collective-permute-start.7
  184.1 1.3 collective-permute-done.7.z_ref
  185.4 0.7 final.1
  (11 shorter events, 0.1 us)
Async XLA Ops:
  0.6 13.5 %copy-start.3 = (bf16[256,896]{1,0:T(8,128)(2,1)S(1)}, bf16[256,896]{1,0:T(8,128)(2,1)}, u32[]{:S(2)}) copy-start(bf16[256,896]{1,0:T(8,128)(2,1)} %constant.8.clone.lift_ref.next_ref) | copy-start | bytes 1376260
  0.6 13.5 %copy-start.4 = (bf16[256,896]{1,0:T(8,128)(2,1)S(1)}, bf16[256,896]{1,0:T(8,128)(2,1)}, u32[]{:S(2)}) copy-start(bf16[256,896]{1,0:T(8,128)(2,1)} %constant.9.clone.lift_end_ref.next_end_ref) | copy-start | bytes 1376260
  0.7 13.5 %copy-start.5 = (bf16[1792,128]{1,0:T(8,128)(2,1)S(1)}, bf16[1792,128]{1,0:T(8,128)(2,1)}, u32[]{:S(2)}) copy-start(bf16[1792,128]{1,0:T(8,128)(2,1)} %constant.10.clone.back_ref) | copy-start | bytes 1376260
  0.7 9.7 %copy-start = (bf16[16,64,1280]{2,1,0:T(8,128)(2,1)S(1)}, bf16[16,64,1280]{2,1,0:T(8,128)(2,1)}, u32[]{:S(2)}) copy-start(bf16[16,64,1280]{2,1,0:T(8,128)(2,1)} %f_ref.5) | copy-start | bytes 7864324
  0.7 13.5 %copy-start.6 = (bf16[1792,128]{1,0:T(8,128)(2,1)S(1)}, bf16[1792,128]{1,0:T(8,128)(2,1)}, u32[]{:S(2)}) copy-start(bf16[1792,128]{1,0:T(8,128)(2,1)} %constant.11.clone.back_end_ref) | copy-start | bytes 1376260
  0.7 13.5 %copy-start.1 = (s32[224,896]{1,0:T(8,128)S(1)}, s32[224,896]{1,0:T(8,128)}, u32[]{:S(2)}) copy-start(s32[224,896]{1,0:T(8,128)} %lab_ref.3) | copy-start | bytes 2408452
  0.7 13.5 %copy-start.2 = (s32[224,896]{1,0:T(8,128)S(1)}, s32[224,896]{1,0:T(8,128)}, u32[]{:S(2)}) copy-start(s32[224,896]{1,0:T(8,128)} %mask_ref.3) | copy-start | bytes 2408452
  2.1 8.2 %collective-permute-start = (f32[176,128]{1,0:T(8,128)S(1)}, f32[176,128]{1,0:T(8,128)S(1)}, u32[]{:S(2)}, u32[]{:S(2)}) collective-permute-start(f32[176,128]{1,0:T(8,128)S(1)} %get-tuple-element.16), channel_id=1, source_target_pairs={{0,14},{2,0},{4,2},{6,4},{8,6},{10,8},{12,10},{14,12},{1,15},{3,1}... | collective-permute-start | bytes 270344 | tf_op jit(solution)/shard_map/ppermute | solution.py:412
  10.4 0.9 copy-start.7
  11.3 0.7 copy-start.8
  12.9 1.3 collective-permute-start.1
  166.0 1.2 collective-permute-start.2
  168.0 1.3 collective-permute-start.3
  169.4 4.7 %collective-permute-start.4 = (f32[168,128]{1,0:T(8,128)S(1)}, f32[168,128]{1,0:T(8,128)S(1)}, u32[]{:S(2)}, u32[]{:S(2)}) collective-permute-start(f32[168,128]{1,0:T(8,128)S(1)} %add.12), channel_id=1, source_target_pairs={{0,2},{2,0},{4,6},{6,4},{8,10},{10,8},{12,14},{14,12},{1,3},{3,1},... | collective-permute-start | bytes 258056 | tf_op jit(solution)/shard_map/ppermute | solution.py:480
  174.0 4.6 %collective-permute-start.5 = (f32[168,128]{1,0:T(8,128)S(1)}, f32[168,128]{1,0:T(8,128)S(1)}, u32[]{:S(2)}, u32[]{:S(2)}) collective-permute-start(f32[168,128]{1,0:T(8,128)S(1)} %add.13), channel_id=1, source_target_pairs={{0,4},{2,6},{4,0},{6,2},{8,12},{10,14},{12,8},{14,10},{1,5},{3,7},... | collective-permute-start | bytes 258056 | tf_op jit(solution)/shard_map/ppermute | solution.py:480
  178.6 5.4 %collective-permute-start.6 = (f32[168,128]{1,0:T(8,128)S(1)}, f32[168,128]{1,0:T(8,128)S(1)}, u32[]{:S(2)}, u32[]{:S(2)}) collective-permute-start(f32[168,128]{1,0:T(8,128)S(1)} %add.14), channel_id=1, source_target_pairs={{0,8},{2,10},{4,12},{6,14},{8,0},{10,2},{12,4},{14,6},{1,9},{3,11}... | collective-permute-start | bytes 258056 | tf_op jit(solution)/shard_map/ppermute | solution.py:480
  184.1 1.3 collective-permute-start.7

commit v5 on v4

--- a/solution.py
+++ b/solution.py
@@ -61,7 +61,9 @@
     return jnp.concatenate([first.astype(bf16), second.astype(bf16)], axis=1)
 
 
-def pack_kernel(rows, f_ref, lab_ref, mask_ref, out_ref, head_ref, f_vmem, l_vmem, h_vmem, sem):
+def pack_kernel(
+    rows, f_ref, lab_ref, mask_ref, w_ref, bias_ref, out_ref, head_ref, weight_ref, shift_ref, f_vmem, l_vmem, h_vmem, b_vmem, sem,
+):
     width = f_vmem.shape[2]
     tiles = head_ref.shape[0] // SUB
     copies = [
@@ -70,6 +72,8 @@
         pltpu.make_async_copy(f_ref.at[:, pl.ds(0, SUB)], f_vmem, sem.at[2]),
         pltpu.make_async_copy(lab_ref.at[pl.ds(0, SUB)], h_vmem.at[0], sem.at[3]),
         pltpu.make_async_copy(mask_ref.at[pl.ds(0, SUB)], h_vmem.at[1], sem.at[4]),
+        pltpu.make_async_copy(w_ref, weight_ref, sem.at[5]),
+        pltpu.make_async_copy(bias_ref, b_vmem, sem.at[6]),
     ]
     for copy in copies:
         copy.start()
@@ -91,41 +95,43 @@
     for t in range(tiles):
         lanes = slice(t * LANES, t * LANES + LANES)
         head_ref[t * SUB : t * SUB + SUB, :] = jnp.where(h_vmem[1, :, lanes] != 0, h_vmem[0, :, lanes], -1).astype(f32)
-
-
-def logits_kernel(
-    rows, cols, chans, slots, per, f_ref, w_ref, bias_ref, side_ref, head_ref, x_ref, e_ref, beside_ref,
-):
+    chans = shift_ref.shape[0]
+    bias = jnp.concatenate([b_vmem[...], jnp.zeros((1, LANES - chans), f32)], axis=1)
+    shift_ref[...] = jnp.broadcast_to(bias, (LANES, LANES)).T[0:chans, :]
+
+
+def score_of(w_ref, shift_ref, block):
+    score = lax.dot_general(w_ref[...], block, (((1,), (1,)), ((), ())), preferred_element_type=f32)
+    score = score + jnp.concatenate([shift_ref[...]] * (block.shape[0] // LANES), axis=1)
+    return (score - jnp.max(score, axis=0, keepdims=True)) * (LOG2E / STEP)
+
+
+def logits_kernel(rows, cols, chans, slots, per, f_ref, w_ref, shift_ref, head_ref, x_ref, e_ref):
     x_ref[...] = jnp.zeros_like(x_ref)
-    bias = jnp.concatenate([bias_ref[...], jnp.zeros((1, LANES - chans), f32)], axis=1)
-    bias = jnp.broadcast_to(bias, (LANES, LANES)).T[0:chans, :]
-    width = f_ref.shape[2]
-
-    def score_of(block):
-        score = lax.dot_general(w_ref[...], block, (((1,), (1,)), ((), ())), preferred_element_type=f32)
-        score = score + jnp.concatenate([bias] * (block.shape[0] // LANES), axis=1)
-        return (score - jnp.max(score, axis=0, keepdims=True)) * (LOG2E / STEP)
-
-    side = jnp.concatenate(
-        [side_ref[rows + k * rows : rows + k * rows + rows, :] for k in range(width // LANES)], axis=1
-    ).astype(bf16)
-    beside_ref[...] = side
-    beyond = score_of(jnp.concatenate([side, jnp.zeros((LANES - rows, width), bf16)], axis=0))
     lane = lax.broadcasted_iota(jnp.int32, (chans, LANES), 1)
     for step in range(rows // per):
-        block = f_ref[step * per : step * per + per].reshape(per * cols, width)
-        score = score_of(block)
+        score = score_of(w_ref, shift_ref, f_ref[step * per : step * per + per].reshape(per * cols, f_ref.shape[2]))
         for k in range(per):
             i, off = step * per + k, k * cols
             tile = score[:, off // LANES * LANES : off // LANES * LANES + LANES]
             if off % LANES:
                 tile = pltpu.roll(tile, LANES - off % LANES, 1)
-            tile = jnp.where(lane < cols, tile, jnp.where(lane == cols, pltpu.roll(beyond, cols - i, 1), 0.0))
+            tile = jnp.where(lane < cols, tile, 0.0)
             x_ref[pl.ds(i, chans, stride=slots), :] = tile
             if i == 0:
                 e_ref[0:chans, :] = tile
-    e_ref[chans : chans + head_ref.shape[0], :] = head_ref[...]
-    e_ref[chans + head_ref.shape[0] :, :] = side_ref[0:SUB, :]
+    e_ref[chans:, :] = head_ref[...]
+
+
+def beside_kernel(rows, chans, side_ref, w_ref, shift_ref, beside_ref, out_ref):
+    width = w_ref.shape[1]
+    side = jnp.concatenate(
+        [side_ref[rows + k * rows : rows + k * rows + rows, :] for k in range(width // LANES)], axis=1
+    ).astype(bf16)
+    beside_ref[...] = side
+    side = jnp.concatenate([side, jnp.zeros((LANES - rows, width), bf16)], axis=0)
+    out_ref[0:chans, :] = score_of(w_ref, shift_ref, side)
+    out_ref[chans:, :] = side_ref[0:SUB, :]
 
 
 def softmax_fast(groups, chans, slots, fold, w_ref, p_ref):
@@ -176,7 +182,7 @@
     return sums, losses
 
 
-def pixels(groups, chans, slots, fold, lab_ref, fast, w_ref, p_ref, s_ref, lhs_ref):
+def pixels(groups, chans, slots, fold, lab_ref, fast, prepare, w_ref, p_ref, s_ref, lhs_ref):
     count = 2 * groups * HALF
     labels = []
     for half in range(2):
@@ -192,6 +198,7 @@
         for k in range(count):
             s_ref[k] = sums[k]
         s_ref[count] = jnp.zeros((SUB, LANES), f32)
+        prepare()
 
     @pl.when(jnp.logical_not(fast))
     def _():
@@ -199,6 +206,7 @@
         for k in range(count):
             s_ref[k] = sums[k]
         s_ref[count] = losses
+        prepare()
 
     loss = jnp.zeros((SUB, LANES), f32)
     scale = []
@@ -254,14 +262,24 @@
     return loss + LN2 * jnp.where(fast, -picked, s_ref[count])
 
 
-def inner_kernel(
-    rows, cols, chans, slots, groups, x_ref, got_ref, strip_ref, lift_ref, lift_end_ref, next_ref, next_end_ref,
-    back_ref, back_end_ref, lab_ref, mask_ref, out_ref, spill_ref, loss_ref,
-    w_ref, p_ref, s_ref, lhs_ref, sum_ref, stack_ref, tile_ref, floor_ref,
-):
+def inner_kernel(rows, cols, chans, slots, groups, part, begin, tiles, *refs):
+    (got_ref, lift_ref, lift_end_ref, next_ref, next_end_ref, back_ref, back_end_ref, lab_ref, mask_ref), refs = (
+        refs[:9], refs[9:],
+    )
+    if part == 0:
+        (x_ref, sum_ref, loss_ref, stack_ref, floor_ref), refs = refs[:5], refs[5:]
+    elif part == 1:
+        (sum_in_ref, loss_in_ref, stack_ref, floor_ref, sum_ref, loss_ref), refs = refs[:6], refs[6:]
+    else:
+        (x_ref, beyond_ref, corner_ref, strip_ref, sum_in_ref, loss_in_ref), refs = refs[:6], refs[6:]
+        (out_ref, spill_ref, loss_ref), refs = refs[:3], refs[3:]
+    (w_ref, p_ref, s_ref, lhs_ref, tile_ref), refs = refs[:5], refs[5:]
+    if part == 2:
+        sum_ref, stack_ref, floor_ref = refs
     step = pl.program_id(0)
     steps = pl.num_programs(0)
     now = lax.rem(step, 2)
+    which = lax.rem(step + begin, tiles)
     last_col = lax.axis_index("gx") == lax.axis_size("gx") - 1
     last_row = lax.axis_index("gy") == lax.axis_size("gy") - 1
     tall = rows * PATCH
@@ -269,55 +287,73 @@
 
     @pl.when(step == 0)
     def _():
-        w_ref[0] = x_ref[...]
-        w_ref[0, pl.ds(rows, chans, stride=slots), :] = got_ref[0:chans, :]
-        full = w_ref[0]
-        floor_ref[0] = jnp.min(full) * STEP
-        stack_ref[...] = stack3(full)
-        sum_ref[...] = jnp.zeros_like(sum_ref)
-        loss_ref[...] = jnp.zeros_like(loss_ref)
+        if part == 0:
+            sum_ref[...] = jnp.zeros_like(sum_ref)
+            loss_ref[...] = jnp.zeros_like(loss_ref)
+        else:
+            sum_ref[...] = sum_in_ref[...]
+            loss_ref[...] = loss_in_ref[...]
+        if part != 1:
+            w_ref[0] = x_ref[...]
+            w_ref[0, pl.ds(rows, chans, stride=slots), :] = got_ref[0:chans, :]
+            if part == 2:
+                wide = lax.broadcasted_iota(jnp.int32, (chans, LANES), 1)
+                for i in range(rows + 1):
+                    column = beyond_ref[0:chans, :] if i < rows else corner_ref[0:chans, :]
+                    column = pltpu.roll(column, cols - i if i < rows else cols, 1)
+                    pick = pl.ds(i, chans, stride=slots)
+                    w_ref[0, pick, :] = jnp.where(wide == cols, column, w_ref[0, pick, :])
+            full = w_ref[0]
+            floor_ref[0] = jnp.min(full) * STEP
+            stack_ref[...] = stack3(full)
         table = jnp.where(last_col, lift_end_ref[...], lift_ref[...])
         w_ref[0] = jnp.dot(stack_ref[...], table, preferred_element_type=f32)
 
     tile_ref[0:tall, :] = jnp.where(mask_ref[...] != 0, lab_ref[...], -1)
-    tile_ref[tall : tall + SUB, :] = got_ref[pl.ds(pl.multiple_of(chans + step * SUB, SUB), SUB), :].astype(jnp.int32)
-
-    @pl.when(step == 0)
-    def _():
-        for j in range(PATCH):
-            for b in range(groups):
-                pick = pl.ds(b * SUB * PATCH + j, SUB, stride=PATCH)
-                strip = strip_ref[b * SUB : b * SUB + SUB, :]
+    tile_ref[tall : tall + SUB, :] = got_ref[pl.ds(pl.multiple_of(chans + which * SUB, SUB), SUB), :].astype(jnp.int32)
+
+    if part == 2:
+
+        @pl.when(which == 0)
+        def _():
+            for j in range(PATCH):
+                for b in range(groups):
+                    pick = pl.ds(b * SUB * PATCH + j, SUB, stride=PATCH)
+                    strip = strip_ref[b * SUB : b * SUB + SUB, :]
+                    strip = pltpu.roll(strip, LANES - j * HALF, 1) if j else strip
+                    tile_ref[pick, :] = jnp.where(lane < HALF, strip.astype(jnp.int32), tile_ref[pick, :])
+            for j in range(HALF):
+                strip = corner_ref[chans : chans + 1, :]
                 strip = pltpu.roll(strip, LANES - j * HALF, 1) if j else strip
-                tile_ref[pick, :] = jnp.where(lane < HALF, strip.astype(jnp.int32), tile_ref[pick, :])
-        at = chans + steps * SUB
-        for j in range(HALF):
-            strip = got_ref[at : at + 1, :]
-            strip = pltpu.roll(strip, LANES - j * HALF, 1) if j else strip
-            row = tile_ref[tall + j : tall + j + 1, :]
-            tile_ref[tall + j : tall + j + 1, :] = jnp.where(lane[0:1] < HALF, strip.astype(jnp.int32), row)
+                row = tile_ref[tall + j : tall + j + 1, :]
+                tile_ref[tall + j : tall + j + 1, :] = jnp.where(lane[0:1] < HALF, strip.astype(jnp.int32), row)
 
     flat = jnp.full((SUB, LANES), 1.0 / STEP, f32)
     sub = lax.broadcasted_iota(jnp.int32, (SUB, LANES), 0)
     fold = [flat] * (groups - 1) + [jnp.where(last_row & (sub == SUB - 1), 0.0, flat)]
     fast = floor_ref[0] >= FLOOR
-    loss_ref[...] += pixels(groups, chans, slots, fold, tile_ref, fast, w_ref.at[now], p_ref, s_ref, lhs_ref)
-    table = jnp.where(last_col, next_end_ref[...], next_ref[...])
-    w_ref[1 - now] = jnp.dot(stack_ref[...], table, preferred_element_type=f32)
+
+    def prepare():
+        table = jnp.where(last_col, next_end_ref[...], next_ref[...])
+        w_ref[1 - now] = jnp.dot(stack_ref[...], table, preferred_element_type=f32)
+
+    loss_ref[...] += pixels(groups, chans, slots, fold, tile_ref, fast, prepare, w_ref.at[now], p_ref, s_ref, lhs_ref)
     table = jnp.where(last_col, back_end_ref[...], back_ref[...])
     sum_ref[...] += jnp.dot(lhs_ref[...], table, preferred_element_type=f32)
 
-    @pl.when(step == steps - 1)
-    def _():
-        w_ref[0] = jnp.zeros_like(w_ref[0])
-        high = groups * SUB
-        for c in range(chans):
-            for kind in range(2):
-                at = (kind * chans + c) * high
-                row = c * slots + kind
-                w_ref[0, row : row + high, :] += sum_ref[at : at + high, :]
-        out_ref[...] = w_ref[0] * (1.0 / STEP)
-        spill_ref[...] = out_ref[pl.ds(rows, chans, stride=slots), :]
+    if part == 2:
+
+        @pl.when(step == steps - 1)
+        def _():
+            w_ref[0] = jnp.zeros_like(w_ref[0])
+            high = groups * SUB
+            for c in range(chans):
+                for kind in range(2):
+                    at = (kind * chans + c) * high
+                    row = c * slots + kind
+                    w_ref[0, row : row + high, :] += sum_ref[at : at + high, :]
+            out_ref[...] = w_ref[0] * (1.0 / STEP)
+            spill_ref[...] = out_ref[pl.ds(rows, chans, stride=slots), :]
 
 
 def grad_kernel(
@@ -413,55 +449,81 @@
     swap = lambda v: lax.ppermute(v, "gy", [(0, 1), (1, 0)])
     tall_x = chans * slots
 
-    side, head = pl.pallas_call(
+    side, head, weight, shift = pl.pallas_call(
         functools.partial(pack_kernel, rows),
-        in_specs=[ANY] * 3,
-        out_specs=[VMEM] * 2,
-        out_shape=[held(rows + rows * width // LANES, LANES), held(tiles * SUB, LANES)],
+        in_specs=[ANY] * 5,
+        out_specs=[VMEM] * 4,
+        out_shape=[
+            held(rows + rows * width // LANES, LANES), held(tiles * SUB, LANES), held(chans, width, kind=bf16),
+            held(chans, LANES),
+        ],
         scratch_shapes=[
             pltpu.VMEM((rows, SUB, width), bf16),
             pltpu.VMEM((2, tall, LANES), jnp.int32),
             pltpu.VMEM((2, SUB, tiles * LANES), jnp.int32),
-            pltpu.SemaphoreType.DMA((5,)),
+            pltpu.VMEM((1, chans), f32),
+            pltpu.SemaphoreType.DMA((7,)),
         ],
         compiler_params=ROOM,
         name="pack",
-    )(far(features), far(labels), far(valid_mask))
+    )(*(far(v) for v in (features, labels, valid_mask, probe_weight.T, probe_bias.reshape(1, chans))))
     side = ring(side, "gx")
-    x, edge, beside = pl.pallas_call(
+    x, edge = pl.pallas_call(
         functools.partial(logits_kernel, rows, cols, chans, slots, 4),
-        in_specs=[VMEM] * 5,
-        out_specs=[VMEM] * 3,
-        out_shape=[
-            held(tall_x, LANES), held(chans + tiles * SUB + SUB, LANES), held(rows, width, kind=bf16),
-        ],
+        in_specs=[VMEM] * 4,
+        out_specs=[VMEM] * 2,
+        out_shape=[held(tall_x, LANES), held(chans + tiles * SUB, LANES)],
         compiler_params=ROOM,
         name="logits",
-    )(*(here(v) for v in (features, probe_weight.T, probe_bias.reshape(1, chans), side, head)))
+    )(*(here(v) for v in (features, weight, shift, head)))
     got = ring(edge, "gy")
-    column = pl.BlockSpec((tall, LANES), lambda t: (0, t))
-    block = pl.BlockSpec((depth, LANES), lambda t: (0, t))
-    ahead = pl.BlockSpec((depth, LANES), lambda t: (0, jnp.minimum(t + 1, tiles - 1)))
-    rear = pl.BlockSpec((depth, LANES), lambda t: (t, 0))
-    grad, spill, loss = pl.pallas_call(
-        functools.partial(inner_kernel, rows, cols, chans, slots, groups),
-        grid=(tiles,),
-        in_specs=[VMEM] * 3 + [block, block, ahead, ahead, rear, rear, column, column],
-        out_specs=[VMEM] * 3,
-        out_shape=[held(tall_x, LANES), held(chans, LANES), held(SUB, LANES)],
-        scratch_shapes=[
-            pltpu.VMEM((2, tall_x, LANES), f32),
-            pltpu.VMEM((2 * chans * count, SUB, LANES), f32),
-            pltpu.VMEM((2 * count + 1, SUB, LANES), f32),
-            pltpu.VMEM((2 * chans * rows, depth), bf16),
-            pltpu.VMEM((2 * chans * rows, LANES), f32),
-            pltpu.VMEM((tall_x, depth), bf16),
-            pltpu.VMEM((tall + SUB, LANES), jnp.int32),
-            pltpu.SMEM((1,), f32),
-        ],
+
+    sums = (2 * chans * rows, LANES)
+    stacked = held(tall_x, depth, kind=bf16)
+
+    def inner(part, begin, steps, *args):
+        at = lambda t: (t + begin) % tiles
+        column = pl.BlockSpec((tall, LANES), lambda t: (0, at(t)))
+        block = pl.BlockSpec((depth, LANES), lambda t: (0, at(t)))
+        ahead = pl.BlockSpec((depth, LANES), lambda t: (0, at(t + 1)))
+        rear = pl.BlockSpec((depth, LANES), lambda t: (at(t), 0))
+        outs = [
+            ([held(*sums), held(SUB, LANES), stacked, shape(1)], [VMEM] * 3 + [SMEM], [VMEM]),
+            ([held(*sums), held(SUB, LANES)], [VMEM] * 2, [VMEM] * 3 + [SMEM]),
+            ([held(tall_x, LANES), held(chans, LANES), held(SUB, LANES)], [VMEM] * 3, [VMEM] * 6),
+        ][part]
+        return pl.pallas_call(
+            functools.partial(inner_kernel, rows, cols, chans, slots, groups, part, begin, tiles),
+            grid=(steps,),
+            in_specs=[VMEM, block, block, ahead, ahead, rear, rear, column, column] + outs[2],
+            out_specs=outs[1],
+            out_shape=outs[0],
+            scratch_shapes=[
+                pltpu.VMEM((2, tall_x, LANES), f32),
+                pltpu.VMEM((2 * chans * count, SUB, LANES), f32),
+                pltpu.VMEM((2 * count + 1, SUB, LANES), f32),
+                pltpu.VMEM((2 * chans * rows, depth), bf16),
+                pltpu.VMEM((tall + SUB, LANES), jnp.int32),
+            ] + ([pltpu.VMEM(sums, f32), stacked, pltpu.SMEM((1,), f32)] if part == 2 else []),
+            cost_estimate=pl.CostEstimate(flops=10**9, bytes_accessed=2 * 10**6, transcendentals=10**6),
+            compiler_params=ROOM,
+            name=("inner_head", "inner_middle", "inner_tail")[part],
+        )(here(got), lift, lift_end, lift, lift_end, back, back_end, labels, valid_mask, *args)
+
+    middle = tiles // 2 + 1
+    total, loss, stack, floor = inner(0, 1, middle - 1, here(x))
+    side, total = lax.optimization_barrier((side, total))
+    beside, beyond = pl.pallas_call(
+        functools.partial(beside_kernel, rows, chans),
+        in_specs=[VMEM] * 3,
+        out_specs=[VMEM] * 2,
+        out_shape=[held(rows, width, kind=bf16), held(chans + SUB, LANES)],
         compiler_params=ROOM,
-        name="inner",
-    )(here(x), here(got), here(side), lift, lift_end, lift, lift_end, back, back_end, labels, valid_mask)
+        name="beside",
+    )(here(side), here(weight), here(shift))
+    corner = ring(beyond, "gy")
+    total, loss = inner(1, middle, tiles - 1 - middle, *(here(v) for v in (total, loss, stack)), floor)
+    grad, spill, loss = inner(2, tiles - 1, 2, *(here(v) for v in (x, beyond, corner, side, total, loss)))
     got = lax.ppermute(spill, "gy", [(i, (i + 1) % gy) for i in range(gy)])
     pack = (chans * width // 2 // LANES + SUB, LANES)
     mine, other = pl.pallas_call(

time: 186 us -> 186 us (level)
  Pallas kernels: 156 us -> 159 us
  starting transfers between devices: 9.66 us -> 7.49 us
    ppermute x2 -> x3, waiting for transfers between devices: 3.35 us -> 0.01 us  [body(): lax.ppermute(v, axis, [(i, (i - 1) % lax.axis_size(axis)) for i in range(...]
    ppermute x3, waiting for transfers between devices: 11.7 us -> 15 us  [body(): lax.ppermute(total, 'gx', [(i, i ^ step) for i in range(gx)])]
    pallas_call x2 -> x5, Pallas kernels: 153 us -> 157 us  [the longest x3 155 us: inner(): pl.pallas_call(functools.partial(inner_kernel, rows, cols, chans, slots,...]
    ppermute x3, starting transfers between devices: 2.99 us -> 0.21 us  [body(): lax.ppermute(total, 'gx', [(i, i ^ step) for i in range(gx)])]
    ppermute x2 -> x3, starting transfers between devices: 6.16 us -> 6.39 us  [body(): lax.ppermute(v, axis, [(i, (i - 1) % lax.axis_size(axis)) for i in range(...]
  transfers between devices with their start and end apart: 8 -> 9, of which waited for: 8 -> 6; matrix products, arithmetic and copies ran while one was open for 0% -> 0% of each run, Pallas kernels for 0% -> 59%
where the time goes in v5:
time: 186 us
  Pallas kernels  159 us (85%)
  waiting for transfers between devices  17.4 us (9%)
  starting transfers between devices  7.49 us (4%)
    pallas_call x3, Pallas kernels, inner(): pl.pallas_call(functools.partial(inner_kernel, rows, cols, chans, slots,...  155 us
    ppermute x3, waiting for transfers between devices, body(): lax.ppermute(total, 'gx', [(i, i ^ step) for i in range(gx)])  15 us
    ppermute x3, starting transfers between devices, body(): lax.ppermute(v, axis, [(i, (i - 1) % lax.axis_size(axis)) for i in range(...  6.39 us
  transfers between devices with their start and end apart: 9, of which 6 were waited for; matrix products, arithmetic and copies ran while one was open for 0% of the time, Pallas kernels for 59%

profile of v5, /device:TPU:0, one launch (start us, length us, event | category | flops | bytes accessed | tf_op | source)
XLA Modules:
  0.0 185.8 jit_solution(7773485281097885111)
XLA Ops:
  0.6 0.0 copy-start
  0.6 0.0 copy-start.1
  0.7 0.0 copy-start.2
  0.7 0.0 copy-start.5
  0.7 0.0 copy-start.6
  0.7 1.5 pack.1
  2.2 0.4 copy-done
  2.6 1.0 logits.1
  3.6 0.6 collective-permute-start.1
  4.2 5.6 %collective-permute-start = (f32[176,128]{1,0:T(8,128)S(1)}, f32[176,128]{1,0:T(8,128)S(1)}, u32[]{:S(2)}, u32[]{:S(2)}) collective-permute-start(f32[176,128]{1,0:T(8,128)S(1)} %get-tuple-element.27), channel_id=1, source_target_pairs={{0,14},{2,0},{4,2},{6,4},{8,6},{10,8},{12,10},{14,12},{1,15},{3,1}... | collective-permute-start | bytes 270344 | tf_op jit(solution)/shard_map/ppermute | solution.py:448
  9.8 0.0 collective-permute-done.1.refs_0_
  9.8 66.0 %inner_head.1 = (f32[1024,128]{1,0:T(8,128)S(1)}, f32[8,128]{1,0:T(8,128)S(1)}, bf16[768,256]{1,0:T(8,128)(2,1)S(1)}, f32[1]{0:T(128)}) custom-call(f32[88,128]{1,0:T(8,128)S(1)} %collective-permute-done.1.refs_0_, bf16[256,896]{1,0:T(8,128)(2,1)S(1)} %copy-done.2, bf16[256,896]{1,0:T(8,128)(2,1)S(1)} %copy-done.1, bf16[256,896]{1,0:T(8,128)(2,1)S(1)} %copy-done.2, ...), custom_call_target="tpu_custom_call" | custom-call | flops 1000000000 | bytes 2000000 | tf_op jit(solution)/shard_map/inner_head/pallas_call | solution.py:495
  75.8 0.0 collective-permute-done.side_ref.refs_12_
  75.8 0.2 beside.1
  76.0 0.2 collective-permute-start.2
  76.2 44.5 %inner_middle.1 = (f32[1024,128]{1,0:T(8,128)S(1)}, f32[8,128]{1,0:T(8,128)S(1)}) custom-call(f32[88,128]{1,0:T(8,128)S(1)} %collective-permute-done.1.refs_0_, bf16[256,896]{1,0:T(8,128)(2,1)S(1)} %copy-done.2, bf16[256,896]{1,0:T(8,128)(2,1)S(1)} %copy-done.1, bf16[256,896]{1,0:T(8,128)(2,1)S(1)} %copy-done.2, bf16[256,896]{1,0:T(8,128)(2,1)S(1)} %copy-done.1, ...), custom_call_target="tpu_custom_call" | custom-call | flops 1000000000 | bytes 2000000 | tf_op jit(solution)/shard_map/inner_middle/pallas_call | solution.py:495
  120.8 0.0 collective-permute-done.2.refs_11_
  120.8 44.3 %inner_tail.1 = (f32[768,128]{1,0:T(8,128)S(1)}, f32[32,128]{1,0:T(8,128)S(1)}, f32[8,128]{1,0:T(8,128)S(1)}) custom-call(f32[88,128]{1,0:T(8,128)S(1)} %collective-permute-done.1.refs_0_, bf16[256,896]{1,0:T(8,128)(2,1)S(1)} %copy-done.2, bf16[256,896]{1,0:T(8,128)(2,1)S(1)} %copy-done.1, bf16[256,896]{1,0:T(8,128)(2,1)S(1)} %copy-done.2, ...), custom_call_target="tpu_custom_call" | custom-call | flops 1000000000 | bytes 2000000 | tf_op jit(solution)/shard_map/inner_tail/pallas_call | solution.py:495
  165.1 0.4 collective-permute-start.3
  166.2 0.2 collective-permute-done.3.got_ref
  166.4 0.7 grad.1
  167.1 0.4 collective-permute-start.4
  167.5 0.9 collective-permute-done.4
  168.4 0.1 collective-permute-start.5
  168.5 4.8 %collective-permute-done.5 = f32[168,128]{1,0:T(8,128)S(1)} collective-permute-done((f32[168,128]{1,0:T(8,128)S(1)}, f32[168,128]{1,0:T(8,128)S(1)}, u32[]{:S(2)}, u32[]{:S(2)}) %collective-permute-start.5) | collective-permute-done | bytes 86048 | tf_op jit(solution)/shard_map/ppermute | solution.py:542
  173.3 0.1 collective-permute-start.6
  173.4 4.5 %collective-permute-done.6 = f32[168,128]{1,0:T(8,128)S(1)} collective-permute-done((f32[168,128]{1,0:T(8,128)S(1)}, f32[168,128]{1,0:T(8,128)S(1)}, u32[]{:S(2)}, u32[]{:S(2)}) %collective-permute-start.6) | collective-permute-done | bytes 86048 | tf_op jit(solution)/shard_map/ppermute | solution.py:542
  177.9 0.1 collective-permute-start.7
  177.9 5.7 %collective-permute-done.7 = f32[168,128]{1,0:T(8,128)S(1)} collective-permute-done((f32[168,128]{1,0:T(8,128)S(1)}, f32[168,128]{1,0:T(8,128)S(1)}, u32[]{:S(2)}, u32[]{:S(2)}) %collective-permute-start.7) | collective-permute-done | bytes 86048 | tf_op jit(solution)/shard_map/ppermute | solution.py:542
  183.7 0.1 collective-permute-start.8
  183.8 1.3 collective-permute-done.8.z_ref
  185.0 0.7 final.1
  (12 shorter events, 0.1 us)
Async XLA Ops:
  0.6 2.0 %copy-start = (bf16[16,64,1280]{2,1,0:T(8,128)(2,1)S(1)}, bf16[16,64,1280]{2,1,0:T(8,128)(2,1)}, u32[]{:S(2)}) copy-start(bf16[16,64,1280]{2,1,0:T(8,128)(2,1)} %f_ref.5) | copy-start | bytes 7864324
  0.6 9.1 %copy-start.1 = (bf16[256,896]{1,0:T(8,128)(2,1)S(1)}, bf16[256,896]{1,0:T(8,128)(2,1)}, u32[]{:S(2)}) copy-start(bf16[256,896]{1,0:T(8,128)(2,1)} %constant.9.clone.refs_2_.refs_4_) | copy-start | bytes 1376260
  0.7 9.1 %copy-start.2 = (bf16[256,896]{1,0:T(8,128)(2,1)S(1)}, bf16[256,896]{1,0:T(8,128)(2,1)}, u32[]{:S(2)}) copy-start(bf16[256,896]{1,0:T(8,128)(2,1)} %constant.8.clone.refs_1_.refs_3_) | copy-start | bytes 1376260
  0.7 9.1 %copy-start.3 = (s32[224,896]{1,0:T(8,128)S(1)}, s32[224,896]{1,0:T(8,128)}, u32[]{:S(2)}) copy-start(s32[224,896]{1,0:T(8,128)} %refs_7_.5) | copy-start | bytes 2408452
  0.7 9.1 %copy-start.4 = (s32[224,896]{1,0:T(8,128)S(1)}, s32[224,896]{1,0:T(8,128)}, u32[]{:S(2)}) copy-start(s32[224,896]{1,0:T(8,128)} %refs_8_.5) | copy-start | bytes 2408452
  0.7 9.1 %copy-start.5 = (bf16[1792,128]{1,0:T(8,128)(2,1)S(1)}, bf16[1792,128]{1,0:T(8,128)(2,1)}, u32[]{:S(2)}) copy-start(bf16[1792,128]{1,0:T(8,128)(2,1)} %constant.11.clone.refs_6_) | copy-start | bytes 1376260
  0.7 9.1 %copy-start.6 = (bf16[1792,128]{1,0:T(8,128)(2,1)S(1)}, bf16[1792,128]{1,0:T(8,128)(2,1)}, u32[]{:S(2)}) copy-start(bf16[1792,128]{1,0:T(8,128)(2,1)} %constant.10.clone.refs_5_) | copy-start | bytes 1376260
  3.6 6.2 %collective-permute-start.1 = (f32[88,128]{1,0:T(8,128)S(1)}, f32[88,128]{1,0:T(8,128)S(1)}, u32[]{:S(2)}, u32[]{:S(2)}) collective-permute-start(f32[88,128]{1,0:T(8,128)S(1)} %get-tuple-element.31), channel_id=1, source_target_pairs={{0,1},{1,0},{2,3},{3,2},{4,5},{5,4},{6,7},{7,6},{8,9},{9,8},{10,11... | collective-permute-start | bytes 135176 | tf_op jit(solution)/shard_map/ppermute | solution.py:448
  4.2 71.7 %collective-permute-start = (f32[176,128]{1,0:T(8,128)S(1)}, f32[176,128]{1,0:T(8,128)S(1)}, u32[]{:S(2)}, u32[]{:S(2)}) collective-permute-start(f32[176,128]{1,0:T(8,128)S(1)} %get-tuple-element.27), channel_id=1, source_target_pairs={{0,14},{2,0},{4,2},{6,4},{8,6},{10,8},{12,10},{14,12},{1,15},{3,1}... | collective-permute-start | bytes 270344 | tf_op jit(solution)/shard_map/ppermute | solution.py:448
  76.0 44.8 %collective-permute-start.2 = (f32[40,128]{1,0:T(8,128)S(1)}, f32[40,128]{1,0:T(8,128)S(1)}, u32[]{:S(2)}, u32[]{:S(2)}) collective-permute-start(f32[40,128]{1,0:T(8,128)S(1)} %get-tuple-element.36.refs_10_), channel_id=1, source_target_pairs={{0,1},{1,0},{2,3},{3,2},{4,5},{5,4},{6,7},{7,6},{8,9},{9,8},{10,11... | collective-permute-start | bytes 61448 | tf_op jit(solution)/shard_map/ppermute | solution.py:448
  165.1 1.2 collective-permute-start.3
  167.1 1.3 collective-permute-start.4
  168.4 4.8 %collective-permute-start.5 = (f32[168,128]{1,0:T(8,128)S(1)}, f32[168,128]{1,0:T(8,128)S(1)}, u32[]{:S(2)}, u32[]{:S(2)}) collective-permute-start(f32[168,128]{1,0:T(8,128)S(1)} %add.12), channel_id=1, source_target_pairs={{0,2},{2,0},{4,6},{6,4},{8,10},{10,8},{12,14},{14,12},{1,3},{3,1},... | collective-permute-start | bytes 258056 | tf_op jit(solution)/shard_map/ppermute | solution.py:542
  173.3 4.6 %collective-permute-start.6 = (f32[168,128]{1,0:T(8,128)S(1)}, f32[168,128]{1,0:T(8,128)S(1)}, u32[]{:S(2)}, u32[]{:S(2)}) collective-permute-start(f32[168,128]{1,0:T(8,128)S(1)} %add.13), channel_id=1, source_target_pairs={{0,4},{2,6},{4,0},{6,2},{8,12},{10,14},{12,8},{14,10},{1,5},{3,7},... | collective-permute-start | bytes 258056 | tf_op jit(solution)/shard_map/ppermute | solution.py:542
  177.9 5.8 %collective-permute-start.7 = (f32[168,128]{1,0:T(8,128)S(1)}, f32[168,128]{1,0:T(8,128)S(1)}, u32[]{:S(2)}, u32[]{:S(2)}) collective-permute-start(f32[168,128]{1,0:T(8,128)S(1)} %add.14), channel_id=1, source_target_pairs={{0,8},{2,10},{4,12},{6,14},{8,0},{10,2},{12,4},{14,6},{1,9},{3,11}... | collective-permute-start | bytes 258056 | tf_op jit(solution)/shard_map/ppermute | solution.py:542
  183.7 1.3 collective-permute-start.8

commit v6 on v5

--- a/solution.py
+++ b/solution.py
@@ -106,7 +106,7 @@
     return (score - jnp.max(score, axis=0, keepdims=True)) * (LOG2E / STEP)
 
 
-def logits_kernel(rows, cols, chans, slots, per, f_ref, w_ref, shift_ref, head_ref, x_ref, e_ref):
+def logits_kernel(rows, cols, chans, slots, per, f_ref, w_ref, shift_ref, head_ref, side_ref, x_ref, e_ref):
     x_ref[...] = jnp.zeros_like(x_ref)
     lane = lax.broadcasted_iota(jnp.int32, (chans, LANES), 1)
     for step in range(rows // per):
@@ -120,7 +120,8 @@
             x_ref[pl.ds(i, chans, stride=slots), :] = tile
             if i == 0:
                 e_ref[0:chans, :] = tile
-    e_ref[chans:, :] = head_ref[...]
+    e_ref[chans : chans + head_ref.shape[0], :] = head_ref[...]
+    e_ref[chans + head_ref.shape[0] :, :] = side_ref[0:SUB, :]
 
 
 def beside_kernel(rows, chans, side_ref, w_ref, shift_ref, beside_ref, out_ref):
@@ -262,12 +263,65 @@
     return loss + LN2 * jnp.where(fast, -picked, s_ref[count])
 
 
+def first_columns(rows, groups, chans, slots, last_row, own_ref, got_ref, w_ref, p_ref, lhs_ref):
+    lane = lax.broadcasted_iota(jnp.int32, (SUB, LANES), 1)
+    sub = lax.broadcasted_iota(jnp.int32, (SUB, LANES), 0)
+    turn = HALF * HALF
+    share = jnp.zeros((SUB, LANES), f32)
+    for k in range(PATCH):
+        share = jnp.where(lane >= k * HALF, (2 * k + 1.0) / STEP, share)
+    end = jnp.where(last_row & (sub == SUB - 1), jnp.where(lane < turn, 0.0, 1.0), share)
+    shares = [share] * (groups - 1) + [end]
+    tall = groups * SUB
+    loss = jnp.zeros((SUB, LANES), f32)
+    scale, labels = [], []
+    for b in range(groups):
+        upper = own_ref[b * SUB : b * SUB + SUB, :]
+        at = (b + 1) * SUB
+        lower = got_ref[got_ref.shape[0] - SUB :, :] if at == rows else own_ref[at : at + SUB, :]
+        lower = jnp.where(sub == SUB - 1, pltpu.roll(lower, SUB - 1, 0), pltpu.roll(upper, SUB - 1, 0))
+        label = jnp.where(lane < turn, pltpu.roll(upper, LANES - turn, 1), pltpu.roll(lower, turn, 1))
+        label = jnp.where(lane < PATCH * HALF, label, -1.0).astype(jnp.int32)
+        top = None
+        for c in range(chans):
+            row = c * slots + SUB * b
+            v = w_ref[row : row + SUB, :]
+            v = v + (w_ref[row + 1 : row + 1 + SUB, :] - v) * shares[b]
+            p_ref[c * groups + b] = v
+            top = v if top is None else jnp.maximum(top, v)
+        total = picked = jnp.zeros((SUB, LANES), f32)
+        for c in range(chans):
+            v = p_ref[c * groups + b] - top
+            picked = jnp.where(label == c, v, picked)
+            v = jnp.exp2(v)
+            p_ref[c * groups + b] = v
+            total = total + v
+        weight = jnp.where(label >= 0, 1.0, 0.0)
+        loss = loss + weight * (jnp.log(total) - LN2 * picked)
+        scale.append(weight / total)
+        labels.append(label)
+    for c in range(chans):
+        parts = [[], []]
+        for b in range(groups):
+            g = p_ref[c * groups + b] * scale[b] - jnp.where(labels[b] == c, 1.0, 0.0)
+            below = g * shares[b]
+            parts[0].append(g - below)
+            parts[1].append(below)
+        for kind in range(2):
+            g = jnp.concatenate(parts[kind], axis=0)
+            hi = g.astype(bf16)
+            at = (kind * chans + c) * tall
+            lhs_ref[at : at + tall, 0:LANES] = hi
+            lhs_ref[at : at + tall, LANES:] = (g - hi.astype(f32)).astype(bf16)
+    return loss
+
+
 def inner_kernel(rows, cols, chans, slots, groups, part, begin, tiles, *refs):
     (got_ref, lift_ref, lift_end_ref, next_ref, next_end_ref, back_ref, back_end_ref, lab_ref, mask_ref), refs = (
         refs[:9], refs[9:],
     )
     if part == 0:
-        (x_ref, sum_ref, loss_ref, stack_ref, floor_ref), refs = refs[:5], refs[5:]
+        (x_ref, own_ref, fill_ref, sum_ref, loss_ref, stack_ref, floor_ref), refs = refs[:7], refs[7:]
     elif part == 1:
         (sum_in_ref, loss_in_ref, stack_ref, floor_ref, sum_ref, loss_ref), refs = refs[:6], refs[6:]
     else:
@@ -321,10 +375,12 @@
                     pick = pl.ds(b * SUB * PATCH + j, SUB, stride=PATCH)
                     strip = strip_ref[b * SUB : b * SUB + SUB, :]
                     strip = pltpu.roll(strip, LANES - j * HALF, 1) if j else strip
+                    strip = jnp.where(last_col, -1.0, strip)
                     tile_ref[pick, :] = jnp.where(lane < HALF, strip.astype(jnp.int32), tile_ref[pick, :])
             for j in range(HALF):
                 strip = corner_ref[chans : chans + 1, :]
                 strip = pltpu.roll(strip, LANES - j * HALF, 1) if j else strip
+                strip = jnp.where(last_col, -1.0, strip)
                 row = tile_ref[tall + j : tall + j + 1, :]
                 tile_ref[tall + j : tall + j + 1, :] = jnp.where(lane[0:1] < HALF, strip.astype(jnp.int32), row)
 
@@ -340,6 +396,15 @@
     loss_ref[...] += pixels(groups, chans, slots, fold, tile_ref, fast, prepare, w_ref.at[now], p_ref, s_ref, lhs_ref)
     table = jnp.where(last_col, back_end_ref[...], back_ref[...])
     sum_ref[...] += jnp.dot(lhs_ref[...], table, preferred_element_type=f32)
+
+    if part == 0:
+
+        @pl.when((step == steps - 1) & (lax.axis_index("gx") == 0))
+        def _():
+            depth = stack_ref.shape[1]
+            w_ref[1 - now] = jnp.dot(stack_ref[...], fill_ref[0:depth, :], preferred_element_type=f32)
+            loss_ref[...] += first_columns(rows, groups, chans, slots, last_row, own_ref, got_ref, w_ref.at[1 - now], p_ref, lhs_ref)
+            sum_ref[...] += jnp.dot(lhs_ref[...], fill_ref[depth:, :], preferred_element_type=f32)
 
     if part == 2:
 
@@ -441,6 +506,12 @@
         jnp.asarray(t, bf16) for t in (forward(inside), forward(ending), backward(inside), backward(ending))
     )
 
+    fill = np.zeros((2 * depth, LANES), np.float32)
+    fill[[0, cols, 2 * cols]] = STEP
+    for part in (depth, depth + LANES):
+        fill[part : part + PATCH * HALF, 0] = STEP
+    fill = jnp.asarray(fill, bf16)
+
     shape = lambda *dims: jax.ShapeDtypeStruct(dims, f32)
     held = lambda *dims, kind=f32: pltpu.VMEM(dims, kind)
     far = lambda v: pltpu.with_memory_space_constraint(v, pltpu.HBM)
@@ -449,7 +520,7 @@
     swap = lambda v: lax.ppermute(v, "gy", [(0, 1), (1, 0)])
     tall_x = chans * slots
 
-    side, head, weight, shift = pl.pallas_call(
+    own, head, weight, shift = pl.pallas_call(
         functools.partial(pack_kernel, rows),
         in_specs=[ANY] * 5,
         out_specs=[VMEM] * 4,
@@ -467,15 +538,15 @@
         compiler_params=ROOM,
         name="pack",
     )(*(far(v) for v in (features, labels, valid_mask, probe_weight.T, probe_bias.reshape(1, chans))))
-    side = ring(side, "gx")
+    side = lax.ppermute(own, "gx", [(i, i - 1) for i in range(1, gx)])
     x, edge = pl.pallas_call(
         functools.partial(logits_kernel, rows, cols, chans, slots, 4),
-        in_specs=[VMEM] * 4,
+        in_specs=[VMEM] * 5,
         out_specs=[VMEM] * 2,
-        out_shape=[held(tall_x, LANES), held(chans + tiles * SUB, LANES)],
+        out_shape=[held(tall_x, LANES), held(chans + tiles * SUB + SUB, LANES)],
         compiler_params=ROOM,
         name="logits",
-    )(*(here(v) for v in (features, weight, shift, head)))
+    )(*(here(v) for v in (features, weight, shift, head, own)))
     got = ring(edge, "gy")
 
     sums = (2 * chans * rows, LANES)
@@ -488,7 +559,7 @@
         ahead = pl.BlockSpec((depth, LANES), lambda t: (0, at(t + 1)))
         rear = pl.BlockSpec((depth, LANES), lambda t: (at(t), 0))
         outs = [
-            ([held(*sums), held(SUB, LANES), stacked, shape(1)], [VMEM] * 3 + [SMEM], [VMEM]),
+            ([held(*sums), held(SUB, LANES), stacked, shape(1)], [VMEM] * 3 + [SMEM], [VMEM] * 3),
             ([held(*sums), held(SUB, LANES)], [VMEM] * 2, [VMEM] * 3 + [SMEM]),
             ([held(tall_x, LANES), held(chans, LANES), held(SUB, LANES)], [VMEM] * 3, [VMEM] * 6),
         ][part]
@@ -511,7 +582,7 @@
         )(here(got), lift, lift_end, lift, lift_end, back, back_end, labels, valid_mask, *args)
 
     middle = tiles // 2 + 1
-    total, loss, stack, floor = inner(0, 1, middle - 1, here(x))
+    total, loss, stack, floor = inner(0, 1, middle - 1, here(x), here(own), fill)
     side, total = lax.optimization_barrier((side, total))
     beside, beyond = pl.pallas_call(
         functools.partial(beside_kernel, rows, chans),

time: 186 us -> 184 us (0.989)
  waiting for transfers between devices: 17.4 us -> 10.2 us
  starting transfers between devices: 7.49 us -> 11.8 us
    ppermute x3, starting transfers between devices: 0.21 us -> 8.89 us  [body(): lax.ppermute(total, 'gx', [(i, i ^ step) for i in range(gx)])]
    ppermute x3, waiting for transfers between devices: 15 us -> 7.79 us  [body(): lax.ppermute(total, 'gx', [(i, i ^ step) for i in range(gx)])]
    ppermute x3 -> x2, starting transfers between devices: 6.39 us -> 0.64 us  [body(): lax.ppermute(v, axis, [(i, (i - 1) % lax.axis_size(axis)) for i in range(...]
  transfers between devices with their start and end apart: 9 -> 9, of which waited for: 6 -> 6; matrix products, arithmetic and copies ran while one was open for 0% -> 0% of each run, Pallas kernels for 59% -> 61%
where the time goes in v6:
time: 184 us
  Pallas kernels  160 us (87%)
  starting transfers between devices  11.8 us (6%)
  waiting for transfers between devices  10.2 us (6%)
    pallas_call x3, Pallas kernels, inner(): pl.pallas_call(functools.partial(inner_kernel, rows, cols, chans, slots,...  156 us
    ppermute x3, starting transfers between devices, body(): lax.ppermute(total, 'gx', [(i, i ^ step) for i in range(gx)])  8.89 us
    ppermute x3, waiting for transfers between devices, body(): lax.ppermute(total, 'gx', [(i, i ^ step) for i in range(gx)])  7.79 us
  transfers between devices with their start and end apart: 9, of which 6 were waited for; matrix products, arithmetic and copies ran while one was open for 0% of the time, Pallas kernels for 61%

profile of v6, /device:TPU:0, one launch (start us, length us, event | category | flops | bytes accessed | tf_op | source)
XLA Modules:
  0.0 184.3 jit_solution(13991257211920748711)
XLA Ops:
  0.6 0.0 copy-start.1
  0.7 0.0 copy-start.2
  0.7 0.0 copy-start.5
  0.7 0.0 copy-start.6
  0.7 0.0 copy-start.7
  0.7 1.5 pack.1
  2.2 0.4 copy-done
  2.6 1.0 logits.1
  3.6 0.6 collective-permute-start.1
  4.2 1.3 collective-permute-start
  5.5 0.0 collective-permute-done.1.refs_0_
  5.5 67.3 %inner_head.1 = (f32[1024,128]{1,0:T(8,128)S(1)}, f32[8,128]{1,0:T(8,128)S(1)}, bf16[768,256]{1,0:T(8,128)(2,1)S(1)}, f32[1]{0:T(128)}) custom-call(f32[96,128]{1,0:T(8,128)S(1)} %collective-permute-done.1.refs_0_, bf16[256,896]{1,0:T(8,128)(2,1)S(1)} %copy-done.2, bf16[256,896]{1,0:T(8,128)(2,1)S(1)} %copy-done.1, bf16[256,896]{1,0:T(8,128)(2,1)S(1)} %copy-done.2, ...), custom_call_target="tpu_custom_call" | custom-call | flops 1000000000 | bytes 2000000 | tf_op jit(solution)/shard_map/inner_head/pallas_call | solution.py:566
  72.9 0.0 collective-permute-done.side_ref.refs_12_
  72.9 0.2 beside.1
  73.1 0.1 collective-permute-start.2
  73.1 44.5 %inner_middle.1 = (f32[1024,128]{1,0:T(8,128)S(1)}, f32[8,128]{1,0:T(8,128)S(1)}) custom-call(f32[96,128]{1,0:T(8,128)S(1)} %collective-permute-done.1.refs_0_, bf16[256,896]{1,0:T(8,128)(2,1)S(1)} %copy-done.2, bf16[256,896]{1,0:T(8,128)(2,1)S(1)} %copy-done.1, bf16[256,896]{1,0:T(8,128)(2,1)S(1)} %copy-done.2, bf16[256,896]{1,0:T(8,128)(2,1)S(1)} %copy-done.1, ...), custom_call_target="tpu_custom_call" | custom-call | flops 1000000000 | bytes 2000000 | tf_op jit(solution)/shard_map/inner_middle/pallas_call | solution.py:566
  117.7 0.0 collective-permute-done.2.refs_11_
  117.7 44.3 %inner_tail.1 = (f32[768,128]{1,0:T(8,128)S(1)}, f32[32,128]{1,0:T(8,128)S(1)}, f32[8,128]{1,0:T(8,128)S(1)}) custom-call(f32[96,128]{1,0:T(8,128)S(1)} %collective-permute-done.1.refs_0_, bf16[256,896]{1,0:T(8,128)(2,1)S(1)} %copy-done.2, bf16[256,896]{1,0:T(8,128)(2,1)S(1)} %copy-done.1, bf16[256,896]{1,0:T(8,128)(2,1)S(1)} %copy-done.2, ...), custom_call_target="tpu_custom_call" | custom-call | flops 1000000000 | bytes 2000000 | tf_op jit(solution)/shard_map/inner_tail/pallas_call | solution.py:566
  162.0 0.5 collective-permute-start.3
  163.2 0.2 collective-permute-done.3.got_ref
  163.4 0.7 grad.1
  164.1 0.4 collective-permute-start.4
  164.5 0.9 collective-permute-done.4
  165.5 2.7 %collective-permute-start.5 = (f32[168,128]{1,0:T(8,128)S(1)}, f32[168,128]{1,0:T(8,128)S(1)}, u32[]{:S(2)}, u32[]{:S(2)}) collective-permute-start(f32[168,128]{1,0:T(8,128)S(1)} %add.12), channel_id=1, source_target_pairs={{0,2},{2,0},{4,6},{6,4},{8,10},{10,8},{12,14},{14,12},{1,3},{3,1},... | collective-permute-start | bytes 258056 | tf_op jit(solution)/shard_map/ppermute | solution.py:613
  168.2 2.9 %collective-permute-done.5 = f32[168,128]{1,0:T(8,128)S(1)} collective-permute-done((f32[168,128]{1,0:T(8,128)S(1)}, f32[168,128]{1,0:T(8,128)S(1)}, u32[]{:S(2)}, u32[]{:S(2)}) %collective-permute-start.5) | collective-permute-done | bytes 86048 | tf_op jit(solution)/shard_map/ppermute | solution.py:613
  171.0 3.1 %collective-permute-start.6 = (f32[168,128]{1,0:T(8,128)S(1)}, f32[168,128]{1,0:T(8,128)S(1)}, u32[]{:S(2)}, u32[]{:S(2)}) collective-permute-start(f32[168,128]{1,0:T(8,128)S(1)} %add.13), channel_id=1, source_target_pairs={{0,4},{2,6},{4,0},{6,2},{8,12},{10,14},{12,8},{14,10},{1,5},{3,7},... | collective-permute-start | bytes 258056 | tf_op jit(solution)/shard_map/ppermute | solution.py:613
  174.1 2.5 %collective-permute-done.6 = f32[168,128]{1,0:T(8,128)S(1)} collective-permute-done((f32[168,128]{1,0:T(8,128)S(1)}, f32[168,128]{1,0:T(8,128)S(1)}, u32[]{:S(2)}, u32[]{:S(2)}) %collective-permute-start.6) | collective-permute-done | bytes 86048 | tf_op jit(solution)/shard_map/ppermute | solution.py:613
  176.6 3.1 %collective-permute-start.7 = (f32[168,128]{1,0:T(8,128)S(1)}, f32[168,128]{1,0:T(8,128)S(1)}, u32[]{:S(2)}, u32[]{:S(2)}) collective-permute-start(f32[168,128]{1,0:T(8,128)S(1)} %add.14), channel_id=1, source_target_pairs={{0,8},{2,10},{4,12},{6,14},{8,0},{10,2},{12,4},{14,6},{1,9},{3,11}... | collective-permute-start | bytes 258056 | tf_op jit(solution)/shard_map/ppermute | solution.py:613
  179.7 2.5 %collective-permute-done.7 = f32[168,128]{1,0:T(8,128)S(1)} collective-permute-done((f32[168,128]{1,0:T(8,128)S(1)}, f32[168,128]{1,0:T(8,128)S(1)}, u32[]{:S(2)}, u32[]{:S(2)}) %collective-permute-start.7) | collective-permute-done | bytes 86048 | tf_op jit(solution)/shard_map/ppermute | solution.py:613
  182.2 0.1 collective-permute-start.8
  182.3 1.3 collective-permute-done.8.z_ref
  183.6 0.7 final.1
  (14 shorter events, 0.1 us)
Async XLA Ops:
  0.6 2.0 %copy-start = (bf16[16,64,1280]{2,1,0:T(8,128)(2,1)S(1)}, bf16[16,64,1280]{2,1,0:T(8,128)(2,1)}, u32[]{:S(2)}) copy-start(bf16[16,64,1280]{2,1,0:T(8,128)(2,1)} %f_ref.5) | copy-start | bytes 7864324
  0.6 4.8 %copy-start.1 = (bf16[256,896]{1,0:T(8,128)(2,1)S(1)}, bf16[256,896]{1,0:T(8,128)(2,1)}, u32[]{:S(2)}) copy-start(bf16[256,896]{1,0:T(8,128)(2,1)} %constant.11.clone.refs_2_.refs_4_) | copy-start | bytes 1376260
  0.7 4.8 %copy-start.2 = (bf16[256,896]{1,0:T(8,128)(2,1)S(1)}, bf16[256,896]{1,0:T(8,128)(2,1)}, u32[]{:S(2)}) copy-start(bf16[256,896]{1,0:T(8,128)(2,1)} %constant.10.clone.refs_1_.refs_3_) | copy-start | bytes 1376260
  0.7 4.8 %copy-start.3 = (s32[224,896]{1,0:T(8,128)S(1)}, s32[224,896]{1,0:T(8,128)}, u32[]{:S(2)}) copy-start(s32[224,896]{1,0:T(8,128)} %refs_7_.5) | copy-start | bytes 2408452
  0.7 4.8 %copy-start.4 = (s32[224,896]{1,0:T(8,128)S(1)}, s32[224,896]{1,0:T(8,128)}, u32[]{:S(2)}) copy-start(s32[224,896]{1,0:T(8,128)} %refs_8_.5) | copy-start | bytes 2408452
  0.7 4.8 %copy-start.5 = (bf16[1792,128]{1,0:T(8,128)(2,1)S(1)}, bf16[1792,128]{1,0:T(8,128)(2,1)}, u32[]{:S(2)}) copy-start(bf16[1792,128]{1,0:T(8,128)(2,1)} %constant.13.clone.refs_6_) | copy-start | bytes 1376260
  0.7 4.8 %copy-start.6 = (bf16[1792,128]{1,0:T(8,128)(2,1)S(1)}, bf16[1792,128]{1,0:T(8,128)(2,1)}, u32[]{:S(2)}) copy-start(bf16[1792,128]{1,0:T(8,128)(2,1)} %constant.12.clone.refs_5_) | copy-start | bytes 1376260
  0.7 4.8 %copy-start.7 = (bf16[512,128]{1,0:T(8,128)(2,1)S(1)}, bf16[512,128]{1,0:T(8,128)(2,1)}, u32[]{:S(2)}) copy-start(bf16[512,128]{1,0:T(8,128)(2,1)} %constant.14.clone.refs_11_) | copy-start | bytes 393220
  3.6 1.8 %collective-permute-start.1 = (f32[96,128]{1,0:T(8,128)S(1)}, f32[96,128]{1,0:T(8,128)S(1)}, u32[]{:S(2)}, u32[]{:S(2)}) collective-permute-start(f32[96,128]{1,0:T(8,128)S(1)} %get-tuple-element.31), channel_id=1, source_target_pairs={{0,1},{1,0},{2,3},{3,2},{4,5},{5,4},{6,7},{7,6},{8,9},{9,8},{10,11... | collective-permute-start | bytes 147464 | tf_op jit(solution)/shard_map/ppermute | solution.py:519
  4.2 68.7 %collective-permute-start = (f32[176,128]{1,0:T(8,128)S(1)}, f32[176,128]{1,0:T(8,128)S(1)}, u32[]{:S(2)}, u32[]{:S(2)}) collective-permute-start(f32[176,128]{1,0:T(8,128)S(1)} %get-tuple-element.27.side_ref.refs_10_), channel_id=1, source_target_pairs={{2,0},{4,2},{6,4},{8,6},{10,8},{12,10},{14,12},{3,1},{5,3},{7,5},{... | collective-permute-start | bytes 270344 | tf_op jit(solution)/shard_map/ppermute | solution.py:541
  73.1 44.6 %collective-permute-start.2 = (f32[40,128]{1,0:T(8,128)S(1)}, f32[40,128]{1,0:T(8,128)S(1)}, u32[]{:S(2)}, u32[]{:S(2)}) collective-permute-start(f32[40,128]{1,0:T(8,128)S(1)} %get-tuple-element.36.refs_10_), channel_id=1, source_target_pairs={{0,1},{1,0},{2,3},{3,2},{4,5},{5,4},{6,7},{7,6},{8,9},{9,8},{10,11... | collective-permute-start | bytes 61448 | tf_op jit(solution)/shard_map/ppermute | solution.py:519
  162.0 1.4 collective-permute-start.3
  164.1 1.3 collective-permute-start.4
  165.5 5.5 %collective-permute-start.5 = (f32[168,128]{1,0:T(8,128)S(1)}, f32[168,128]{1,0:T(8,128)S(1)}, u32[]{:S(2)}, u32[]{:S(2)}) collective-permute-start(f32[168,128]{1,0:T(8,128)S(1)} %add.12), channel_id=1, source_target_pairs={{0,2},{2,0},{4,6},{6,4},{8,10},{10,8},{12,14},{14,12},{1,3},{3,1},... | collective-permute-start | bytes 258056 | tf_op jit(solution)/shard_map/ppermute | solution.py:613
  171.0 5.6 %collective-permute-start.6 = (f32[168,128]{1,0:T(8,128)S(1)}, f32[168,128]{1,0:T(8,128)S(1)}, u32[]{:S(2)}, u32[]{:S(2)}) collective-permute-start(f32[168,128]{1,0:T(8,128)S(1)} %add.13), channel_id=1, source_target_pairs={{0,4},{2,6},{4,0},{6,2},{8,12},{10,14},{12,8},{14,10},{1,5},{3,7},... | collective-permute-start | bytes 258056 | tf_op jit(solution)/shard_map/ppermute | solution.py:613
  176.6 5.6 %collective-permute-start.7 = (f32[168,128]{1,0:T(8,128)S(1)}, f32[168,128]{1,0:T(8,128)S(1)}, u32[]{:S(2)}, u32[]{:S(2)}) collective-permute-start(f32[168,128]{1,0:T(8,128)S(1)} %add.14), channel_id=1, source_target_pairs={{0,8},{2,10},{4,12},{6,14},{8,0},{10,2},{12,4},{14,6},{1,9},{3,11}... | collective-permute-start | bytes 258056 | tf_op jit(solution)/shard_map/ppermute | solution.py:613
  182.2 1.3 collective-permute-start.8

commit v7 on v6

--- a/solution.py
+++ b/solution.py
@@ -317,9 +317,7 @@
 
 
 def inner_kernel(rows, cols, chans, slots, groups, part, begin, tiles, *refs):
-    (got_ref, lift_ref, lift_end_ref, next_ref, next_end_ref, back_ref, back_end_ref, lab_ref, mask_ref), refs = (
-        refs[:9], refs[9:],
-    )
+    (got_ref, lift_ref, lift_end_ref, back_ref, back_end_ref, lab_ref, mask_ref), refs = refs[:7], refs[7:]
     if part == 0:
         (x_ref, own_ref, fill_ref, sum_ref, loss_ref, stack_ref, floor_ref), refs = refs[:7], refs[7:]
     elif part == 1:
@@ -338,6 +336,12 @@
     last_row = lax.axis_index("gy") == lax.axis_size("gy") - 1
     tall = rows * PATCH
     lane = lax.broadcasted_iota(jnp.int32, (SUB, LANES), 1)
+    lanes = pl.ds(pl.multiple_of(which * LANES, LANES), LANES)
+
+    def lift(at):
+        lanes = pl.ds(pl.multiple_of(at * LANES, LANES), LANES)
+        table = jnp.where(last_col, lift_end_ref[:, lanes], lift_ref[:, lanes])
+        return jnp.dot(stack_ref[...], table, preferred_element_type=f32)
 
     @pl.when(step == 0)
     def _():
@@ -360,10 +364,9 @@
             full = w_ref[0]
             floor_ref[0] = jnp.min(full) * STEP
             stack_ref[...] = stack3(full)
-        table = jnp.where(last_col, lift_end_ref[...], lift_ref[...])
-        w_ref[0] = jnp.dot(stack_ref[...], table, preferred_element_type=f32)
-
-    tile_ref[0:tall, :] = jnp.where(mask_ref[...] != 0, lab_ref[...], -1)
+        w_ref[0] = lift(which)
+
+    tile_ref[0:tall, :] = jnp.where(mask_ref[:, lanes] != 0, lab_ref[:, lanes], -1)
     tile_ref[tall : tall + SUB, :] = got_ref[pl.ds(pl.multiple_of(chans + which * SUB, SUB), SUB), :].astype(jnp.int32)
 
     if part == 2:
@@ -390,11 +393,12 @@
     fast = floor_ref[0] >= FLOOR
 
     def prepare():
-        table = jnp.where(last_col, next_end_ref[...], next_ref[...])
-        w_ref[1 - now] = jnp.dot(stack_ref[...], table, preferred_element_type=f32)
+        w_ref[1 - now] = lift(lax.rem(which + 1, tiles))
 
     loss_ref[...] += pixels(groups, chans, slots, fold, tile_ref, fast, prepare, w_ref.at[now], p_ref, s_ref, lhs_ref)
-    table = jnp.where(last_col, back_end_ref[...], back_ref[...])
+    depth = 2 * LANES
+    deep = pl.ds(pl.multiple_of(which * depth, depth), depth)
+    table = jnp.where(last_col, back_end_ref[deep, :], back_ref[deep, :])
     sum_ref[...] += jnp.dot(lhs_ref[...], table, preferred_element_type=f32)
 
     if part == 0:
@@ -553,11 +557,6 @@
     stacked = held(tall_x, depth, kind=bf16)
 
     def inner(part, begin, steps, *args):
-        at = lambda t: (t + begin) % tiles
-        column = pl.BlockSpec((tall, LANES), lambda t: (0, at(t)))
-        block = pl.BlockSpec((depth, LANES), lambda t: (0, at(t)))
-        ahead = pl.BlockSpec((depth, LANES), lambda t: (0, at(t + 1)))
-        rear = pl.BlockSpec((depth, LANES), lambda t: (at(t), 0))
         outs = [
             ([held(*sums), held(SUB, LANES), stacked, shape(1)], [VMEM] * 3 + [SMEM], [VMEM] * 3),
             ([held(*sums), held(SUB, LANES)], [VMEM] * 2, [VMEM] * 3 + [SMEM]),
@@ -566,7 +565,7 @@
         return pl.pallas_call(
             functools.partial(inner_kernel, rows, cols, chans, slots, groups, part, begin, tiles),
             grid=(steps,),
-            in_specs=[VMEM, block, block, ahead, ahead, rear, rear, column, column] + outs[2],
+            in_specs=[VMEM] * 7 + outs[2],
             out_specs=outs[1],
             out_shape=outs[0],
             scratch_shapes=[
@@ -579,10 +578,10 @@
             cost_estimate=pl.CostEstimate(flops=10**9, bytes_accessed=2 * 10**6, transcendentals=10**6),
             compiler_params=ROOM,
             name=("inner_head", "inner_middle", "inner_tail")[part],
-        )(here(got), lift, lift_end, lift, lift_end, back, back_end, labels, valid_mask, *args)
+        )(*(here(v) for v in (got, lift, lift_end, back, back_end, labels, valid_mask)), *args)
 
     middle = tiles // 2 + 1
-    total, loss, stack, floor = inner(0, 1, middle - 1, here(x), here(own), fill)
+    total, loss, stack, floor = inner(0, 1, middle - 1, here(x), here(own), here(fill))
     side, total = lax.optimization_barrier((side, total))
     beside, beyond = pl.pallas_call(
         functools.partial(beside_kernel, rows, chans),

time: 184 us -> 182 us (0.989)
  Pallas kernels: 160 us -> 158 us
    pallas_call x3, Pallas kernels: 156 us -> 154 us  [inner(): pl.pallas_call(functools.partial(inner_kernel, rows, cols, chans, slots,...]
where the time goes in v7:
time: 182 us
  Pallas kernels  158 us (87%)
  starting transfers between devices  11.9 us (7%)
  waiting for transfers between devices  10.2 us (6%)
    pallas_call x3, Pallas kernels, inner(): pl.pallas_call(functools.partial(inner_kernel, rows, cols, chans, slots,...  154 us
    ppermute x3, starting transfers between devices, body(): lax.ppermute(total, 'gx', [(i, i ^ step) for i in range(gx)])  8.9 us
    ppermute x3, waiting for transfers between devices, body(): lax.ppermute(total, 'gx', [(i, i ^ step) for i in range(gx)])  7.79 us
  transfers between devices with their start and end apart: 9, of which 6 were waited for; matrix products, arithmetic and copies ran while one was open for 0% of the time, Pallas kernels for 61%

profile of v7, /device:TPU:0, one launch (start us, length us, event | category | flops | bytes accessed | tf_op | source)
XLA Modules:
  0.0 181.7 jit_solution(18377372133136538300)
XLA Ops:
  0.7 0.0 copy-start.3
  0.7 0.0 copy-start.4
  0.7 0.0 copy-start.5
  0.7 0.0 copy-start.6
  0.7 0.0 copy-start.7
  0.7 1.5 pack.1
  2.2 0.4 copy-done
  2.6 1.0 logits.1
  3.6 0.6 collective-permute-start.1
  4.2 1.3 collective-permute-start
  5.5 0.0 collective-permute-done.1.refs_0_
  5.5 66.2 %inner_head.1 = (f32[1024,128]{1,0:T(8,128)S(1)}, f32[8,128]{1,0:T(8,128)S(1)}, bf16[768,256]{1,0:T(8,128)(2,1)S(1)}, f32[1]{0:T(128)}) custom-call(f32[96,128]{1,0:T(8,128)S(1)} %collective-permute-done.1.refs_0_, bf16[256,896]{1,0:T(8,128)(2,1)S(1)} %copy-done.6, bf16[256,896]{1,0:T(8,128)(2,1)S(1)} %copy-done.5, bf16[1792,128]{1,0:T(8,128)(2,1)S(1)} %copy-done.4, ...), custom_call_target="tpu_custom_call" | custom-call | flops 1000000000 | bytes 2000000 | tf_op jit(solution)/shard_map/inner_head/pallas_call | solution.py:565
  71.8 0.0 collective-permute-done.side_ref.refs_10_
  71.8 0.2 beside.1
  71.9 0.1 collective-permute-start.2
  72.1 43.8 %inner_middle.1 = (f32[1024,128]{1,0:T(8,128)S(1)}, f32[8,128]{1,0:T(8,128)S(1)}) custom-call(f32[96,128]{1,0:T(8,128)S(1)} %collective-permute-done.1.refs_0_, bf16[256,896]{1,0:T(8,128)(2,1)S(1)} %copy-done.6, bf16[256,896]{1,0:T(8,128)(2,1)S(1)} %copy-done.5, bf16[1792,128]{1,0:T(8,128)(2,1)S(1)} %copy-done.4, bf16[1792,128]{1,0:T(8,128)(2,1)S(1)} %copy-done.3, ...), custom_call_target="tpu_custom_call" | custom-call | flops 1000000000 | bytes 2000000 | tf_op jit(solution)/shard_map/inner_middle/pallas_call | solution.py:565
  115.8 0.0 collective-permute-done.2.refs_9_
  115.8 43.6 %inner_tail.1 = (f32[768,128]{1,0:T(8,128)S(1)}, f32[32,128]{1,0:T(8,128)S(1)}, f32[8,128]{1,0:T(8,128)S(1)}) custom-call(f32[96,128]{1,0:T(8,128)S(1)} %collective-permute-done.1.refs_0_, bf16[256,896]{1,0:T(8,128)(2,1)S(1)} %copy-done.6, bf16[256,896]{1,0:T(8,128)(2,1)S(1)} %copy-done.5, bf16[1792,128]{1,0:T(8,128)(2,1)S(1)} %copy-done.4, ...), custom_call_target="tpu_custom_call" | custom-call | flops 1000000000 | bytes 2000000 | tf_op jit(solution)/shard_map/inner_tail/pallas_call | solution.py:565
  159.4 0.5 collective-permute-start.3
  160.6 0.2 collective-permute-done.3.got_ref
  160.8 0.7 grad.1
  161.5 0.4 collective-permute-start.4
  161.9 0.9 collective-permute-done.4
  162.9 2.7 %collective-permute-start.5 = (f32[168,128]{1,0:T(8,128)S(1)}, f32[168,128]{1,0:T(8,128)S(1)}, u32[]{:S(2)}, u32[]{:S(2)}) collective-permute-start(f32[168,128]{1,0:T(8,128)S(1)} %add.12), channel_id=1, source_target_pairs={{0,2},{2,0},{4,6},{6,4},{8,10},{10,8},{12,14},{14,12},{1,3},{3,1},... | collective-permute-start | bytes 258056 | tf_op jit(solution)/shard_map/ppermute | solution.py:612
  165.5 2.9 %collective-permute-done.5 = f32[168,128]{1,0:T(8,128)S(1)} collective-permute-done((f32[168,128]{1,0:T(8,128)S(1)}, f32[168,128]{1,0:T(8,128)S(1)}, u32[]{:S(2)}, u32[]{:S(2)}) %collective-permute-start.5) | collective-permute-done | bytes 86048 | tf_op jit(solution)/shard_map/ppermute | solution.py:612
  168.4 3.1 %collective-permute-start.6 = (f32[168,128]{1,0:T(8,128)S(1)}, f32[168,128]{1,0:T(8,128)S(1)}, u32[]{:S(2)}, u32[]{:S(2)}) collective-permute-start(f32[168,128]{1,0:T(8,128)S(1)} %add.13), channel_id=1, source_target_pairs={{0,4},{2,6},{4,0},{6,2},{8,12},{10,14},{12,8},{14,10},{1,5},{3,7},... | collective-permute-start | bytes 258056 | tf_op jit(solution)/shard_map/ppermute | solution.py:612
  171.5 2.5 %collective-permute-done.6 = f32[168,128]{1,0:T(8,128)S(1)} collective-permute-done((f32[168,128]{1,0:T(8,128)S(1)}, f32[168,128]{1,0:T(8,128)S(1)}, u32[]{:S(2)}, u32[]{:S(2)}) %collective-permute-start.6) | collective-permute-done | bytes 86048 | tf_op jit(solution)/shard_map/ppermute | solution.py:612
  174.0 3.1 %collective-permute-start.7 = (f32[168,128]{1,0:T(8,128)S(1)}, f32[168,128]{1,0:T(8,128)S(1)}, u32[]{:S(2)}, u32[]{:S(2)}) collective-permute-start(f32[168,128]{1,0:T(8,128)S(1)} %add.14), channel_id=1, source_target_pairs={{0,8},{2,10},{4,12},{6,14},{8,0},{10,2},{12,4},{14,6},{1,9},{3,11}... | collective-permute-start | bytes 258056 | tf_op jit(solution)/shard_map/ppermute | solution.py:612
  177.1 2.5 %collective-permute-done.7 = f32[168,128]{1,0:T(8,128)S(1)} collective-permute-done((f32[168,128]{1,0:T(8,128)S(1)}, f32[168,128]{1,0:T(8,128)S(1)}, u32[]{:S(2)}, u32[]{:S(2)}) %collective-permute-start.7) | collective-permute-done | bytes 86048 | tf_op jit(solution)/shard_map/ppermute | solution.py:612
  179.6 0.1 collective-permute-start.8
  179.7 1.3 collective-permute-done.8.z_ref
  181.0 0.7 final.1
  (14 shorter events, 0.1 us)
Async XLA Ops:
  0.6 2.0 %copy-start = (bf16[16,64,1280]{2,1,0:T(8,128)(2,1)S(1)}, bf16[16,64,1280]{2,1,0:T(8,128)(2,1)}, u32[]{:S(2)}) copy-start(bf16[16,64,1280]{2,1,0:T(8,128)(2,1)} %f_ref.5) | copy-start | bytes 7864324
  0.6 4.8 %copy-start.1 = (s32[224,896]{1,0:T(8,128)S(1)}, s32[224,896]{1,0:T(8,128)}, u32[]{:S(2)}) copy-start(s32[224,896]{1,0:T(8,128)} %refs_5_.5) | copy-start | bytes 2408452
  0.7 4.8 %copy-start.2 = (s32[224,896]{1,0:T(8,128)S(1)}, s32[224,896]{1,0:T(8,128)}, u32[]{:S(2)}) copy-start(s32[224,896]{1,0:T(8,128)} %refs_6_.5) | copy-start | bytes 2408452
  0.7 4.8 %copy-start.3 = (bf16[1792,128]{1,0:T(8,128)(2,1)S(1)}, bf16[1792,128]{1,0:T(8,128)(2,1)}, u32[]{:S(2)}) copy-start(bf16[1792,128]{1,0:T(8,128)(2,1)} %constant.13.clone.refs_4_) | copy-start | bytes 1376260
  0.7 4.8 %copy-start.4 = (bf16[1792,128]{1,0:T(8,128)(2,1)S(1)}, bf16[1792,128]{1,0:T(8,128)(2,1)}, u32[]{:S(2)}) copy-start(bf16[1792,128]{1,0:T(8,128)(2,1)} %constant.12.clone.refs_3_) | copy-start | bytes 1376260
  0.7 4.8 %copy-start.5 = (bf16[256,896]{1,0:T(8,128)(2,1)S(1)}, bf16[256,896]{1,0:T(8,128)(2,1)}, u32[]{:S(2)}) copy-start(bf16[256,896]{1,0:T(8,128)(2,1)} %constant.11.clone.refs_2_) | copy-start | bytes 1376260
  0.7 4.8 %copy-start.6 = (bf16[256,896]{1,0:T(8,128)(2,1)S(1)}, bf16[256,896]{1,0:T(8,128)(2,1)}, u32[]{:S(2)}) copy-start(bf16[256,896]{1,0:T(8,128)(2,1)} %constant.10.clone.refs_1_) | copy-start | bytes 1376260
  0.7 4.8 %copy-start.7 = (bf16[512,128]{1,0:T(8,128)(2,1)S(1)}, bf16[512,128]{1,0:T(8,128)(2,1)}, u32[]{:S(2)}) copy-start(bf16[512,128]{1,0:T(8,128)(2,1)} %constant.14.clone.refs_9_) | copy-start | bytes 393220
  3.6 1.8 %collective-permute-start.1 = (f32[96,128]{1,0:T(8,128)S(1)}, f32[96,128]{1,0:T(8,128)S(1)}, u32[]{:S(2)}, u32[]{:S(2)}) collective-permute-start(f32[96,128]{1,0:T(8,128)S(1)} %get-tuple-element.31), channel_id=1, source_target_pairs={{0,1},{1,0},{2,3},{3,2},{4,5},{5,4},{6,7},{7,6},{8,9},{9,8},{10,11... | collective-permute-start | bytes 147464 | tf_op jit(solution)/shard_map/ppermute | solution.py:523
  4.2 67.6 %collective-permute-start = (f32[176,128]{1,0:T(8,128)S(1)}, f32[176,128]{1,0:T(8,128)S(1)}, u32[]{:S(2)}, u32[]{:S(2)}) collective-permute-start(f32[176,128]{1,0:T(8,128)S(1)} %get-tuple-element.27.side_ref.refs_8_), channel_id=1, source_target_pairs={{2,0},{4,2},{6,4},{8,6},{10,8},{12,10},{14,12},{3,1},{5,3},{7,5},{... | collective-permute-start | bytes 270344 | tf_op jit(solution)/shard_map/ppermute | solution.py:545
  71.9 43.9 %collective-permute-start.2 = (f32[40,128]{1,0:T(8,128)S(1)}, f32[40,128]{1,0:T(8,128)S(1)}, u32[]{:S(2)}, u32[]{:S(2)}) collective-permute-start(f32[40,128]{1,0:T(8,128)S(1)} %get-tuple-element.36.refs_8_), channel_id=1, source_target_pairs={{0,1},{1,0},{2,3},{3,2},{4,5},{5,4},{6,7},{7,6},{8,9},{9,8},{10,11... | collective-permute-start | bytes 61448 | tf_op jit(solution)/shard_map/ppermute | solution.py:523
  159.4 1.4 collective-permute-start.3
  161.5 1.3 collective-permute-start.4
  162.9 5.5 %collective-permute-start.5 = (f32[168,128]{1,0:T(8,128)S(1)}, f32[168,128]{1,0:T(8,128)S(1)}, u32[]{:S(2)}, u32[]{:S(2)}) collective-permute-start(f32[168,128]{1,0:T(8,128)S(1)} %add.12), channel_id=1, source_target_pairs={{0,2},{2,0},{4,6},{6,4},{8,10},{10,8},{12,14},{14,12},{1,3},{3,1},... | collective-permute-start | bytes 258056 | tf_op jit(solution)/shard_map/ppermute | solution.py:612
  168.4 5.6 %collective-permute-start.6 = (f32[168,128]{1,0:T(8,128)S(1)}, f32[168,128]{1,0:T(8,128)S(1)}, u32[]{:S(2)}, u32[]{:S(2)}) collective-permute-start(f32[168,128]{1,0:T(8,128)S(1)} %add.13), channel_id=1, source_target_pairs={{0,4},{2,6},{4,0},{6,2},{8,12},{10,14},{12,8},{14,10},{1,5},{3,7},... | collective-permute-start | bytes 258056 | tf_op jit(solution)/shard_map/ppermute | solution.py:612
  174.0 5.6 %collective-permute-start.7 = (f32[168,128]{1,0:T(8,128)S(1)}, f32[168,128]{1,0:T(8,128)S(1)}, u32[]{:S(2)}, u32[]{:S(2)}) collective-permute-start(f32[168,128]{1,0:T(8,128)S(1)} %add.14), channel_id=1, source_target_pairs={{0,8},{2,10},{4,12},{6,14},{8,0},{10,2},{12,4},{14,6},{1,9},{3,11}... | collective-permute-start | bytes 258056 | tf_op jit(solution)/shard_map/ppermute | solution.py:612
  179.6 1.3 collective-permute-start.8

commit v8 on v7

--- a/solution.py
+++ b/solution.py
@@ -135,9 +135,33 @@
     out_ref[chans:, :] = side_ref[0:SUB, :]
 
 
-def softmax_fast(groups, chans, slots, fold, w_ref, p_ref):
+def two_sums(item):
+    totals, runs = [], []
+    for half in range(2):
+        total = run = None
+        for m in reversed(range(HALF)):
+            v = item(half, m)
+            total = v if total is None else total + v
+            if m:
+                run = total if run is None else run + total
+        totals.append(total)
+        runs.append(run)
+    return totals[0], totals[1], runs[0] - runs[1], totals[0] - totals[1]
+
+
+def tally(packed, c, h_ref):
+    one, none, mid = (jnp.asarray(v, bf16) for v in (1, 0, 0.5))
+    mark = jnp.asarray(c, bf16) if isinstance(c, int) else c.astype(f32).astype(bf16)
+    up, down, run, lean = two_sums(lambda half, m: jnp.where(packed[half * HALF + m] == mark, one, none))
+    h_ref[3 * c] = up
+    h_ref[3 * c + 1] = down
+    h_ref[3 * c + 2] = run + lean * mid
+
+
+def softmax_fast(groups, chans, slots, fold, w_ref, p_ref, packed, h_ref):
     sums = [None] * (2 * groups * HALF)
     for c in range(chans):
+        tally(packed, c, h_ref)
         for b in range(groups):
             row = c * slots + SUB * b
             upper = w_ref[row : row + SUB, :]
@@ -183,7 +207,7 @@
     return sums, losses
 
 
-def pixels(groups, chans, slots, fold, lab_ref, fast, prepare, w_ref, p_ref, s_ref, lhs_ref):
+def pixels(groups, chans, slots, fold, lab_ref, fast, prepare, w_ref, p_ref, s_ref, lhs_ref, h_ref):
     count = 2 * groups * HALF
     labels = []
     for half in range(2):
@@ -192,10 +216,15 @@
                 k = PATCH - 1 - m if half else m
                 labels.append(lab_ref[pl.ds(b * SUB * PATCH + HALF + k, SUB, stride=PATCH), :])
     weights = [jnp.where(lab >= 0, 1.0, 0.0) for lab in labels]
+    packed = [
+        jnp.concatenate([labels[(half * groups + b) * HALF + m] for b in range(groups)], axis=0).astype(f32).astype(bf16)
+        for half in range(2)
+        for m in range(HALF)
+    ]
 
     @pl.when(fast)
     def _():
-        sums = softmax_fast(groups, chans, slots, fold, w_ref, p_ref)
+        sums = softmax_fast(groups, chans, slots, fold, w_ref, p_ref, packed, h_ref)
         for k in range(count):
             s_ref[k] = sums[k]
         s_ref[count] = jnp.zeros((SUB, LANES), f32)
@@ -207,6 +236,7 @@
         for k in range(count):
             s_ref[k] = sums[k]
         s_ref[count] = losses
+        lax.fori_loop(0, chans, lambda c, _: tally(packed, c, h_ref), None)
         prepare()
 
     loss = jnp.zeros((SUB, LANES), f32)
@@ -215,32 +245,10 @@
         total = s_ref[k]
         loss = loss + weights[k] * jnp.log(total)
         scale.append(weights[k] / total)
-    packed = [
-        jnp.concatenate([labels[(half * groups + b) * HALF + m] for b in range(groups)], axis=0).astype(f32).astype(bf16)
-        for half in range(2)
-        for m in range(HALF)
-    ]
-    one, none, mid = (jnp.asarray(v, bf16) for v in (1, 0, 0.5))
     picked = jnp.zeros((SUB, LANES), f32)
     tall = groups * SUB
-
-    def two_sums(item):
-        totals, runs = [], []
-        for half in range(2):
-            total = run = None
-            for m in reversed(range(HALF)):
-                v = item(half, m)
-                total = v if total is None else total + v
-                if m:
-                    run = total if run is None else run + total
-            totals.append(total)
-            runs.append(run)
-        return totals[0], totals[1], runs[0] - runs[1], totals[0] - totals[1]
-
     for c in range(chans):
-        mark = jnp.asarray(c, bf16)
-        up, down, run, lean = two_sums(lambda half, m: jnp.where(packed[half * HALF + m] == mark, one, none))
-        hits = [v.astype(f32) for v in (up, down, run + lean * mid)]
+        hits = [h_ref[3 * c + k].astype(f32) for k in range(3)]
         parts = [[], []]
         for b in range(groups):
             row = c * slots + SUB * b
@@ -319,15 +327,15 @@
 def inner_kernel(rows, cols, chans, slots, groups, part, begin, tiles, *refs):
     (got_ref, lift_ref, lift_end_ref, back_ref, back_end_ref, lab_ref, mask_ref), refs = refs[:7], refs[7:]
     if part == 0:
-        (x_ref, own_ref, fill_ref, sum_ref, loss_ref, stack_ref, floor_ref), refs = refs[:7], refs[7:]
+        (x_ref, own_ref, fill_ref, sum_ref, loss_ref, stack_ref, floor_out_ref), refs = refs[:7], refs[7:]
     elif part == 1:
-        (sum_in_ref, loss_in_ref, stack_ref, floor_ref, sum_ref, loss_ref), refs = refs[:6], refs[6:]
+        (sum_in_ref, loss_in_ref, stack_ref, floor_in_ref, sum_ref, loss_ref), refs = refs[:6], refs[6:]
     else:
         (x_ref, beyond_ref, corner_ref, strip_ref, sum_in_ref, loss_in_ref), refs = refs[:6], refs[6:]
         (out_ref, spill_ref, loss_ref), refs = refs[:3], refs[3:]
-    (w_ref, p_ref, s_ref, lhs_ref, tile_ref), refs = refs[:5], refs[5:]
+    (w_ref, p_ref, s_ref, lhs_ref, tile_ref, h_ref, floor_ref), refs = refs[:7], refs[7:]
     if part == 2:
-        sum_ref, stack_ref, floor_ref = refs
+        sum_ref, stack_ref = refs
     step = pl.program_id(0)
     steps = pl.num_programs(0)
     now = lax.rem(step, 2)
@@ -364,6 +372,10 @@
             full = w_ref[0]
             floor_ref[0] = jnp.min(full) * STEP
             stack_ref[...] = stack3(full)
+            if part == 0:
+                floor_out_ref[...] = jnp.full((SUB, LANES), floor_ref[0], f32)
+        else:
+            floor_ref[0] = jnp.min(floor_in_ref[...])
         w_ref[0] = lift(which)
 
     tile_ref[0:tall, :] = jnp.where(mask_ref[:, lanes] != 0, lab_ref[:, lanes], -1)
@@ -395,7 +407,7 @@
     def prepare():
         w_ref[1 - now] = lift(lax.rem(which + 1, tiles))
 
-    loss_ref[...] += pixels(groups, chans, slots, fold, tile_ref, fast, prepare, w_ref.at[now], p_ref, s_ref, lhs_ref)
+    loss_ref[...] += pixels(groups, chans, slots, fold, tile_ref, fast, prepare, w_ref.at[now], p_ref, s_ref, lhs_ref, h_ref)
     depth = 2 * LANES
     deep = pl.ds(pl.multiple_of(which * depth, depth), depth)
     table = jnp.where(last_col, back_end_ref[deep, :], back_ref[deep, :])
@@ -558,8 +570,8 @@
 
     def inner(part, begin, steps, *args):
         outs = [
-            ([held(*sums), held(SUB, LANES), stacked, shape(1)], [VMEM] * 3 + [SMEM], [VMEM] * 3),
-            ([held(*sums), held(SUB, LANES)], [VMEM] * 2, [VMEM] * 3 + [SMEM]),
+            ([held(*sums), held(SUB, LANES), stacked, held(SUB, LANES)], [VMEM] * 4, [VMEM] * 3),
+            ([held(*sums), held(SUB, LANES)], [VMEM] * 2, [VMEM] * 4),
             ([held(tall_x, LANES), held(chans, LANES), held(SUB, LANES)], [VMEM] * 3, [VMEM] * 6),
         ][part]
         return pl.pallas_call(
@@ -574,7 +586,9 @@
                 pltpu.VMEM((2 * count + 1, SUB, LANES), f32),
                 pltpu.VMEM((2 * chans * rows, depth), bf16),
                 pltpu.VMEM((tall + SUB, LANES), jnp.int32),
-            ] + ([pltpu.VMEM(sums, f32), stacked, pltpu.SMEM((1,), f32)] if part == 2 else []),
+                pltpu.VMEM((3 * chans, rows, LANES), bf16),
+                pltpu.SMEM((1,), f32),
+            ] + ([pltpu.VMEM(sums, f32), stacked] if part == 2 else []),
             cost_estimate=pl.CostEstimate(flops=10**9, bytes_accessed=2 * 10**6, transcendentals=10**6),
             compiler_params=ROOM,
             name=("inner_head", "inner_middle", "inner_tail")[part],
@@ -592,7 +606,7 @@
         name="beside",
     )(here(side), here(weight), here(shift))
     corner = ring(beyond, "gy")
-    total, loss = inner(1, middle, tiles - 1 - middle, *(here(v) for v in (total, loss, stack)), floor)
+    total, loss = inner(1, middle, tiles - 1 - middle, *(here(v) for v in (total, loss, stack, floor)))
     grad, spill, loss = inner(2, tiles - 1, 2, *(here(v) for v in (x, beyond, corner, side, total, loss)))
     got = lax.ppermute(spill, "gy", [(i, (i + 1) % gy) for i in range(gy)])
     pack = (chans * width // 2 // LANES + SUB, LANES)

time: 182 us -> 183 us (level)
  transfers between devices with their start and end apart: 9 -> 9, of which waited for: 6 -> 6; matrix products, arithmetic and copies ran while one was open for 0% -> 0% of each run, Pallas kernels for 61% -> 60%
where the time goes in v8:
time: 183 us
  Pallas kernels  159 us (87%)
  starting transfers between devices  11.8 us (6%)
  waiting for transfers between devices  10.2 us (6%)
    pallas_call x3, Pallas kernels, inner(): pl.pallas_call(functools.partial(inner_kernel, rows, cols, chans, slots,...  155 us
    ppermute x3, starting transfers between devices, body(): lax.ppermute(total, 'gx', [(i, i ^ step) for i in range(gx)])  8.84 us
    ppermute x3, waiting for transfers between devices, body(): lax.ppermute(total, 'gx', [(i, i ^ step) for i in range(gx)])  7.79 us
  transfers between devices with their start and end apart: 9, of which 6 were waited for; matrix products, arithmetic and copies ran while one was open for 0% of the time, Pallas kernels for 60%

profile of v8, /device:TPU:0, one launch (start us, length us, event | category | flops | bytes accessed | tf_op | source)
XLA Modules:
  0.0 183.3 jit_solution(12269554163497125495)
XLA Ops:
  0.7 0.0 copy-start.3
  0.7 0.0 copy-start.4
  0.7 0.0 copy-start.5
  0.7 0.0 copy-start.6
  0.7 0.0 copy-start.7
  0.7 1.5 pack.1
  2.2 0.4 copy-done
  2.6 1.0 logits.1
  3.6 0.6 collective-permute-start.1
  4.2 1.3 collective-permute-start
  5.5 0.0 collective-permute-done.1.refs_0_
  5.5 66.9 %inner_head.1 = (f32[1024,128]{1,0:T(8,128)S(1)}, f32[8,128]{1,0:T(8,128)S(1)}, bf16[768,256]{1,0:T(8,128)(2,1)S(1)}, f32[8,128]{1,0:T(8,128)S(1)}) custom-call(f32[96,128]{1,0:T(8,128)S(1)} %collective-permute-done.1.refs_0_, bf16[256,896]{1,0:T(8,128)(2,1)S(1)} %copy-done.6, bf16[256,896]{1,0:T(8,128)(2,1)S(1)} %copy-done.5, ...), custom_call_target="tpu_custom_call" | custom-call | flops 1000000000 | bytes 2000000 | tf_op jit(solution)/shard_map/inner_head/pallas_call | solution.py:577
  72.4 0.0 collective-permute-done.side_ref.refs_10_
  72.5 0.2 beside.1
  72.6 0.1 collective-permute-start.2
  72.7 43.9 %inner_middle.1 = (f32[1024,128]{1,0:T(8,128)S(1)}, f32[8,128]{1,0:T(8,128)S(1)}) custom-call(f32[96,128]{1,0:T(8,128)S(1)} %collective-permute-done.1.refs_0_, bf16[256,896]{1,0:T(8,128)(2,1)S(1)} %copy-done.6, bf16[256,896]{1,0:T(8,128)(2,1)S(1)} %copy-done.5, bf16[1792,128]{1,0:T(8,128)(2,1)S(1)} %copy-done.4, bf16[1792,128]{1,0:T(8,128)(2,1)S(1)} %copy-done.3, ...), custom_call_target="tpu_custom_call" | custom-call | flops 1000000000 | bytes 2000000 | tf_op jit(solution)/shard_map/inner_middle/pallas_call | solution.py:577
  116.6 0.0 collective-permute-done.2.refs_9_
  116.6 44.4 %inner_tail.1 = (f32[768,128]{1,0:T(8,128)S(1)}, f32[32,128]{1,0:T(8,128)S(1)}, f32[8,128]{1,0:T(8,128)S(1)}) custom-call(f32[96,128]{1,0:T(8,128)S(1)} %collective-permute-done.1.refs_0_, bf16[256,896]{1,0:T(8,128)(2,1)S(1)} %copy-done.6, bf16[256,896]{1,0:T(8,128)(2,1)S(1)} %copy-done.5, bf16[1792,128]{1,0:T(8,128)(2,1)S(1)} %copy-done.4, ...), custom_call_target="tpu_custom_call" | custom-call | flops 1000000000 | bytes 2000000 | tf_op jit(solution)/shard_map/inner_tail/pallas_call | solution.py:577
  161.1 0.5 collective-permute-start.3
  162.3 0.2 collective-permute-done.3.got_ref
  162.4 0.7 grad.1
  163.2 0.4 collective-permute-start.4
  163.6 0.9 collective-permute-done.4
  164.5 2.6 %collective-permute-start.5 = (f32[168,128]{1,0:T(8,128)S(1)}, f32[168,128]{1,0:T(8,128)S(1)}, u32[]{:S(2)}, u32[]{:S(2)}) collective-permute-start(f32[168,128]{1,0:T(8,128)S(1)} %add.12), channel_id=1, source_target_pairs={{0,2},{2,0},{4,6},{6,4},{8,10},{10,8},{12,14},{14,12},{1,3},{3,1},... | collective-permute-start | bytes 258056 | tf_op jit(solution)/shard_map/ppermute | solution.py:626
  167.2 2.9 %collective-permute-done.5 = f32[168,128]{1,0:T(8,128)S(1)} collective-permute-done((f32[168,128]{1,0:T(8,128)S(1)}, f32[168,128]{1,0:T(8,128)S(1)}, u32[]{:S(2)}, u32[]{:S(2)}) %collective-permute-start.5) | collective-permute-done | bytes 86048 | tf_op jit(solution)/shard_map/ppermute | solution.py:626
  170.0 3.1 %collective-permute-start.6 = (f32[168,128]{1,0:T(8,128)S(1)}, f32[168,128]{1,0:T(8,128)S(1)}, u32[]{:S(2)}, u32[]{:S(2)}) collective-permute-start(f32[168,128]{1,0:T(8,128)S(1)} %add.13), channel_id=1, source_target_pairs={{0,4},{2,6},{4,0},{6,2},{8,12},{10,14},{12,8},{14,10},{1,5},{3,7},... | collective-permute-start | bytes 258056 | tf_op jit(solution)/shard_map/ppermute | solution.py:626
  173.1 2.5 %collective-permute-done.6 = f32[168,128]{1,0:T(8,128)S(1)} collective-permute-done((f32[168,128]{1,0:T(8,128)S(1)}, f32[168,128]{1,0:T(8,128)S(1)}, u32[]{:S(2)}, u32[]{:S(2)}) %collective-permute-start.6) | collective-permute-done | bytes 86048 | tf_op jit(solution)/shard_map/ppermute | solution.py:626
  175.6 3.1 %collective-permute-start.7 = (f32[168,128]{1,0:T(8,128)S(1)}, f32[168,128]{1,0:T(8,128)S(1)}, u32[]{:S(2)}, u32[]{:S(2)}) collective-permute-start(f32[168,128]{1,0:T(8,128)S(1)} %add.14), channel_id=1, source_target_pairs={{0,8},{2,10},{4,12},{6,14},{8,0},{10,2},{12,4},{14,6},{1,9},{3,11}... | collective-permute-start | bytes 258056 | tf_op jit(solution)/shard_map/ppermute | solution.py:626
  178.7 2.5 %collective-permute-done.7 = f32[168,128]{1,0:T(8,128)S(1)} collective-permute-done((f32[168,128]{1,0:T(8,128)S(1)}, f32[168,128]{1,0:T(8,128)S(1)}, u32[]{:S(2)}, u32[]{:S(2)}) %collective-permute-start.7) | collective-permute-done | bytes 86048 | tf_op jit(solution)/shard_map/ppermute | solution.py:626
  181.2 0.1 collective-permute-start.8
  181.3 1.3 collective-permute-done.8.z_ref
  182.5 0.7 final.1
  (14 shorter events, 0.1 us)
Async XLA Ops:
  0.6 2.0 %copy-start = (bf16[16,64,1280]{2,1,0:T(8,128)(2,1)S(1)}, bf16[16,64,1280]{2,1,0:T(8,128)(2,1)}, u32[]{:S(2)}) copy-start(bf16[16,64,1280]{2,1,0:T(8,128)(2,1)} %f_ref.5) | copy-start | bytes 7864324
  0.6 4.8 %copy-start.1 = (s32[224,896]{1,0:T(8,128)S(1)}, s32[224,896]{1,0:T(8,128)}, u32[]{:S(2)}) copy-start(s32[224,896]{1,0:T(8,128)} %refs_5_.5) | copy-start | bytes 2408452
  0.7 4.8 %copy-start.2 = (s32[224,896]{1,0:T(8,128)S(1)}, s32[224,896]{1,0:T(8,128)}, u32[]{:S(2)}) copy-start(s32[224,896]{1,0:T(8,128)} %refs_6_.5) | copy-start | bytes 2408452
  0.7 4.8 %copy-start.3 = (bf16[1792,128]{1,0:T(8,128)(2,1)S(1)}, bf16[1792,128]{1,0:T(8,128)(2,1)}, u32[]{:S(2)}) copy-start(bf16[1792,128]{1,0:T(8,128)(2,1)} %constant.13.clone.refs_4_) | copy-start | bytes 1376260
  0.7 4.8 %copy-start.4 = (bf16[1792,128]{1,0:T(8,128)(2,1)S(1)}, bf16[1792,128]{1,0:T(8,128)(2,1)}, u32[]{:S(2)}) copy-start(bf16[1792,128]{1,0:T(8,128)(2,1)} %constant.12.clone.refs_3_) | copy-start | bytes 1376260
  0.7 4.8 %copy-start.5 = (bf16[256,896]{1,0:T(8,128)(2,1)S(1)}, bf16[256,896]{1,0:T(8,128)(2,1)}, u32[]{:S(2)}) copy-start(bf16[256,896]{1,0:T(8,128)(2,1)} %constant.11.clone.refs_2_) | copy-start | bytes 1376260
  0.7 4.8 %copy-start.6 = (bf16[256,896]{1,0:T(8,128)(2,1)S(1)}, bf16[256,896]{1,0:T(8,128)(2,1)}, u32[]{:S(2)}) copy-start(bf16[256,896]{1,0:T(8,128)(2,1)} %constant.10.clone.refs_1_) | copy-start | bytes 1376260
  0.7 4.8 %copy-start.7 = (bf16[512,128]{1,0:T(8,128)(2,1)S(1)}, bf16[512,128]{1,0:T(8,128)(2,1)}, u32[]{:S(2)}) copy-start(bf16[512,128]{1,0:T(8,128)(2,1)} %constant.14.clone.refs_9_) | copy-start | bytes 393220
  3.6 1.8 %collective-permute-start.1 = (f32[96,128]{1,0:T(8,128)S(1)}, f32[96,128]{1,0:T(8,128)S(1)}, u32[]{:S(2)}, u32[]{:S(2)}) collective-permute-start(f32[96,128]{1,0:T(8,128)S(1)} %get-tuple-element.31), channel_id=1, source_target_pairs={{0,1},{1,0},{2,3},{3,2},{4,5},{5,4},{6,7},{7,6},{8,9},{9,8},{10,11... | collective-permute-start | bytes 147464 | tf_op jit(solution)/shard_map/ppermute | solution.py:535
  4.2 68.3 %collective-permute-start = (f32[176,128]{1,0:T(8,128)S(1)}, f32[176,128]{1,0:T(8,128)S(1)}, u32[]{:S(2)}, u32[]{:S(2)}) collective-permute-start(f32[176,128]{1,0:T(8,128)S(1)} %get-tuple-element.27.side_ref.refs_8_), channel_id=1, source_target_pairs={{2,0},{4,2},{6,4},{8,6},{10,8},{12,10},{14,12},{3,1},{5,3},{7,5},{... | collective-permute-start | bytes 270344 | tf_op jit(solution)/shard_map/ppermute | solution.py:557
  72.6 44.0 %collective-permute-start.2 = (f32[40,128]{1,0:T(8,128)S(1)}, f32[40,128]{1,0:T(8,128)S(1)}, u32[]{:S(2)}, u32[]{:S(2)}) collective-permute-start(f32[40,128]{1,0:T(8,128)S(1)} %get-tuple-element.36.refs_8_), channel_id=1, source_target_pairs={{0,1},{1,0},{2,3},{3,2},{4,5},{5,4},{6,7},{7,6},{8,9},{9,8},{10,11... | collective-permute-start | bytes 61448 | tf_op jit(solution)/shard_map/ppermute | solution.py:535
  161.1 1.4 collective-permute-start.3
  163.2 1.3 collective-permute-start.4
  164.5 5.5 %collective-permute-start.5 = (f32[168,128]{1,0:T(8,128)S(1)}, f32[168,128]{1,0:T(8,128)S(1)}, u32[]{:S(2)}, u32[]{:S(2)}) collective-permute-start(f32[168,128]{1,0:T(8,128)S(1)} %add.12), channel_id=1, source_target_pairs={{0,2},{2,0},{4,6},{6,4},{8,10},{10,8},{12,14},{14,12},{1,3},{3,1},... | collective-permute-start | bytes 258056 | tf_op jit(solution)/shard_map/ppermute | solution.py:626
  170.0 5.6 %collective-permute-start.6 = (f32[168,128]{1,0:T(8,128)S(1)}, f32[168,128]{1,0:T(8,128)S(1)}, u32[]{:S(2)}, u32[]{:S(2)}) collective-permute-start(f32[168,128]{1,0:T(8,128)S(1)} %add.13), channel_id=1, source_target_pairs={{0,4},{2,6},{4,0},{6,2},{8,12},{10,14},{12,8},{14,10},{1,5},{3,7},... | collective-permute-start | bytes 258056 | tf_op jit(solution)/shard_map/ppermute | solution.py:626
  175.6 5.6 %collective-permute-start.7 = (f32[168,128]{1,0:T(8,128)S(1)}, f32[168,128]{1,0:T(8,128)S(1)}, u32[]{:S(2)}, u32[]{:S(2)}) collective-permute-start(f32[168,128]{1,0:T(8,128)S(1)} %add.14), channel_id=1, source_target_pairs={{0,8},{2,10},{4,12},{6,14},{8,0},{10,2},{12,4},{14,6},{1,9},{3,11}... | collective-permute-start | bytes 258056 | tf_op jit(solution)/shard_map/ppermute | solution.py:626
  181.2 1.3 collective-permute-start.8

commit v9 on v8

--- a/solution.py
+++ b/solution.py
@@ -8,6 +8,7 @@
 from jax.experimental import pallas as pl
 from jax.experimental.pallas import tpu as pltpu
 from jax.sharding import PartitionSpec as P
+
 
 PATCH = 14
 HALF = PATCH // 2
@@ -23,10 +24,6 @@
 ANY = pl.BlockSpec(memory_space=pl.ANY)
 ROOM = pltpu.CompilerParams(vmem_limit_bytes=16 * 2**20)
 SMEM = pl.BlockSpec(memory_space=pltpu.SMEM)
-
-
-def whole(shape):
-    return pl.BlockSpec(shape, lambda *ids: (0,) * len(shape))
 
 
 def column_tables(cols):
@@ -158,11 +155,10 @@
     h_ref[3 * c + 2] = run + lean * mid
 
 
-def softmax_fast(groups, chans, slots, fold, w_ref, p_ref, packed, h_ref):
+def softmax_fast(groups, chans, slots, fold, w_ref, p_ref):
     sums = [None] * (2 * groups * HALF)
-    for c in range(chans):
-        tally(packed, c, h_ref)
-        for b in range(groups):
+    for b in range(groups):
+        for c in range(chans):
             row = c * slots + SUB * b
             upper = w_ref[row : row + SUB, :]
             lower = w_ref[row + 1 : row + 1 + SUB, :]
@@ -224,7 +220,7 @@
 
     @pl.when(fast)
     def _():
-        sums = softmax_fast(groups, chans, slots, fold, w_ref, p_ref, packed, h_ref)
+        sums = softmax_fast(groups, chans, slots, fold, w_ref, p_ref)
         for k in range(count):
             s_ref[k] = sums[k]
         s_ref[count] = jnp.zeros((SUB, LANES), f32)
@@ -236,7 +232,6 @@
         for k in range(count):
             s_ref[k] = sums[k]
         s_ref[count] = losses
-        lax.fori_loop(0, chans, lambda c, _: tally(packed, c, h_ref), None)
         prepare()
 
     loss = jnp.zeros((SUB, LANES), f32)
@@ -248,6 +243,7 @@
     picked = jnp.zeros((SUB, LANES), f32)
     tall = groups * SUB
     for c in range(chans):
+        tally(packed, c, h_ref)
         hits = [h_ref[3 * c + k].astype(f32) for k in range(3)]
         parts = [[], []]
         for b in range(groups):
@@ -591,7 +587,6 @@
             ] + ([pltpu.VMEM(sums, f32), stacked] if part == 2 else []),
             cost_estimate=pl.CostEstimate(flops=10**9, bytes_accessed=2 * 10**6, transcendentals=10**6),
             compiler_params=ROOM,
-            name=("inner_head", "inner_middle", "inner_tail")[part],
         )(*(here(v) for v in (got, lift, lift_end, back, back_end, labels, valid_mask)), *args)
 
     middle = tiles // 2 + 1

time: 183 us -> 181 us (0.989)
  Pallas kernels: 159 us -> 157 us
    pallas_call x3, Pallas kernels: 155 us -> 153 us  [inner(): pl.pallas_call(functools.partial(inner_kernel, rows, cols, chans, slots,...]
where the time goes in v9:
time: 181 us
  Pallas kernels  157 us (87%)
  starting transfers between devices  11.8 us (7%)
  waiting for transfers between devices  10.2 us (6%)
    pallas_call x3, Pallas kernels, inner(): pl.pallas_call(functools.partial(inner_kernel, rows, cols, chans, slots,...  153 us
    ppermute x3, starting transfers between devices, body(): lax.ppermute(total, 'gx', [(i, i ^ step) for i in range(gx)])  8.87 us
    ppermute x3, waiting for transfers between devices, body(): lax.ppermute(total, 'gx', [(i, i ^ step) for i in range(gx)])  7.79 us
  transfers between devices with their start and end apart: 9, of which 6 were waited for; matrix products, arithmetic and copies ran while one was open for 0% of the time, Pallas kernels for 60%

profile of v9, /device:TPU:0, one launch (start us, length us, event | category | flops | bytes accessed | tf_op | source)
XLA Modules:
  0.0 181.2 jit_solution(16694522770653319871)
XLA Ops:
  0.7 0.0 copy-start.3
  0.7 0.0 copy-start.4
  0.7 0.0 copy-start.5
  0.7 0.0 copy-start.6
  0.7 0.0 copy-start.7
  0.7 1.5 pack.1
  2.2 0.4 copy-done
  2.6 1.0 logits.1
  3.6 0.6 collective-permute-start.1
  4.2 1.3 collective-permute-start
  5.5 0.0 collective-permute-done.1.refs_0_
  5.5 66.0 %shard_map.130 = (f32[1024,128]{1,0:T(8,128)S(1)}, f32[8,128]{1,0:T(8,128)S(1)}, bf16[768,256]{1,0:T(8,128)(2,1)S(1)}, f32[8,128]{1,0:T(8,128)S(1)}) custom-call(f32[96,128]{1,0:T(8,128)S(1)} %collective-permute-done.1.refs_0_, bf16[256,896]{1,0:T(8,128)(2,1)S(1)} %copy-done.6, bf16[256,896]{1,0:T(8,128)(2,1)S(1)} %copy-done.5, ...), custom_call_target="tpu_custom_call" | custom-call | flops 1000000000 | bytes 2000000 | tf_op jit(solution)/shard_map/pallas_call | solution.py:573
  71.5 0.0 collective-permute-done.side_ref.refs_10_
  71.6 0.2 beside.1
  71.7 0.1 collective-permute-start.2
  71.8 43.3 %shard_map.131 = (f32[1024,128]{1,0:T(8,128)S(1)}, f32[8,128]{1,0:T(8,128)S(1)}) custom-call(f32[96,128]{1,0:T(8,128)S(1)} %collective-permute-done.1.refs_0_, bf16[256,896]{1,0:T(8,128)(2,1)S(1)} %copy-done.6, bf16[256,896]{1,0:T(8,128)(2,1)S(1)} %copy-done.5, bf16[1792,128]{1,0:T(8,128)(2,1)S(1)} %copy-done.4, bf16[1792,128]{1,0:T(8,128)(2,1)S(1)} %copy-done.3, ...), custom_call_target="tpu_custom_call" | custom-call | flops 1000000000 | bytes 2000000 | tf_op jit(solution)/shard_map/pallas_call | solution.py:573
  115.2 0.0 collective-permute-done.2.refs_9_
  115.2 43.8 %shard_map.132 = (f32[768,128]{1,0:T(8,128)S(1)}, f32[32,128]{1,0:T(8,128)S(1)}, f32[8,128]{1,0:T(8,128)S(1)}) custom-call(f32[96,128]{1,0:T(8,128)S(1)} %collective-permute-done.1.refs_0_, bf16[256,896]{1,0:T(8,128)(2,1)S(1)} %copy-done.6, bf16[256,896]{1,0:T(8,128)(2,1)S(1)} %copy-done.5, bf16[1792,128]{1,0:T(8,128)(2,1)S(1)} %copy-done.4, ...), custom_call_target="tpu_custom_call" | custom-call | flops 1000000000 | bytes 2000000 | tf_op jit(solution)/shard_map/pallas_call | solution.py:573
  159.0 0.5 collective-permute-start.3
  160.2 0.2 collective-permute-done.3.got_ref
  160.3 0.7 grad.1
  161.1 0.4 collective-permute-start.4
  161.5 0.9 collective-permute-done.4
  162.4 2.6 %collective-permute-start.5 = (f32[168,128]{1,0:T(8,128)S(1)}, f32[168,128]{1,0:T(8,128)S(1)}, u32[]{:S(2)}, u32[]{:S(2)}) collective-permute-start(f32[168,128]{1,0:T(8,128)S(1)} %add.12), channel_id=1, source_target_pairs={{0,2},{2,0},{4,6},{6,4},{8,10},{10,8},{12,14},{14,12},{1,3},{3,1},... | collective-permute-start | bytes 258056 | tf_op jit(solution)/shard_map/ppermute | solution.py:621
  165.1 2.9 %collective-permute-done.5 = f32[168,128]{1,0:T(8,128)S(1)} collective-permute-done((f32[168,128]{1,0:T(8,128)S(1)}, f32[168,128]{1,0:T(8,128)S(1)}, u32[]{:S(2)}, u32[]{:S(2)}) %collective-permute-start.5) | collective-permute-done | bytes 86048 | tf_op jit(solution)/shard_map/ppermute | solution.py:621
  167.9 3.1 %collective-permute-start.6 = (f32[168,128]{1,0:T(8,128)S(1)}, f32[168,128]{1,0:T(8,128)S(1)}, u32[]{:S(2)}, u32[]{:S(2)}) collective-permute-start(f32[168,128]{1,0:T(8,128)S(1)} %add.13), channel_id=1, source_target_pairs={{0,4},{2,6},{4,0},{6,2},{8,12},{10,14},{12,8},{14,10},{1,5},{3,7},... | collective-permute-start | bytes 258056 | tf_op jit(solution)/shard_map/ppermute | solution.py:621
  171.1 2.5 %collective-permute-done.6 = f32[168,128]{1,0:T(8,128)S(1)} collective-permute-done((f32[168,128]{1,0:T(8,128)S(1)}, f32[168,128]{1,0:T(8,128)S(1)}, u32[]{:S(2)}, u32[]{:S(2)}) %collective-permute-start.6) | collective-permute-done | bytes 86048 | tf_op jit(solution)/shard_map/ppermute | solution.py:621
  173.5 3.1 %collective-permute-start.7 = (f32[168,128]{1,0:T(8,128)S(1)}, f32[168,128]{1,0:T(8,128)S(1)}, u32[]{:S(2)}, u32[]{:S(2)}) collective-permute-start(f32[168,128]{1,0:T(8,128)S(1)} %add.14), channel_id=1, source_target_pairs={{0,8},{2,10},{4,12},{6,14},{8,0},{10,2},{12,4},{14,6},{1,9},{3,11}... | collective-permute-start | bytes 258056 | tf_op jit(solution)/shard_map/ppermute | solution.py:621
  176.6 2.5 %collective-permute-done.7 = f32[168,128]{1,0:T(8,128)S(1)} collective-permute-done((f32[168,128]{1,0:T(8,128)S(1)}, f32[168,128]{1,0:T(8,128)S(1)}, u32[]{:S(2)}, u32[]{:S(2)}) %collective-permute-start.7) | collective-permute-done | bytes 86048 | tf_op jit(solution)/shard_map/ppermute | solution.py:621
  179.1 0.1 collective-permute-start.8
  179.2 1.3 collective-permute-done.8.z_ref
  180.5 0.7 final.1
  (14 shorter events, 0.1 us)
Async XLA Ops:
  0.6 2.0 %copy-start = (bf16[16,64,1280]{2,1,0:T(8,128)(2,1)S(1)}, bf16[16,64,1280]{2,1,0:T(8,128)(2,1)}, u32[]{:S(2)}) copy-start(bf16[16,64,1280]{2,1,0:T(8,128)(2,1)} %f_ref.5) | copy-start | bytes 7864324
  0.6 4.8 %copy-start.1 = (s32[224,896]{1,0:T(8,128)S(1)}, s32[224,896]{1,0:T(8,128)}, u32[]{:S(2)}) copy-start(s32[224,896]{1,0:T(8,128)} %refs_5_.5) | copy-start | bytes 2408452
  0.7 4.8 %copy-start.2 = (s32[224,896]{1,0:T(8,128)S(1)}, s32[224,896]{1,0:T(8,128)}, u32[]{:S(2)}) copy-start(s32[224,896]{1,0:T(8,128)} %refs_6_.5) | copy-start | bytes 2408452
  0.7 4.8 %copy-start.3 = (bf16[1792,128]{1,0:T(8,128)(2,1)S(1)}, bf16[1792,128]{1,0:T(8,128)(2,1)}, u32[]{:S(2)}) copy-start(bf16[1792,128]{1,0:T(8,128)(2,1)} %constant.13.clone.refs_4_) | copy-start | bytes 1376260
  0.7 4.8 %copy-start.4 = (bf16[1792,128]{1,0:T(8,128)(2,1)S(1)}, bf16[1792,128]{1,0:T(8,128)(2,1)}, u32[]{:S(2)}) copy-start(bf16[1792,128]{1,0:T(8,128)(2,1)} %constant.12.clone.refs_3_) | copy-start | bytes 1376260
  0.7 4.8 %copy-start.5 = (bf16[256,896]{1,0:T(8,128)(2,1)S(1)}, bf16[256,896]{1,0:T(8,128)(2,1)}, u32[]{:S(2)}) copy-start(bf16[256,896]{1,0:T(8,128)(2,1)} %constant.11.clone.refs_2_) | copy-start | bytes 1376260
  0.7 4.8 %copy-start.6 = (bf16[256,896]{1,0:T(8,128)(2,1)S(1)}, bf16[256,896]{1,0:T(8,128)(2,1)}, u32[]{:S(2)}) copy-start(bf16[256,896]{1,0:T(8,128)(2,1)} %constant.10.clone.refs_1_) | copy-start | bytes 1376260
  0.7 4.8 %copy-start.7 = (bf16[512,128]{1,0:T(8,128)(2,1)S(1)}, bf16[512,128]{1,0:T(8,128)(2,1)}, u32[]{:S(2)}) copy-start(bf16[512,128]{1,0:T(8,128)(2,1)} %constant.14.clone.refs_9_) | copy-start | bytes 393220
  3.6 1.8 %collective-permute-start.1 = (f32[96,128]{1,0:T(8,128)S(1)}, f32[96,128]{1,0:T(8,128)S(1)}, u32[]{:S(2)}, u32[]{:S(2)}) collective-permute-start(f32[96,128]{1,0:T(8,128)S(1)} %get-tuple-element.31), channel_id=1, source_target_pairs={{0,1},{1,0},{2,3},{3,2},{4,5},{5,4},{6,7},{7,6},{8,9},{9,8},{10,11... | collective-permute-start | bytes 147464 | tf_op jit(solution)/shard_map/ppermute | solution.py:531
  4.2 67.4 %collective-permute-start = (f32[176,128]{1,0:T(8,128)S(1)}, f32[176,128]{1,0:T(8,128)S(1)}, u32[]{:S(2)}, u32[]{:S(2)}) collective-permute-start(f32[176,128]{1,0:T(8,128)S(1)} %get-tuple-element.27.side_ref.refs_8_), channel_id=1, source_target_pairs={{2,0},{4,2},{6,4},{8,6},{10,8},{12,10},{14,12},{3,1},{5,3},{7,5},{... | collective-permute-start | bytes 270344 | tf_op jit(solution)/shard_map/ppermute | solution.py:553
  71.7 43.4 %collective-permute-start.2 = (f32[40,128]{1,0:T(8,128)S(1)}, f32[40,128]{1,0:T(8,128)S(1)}, u32[]{:S(2)}, u32[]{:S(2)}) collective-permute-start(f32[40,128]{1,0:T(8,128)S(1)} %get-tuple-element.36.refs_8_), channel_id=1, source_target_pairs={{0,1},{1,0},{2,3},{3,2},{4,5},{5,4},{6,7},{7,6},{8,9},{9,8},{10,11... | collective-permute-start | bytes 61448 | tf_op jit(solution)/shard_map/ppermute | solution.py:531
  159.0 1.4 collective-permute-start.3
  161.1 1.3 collective-permute-start.4
  162.4 5.5 %collective-permute-start.5 = (f32[168,128]{1,0:T(8,128)S(1)}, f32[168,128]{1,0:T(8,128)S(1)}, u32[]{:S(2)}, u32[]{:S(2)}) collective-permute-start(f32[168,128]{1,0:T(8,128)S(1)} %add.12), channel_id=1, source_target_pairs={{0,2},{2,0},{4,6},{6,4},{8,10},{10,8},{12,14},{14,12},{1,3},{3,1},... | collective-permute-start | bytes 258056 | tf_op jit(solution)/shard_map/ppermute | solution.py:621
  167.9 5.6 %collective-permute-start.6 = (f32[168,128]{1,0:T(8,128)S(1)}, f32[168,128]{1,0:T(8,128)S(1)}, u32[]{:S(2)}, u32[]{:S(2)}) collective-permute-start(f32[168,128]{1,0:T(8,128)S(1)} %add.13), channel_id=1, source_target_pairs={{0,4},{2,6},{4,0},{6,2},{8,12},{10,14},{12,8},{14,10},{1,5},{3,7},... | collective-permute-start | bytes 258056 | tf_op jit(solution)/shard_map/ppermute | solution.py:621
  173.5 5.6 %collective-permute-start.7 = (f32[168,128]{1,0:T(8,128)S(1)}, f32[168,128]{1,0:T(8,128)S(1)}, u32[]{:S(2)}, u32[]{:S(2)}) collective-permute-start(f32[168,128]{1,0:T(8,128)S(1)} %add.14), channel_id=1, source_target_pairs={{0,8},{2,10},{4,12},{6,14},{8,0},{10,2},{12,4},{14,6},{1,9},{3,11}... | collective-permute-start | bytes 258056 | tf_op jit(solution)/shard_map/ppermute | solution.py:621
  179.1 1.3 collective-permute-start.8

commit v10 on v8

--- a/solution.py
+++ b/solution.py
@@ -325,13 +325,15 @@
 
 
 def inner_kernel(rows, cols, chans, slots, groups, part, begin, tiles, *refs):
-    (got_ref, lift_ref, lift_end_ref, back_ref, back_end_ref, lab_ref, mask_ref), refs = refs[:7], refs[7:]
+    (got_ref, lift_ref, back_ref, lab_ref, mask_ref), refs = refs[:5], refs[5:]
     if part == 0:
         (x_ref, own_ref, fill_ref, sum_ref, loss_ref, stack_ref, floor_out_ref), refs = refs[:7], refs[7:]
     elif part == 1:
         (sum_in_ref, loss_in_ref, stack_ref, floor_in_ref, sum_ref, loss_ref), refs = refs[:6], refs[6:]
     else:
-        (x_ref, beyond_ref, corner_ref, strip_ref, sum_in_ref, loss_in_ref), refs = refs[:6], refs[6:]
+        (x_ref, beyond_ref, corner_ref, strip_ref, sum_in_ref, loss_in_ref, lift_end_ref, back_end_ref), refs = (
+            refs[:8], refs[8:],
+        )
         (out_ref, spill_ref, loss_ref), refs = refs[:3], refs[3:]
     (w_ref, p_ref, s_ref, lhs_ref, tile_ref, h_ref, floor_ref), refs = refs[:7], refs[7:]
     if part == 2:
@@ -348,7 +350,11 @@
 
     def lift(at):
         lanes = pl.ds(pl.multiple_of(at * LANES, LANES), LANES)
-        table = jnp.where(last_col, lift_end_ref[:, lanes], lift_ref[:, lanes])
+        table = lift_ref[:, lanes]
+        if part == 2:
+            order = jnp.minimum(lax.rem(at + 1, tiles), 1)
+            end = lift_end_ref[:, pl.ds(pl.multiple_of(order * LANES, LANES), LANES)]
+            table = jnp.where(last_col, end, table)
         return jnp.dot(stack_ref[...], table, preferred_element_type=f32)
 
     @pl.when(step == 0)
@@ -410,7 +416,10 @@
     loss_ref[...] += pixels(groups, chans, slots, fold, tile_ref, fast, prepare, w_ref.at[now], p_ref, s_ref, lhs_ref, h_ref)
     depth = 2 * LANES
     deep = pl.ds(pl.multiple_of(which * depth, depth), depth)
-    table = jnp.where(last_col, back_end_ref[deep, :], back_ref[deep, :])
+    table = back_ref[deep, :]
+    if part == 2:
+        end = back_end_ref[pl.ds(pl.multiple_of(lax.rem(which + 1, tiles) * depth, depth), depth), :]
+        table = jnp.where(last_col, end, table)
     sum_ref[...] += jnp.dot(lhs_ref[...], table, preferred_element_type=f32)
 
     if part == 0:
@@ -518,6 +527,7 @@
         return out.reshape(-1, LANES)
 
     inside, ending = column_tables(cols)
+    ending = np.concatenate([ending[:, -LANES:], ending[:, :LANES]], axis=1)
     lift, lift_end, back, back_end = (
         jnp.asarray(t, bf16) for t in (forward(inside), forward(ending), backward(inside), backward(ending))
     )
@@ -572,12 +582,12 @@
         outs = [
             ([held(*sums), held(SUB, LANES), stacked, held(SUB, LANES)], [VMEM] * 4, [VMEM] * 3),
             ([held(*sums), held(SUB, LANES)], [VMEM] * 2, [VMEM] * 4),
-            ([held(tall_x, LANES), held(chans, LANES), held(SUB, LANES)], [VMEM] * 3, [VMEM] * 6),
+            ([held(tall_x, LANES), held(chans, LANES), held(SUB, LANES)], [VMEM] * 3, [VMEM] * 8),
         ][part]
         return pl.pallas_call(
             functools.partial(inner_kernel, rows, cols, chans, slots, groups, part, begin, tiles),
             grid=(steps,),
-            in_specs=[VMEM] * 7 + outs[2],
+            in_specs=[VMEM] * 5 + outs[2],
             out_specs=outs[1],
             out_shape=outs[0],
             scratch_shapes=[
@@ -592,7 +602,7 @@
             cost_estimate=pl.CostEstimate(flops=10**9, bytes_accessed=2 * 10**6, transcendentals=10**6),
             compiler_params=ROOM,
             name=("inner_head", "inner_middle", "inner_tail")[part],
-        )(*(here(v) for v in (got, lift, lift_end, back, back_end, labels, valid_mask)), *args)
+        )(*(here(v) for v in (got, lift, back, labels, valid_mask)), *args)
 
     middle = tiles // 2 + 1
     total, loss, stack, floor = inner(0, 1, middle - 1, here(x), here(own), here(fill))
@@ -607,7 +617,7 @@
     )(here(side), here(weight), here(shift))
     corner = ring(beyond, "gy")
     total, loss = inner(1, middle, tiles - 1 - middle, *(here(v) for v in (total, loss, stack, floor)))
-    grad, spill, loss = inner(2, tiles - 1, 2, *(here(v) for v in (x, beyond, corner, side, total, loss)))
+    grad, spill, loss = inner(2, tiles - 1, 2, *(here(v) for v in (x, beyond, corner, side, total, loss, lift_end, back_end)))
     got = lax.ppermute(spill, "gy", [(i, (i + 1) % gy) for i in range(gy)])
     pack = (chans * width // 2 // LANES + SUB, LANES)
     mine, other = pl.pallas_call(

time: 183 us -> 185 us (1.011)
  Pallas kernels: 159 us -> 161 us
  transfers between devices with their start and end apart: 9 -> 9, of which waited for: 6 -> 6; matrix products, arithmetic and copies ran while one was open for 0% -> 0% of each run, Pallas kernels for 60% -> 61%
where the time goes in v10:
time: 185 us
  Pallas kernels  161 us (87%)
  starting transfers between devices  11.8 us (6%)
  waiting for transfers between devices  10.2 us (6%)
    pallas_call x3, Pallas kernels, inner(): pl.pallas_call(functools.partial(inner_kernel, rows, cols, chans, slots,...  157 us
    ppermute x3, starting transfers between devices, body(): lax.ppermute(total, 'gx', [(i, i ^ step) for i in range(gx)])  8.85 us
    ppermute x3, waiting for transfers between devices, body(): lax.ppermute(total, 'gx', [(i, i ^ step) for i in range(gx)])  7.79 us
  transfers between devices with their start and end apart: 9, of which 6 were waited for; matrix products, arithmetic and copies ran while one was open for 0% of the time, Pallas kernels for 61%

profile of v10, /device:TPU:0, one launch (start us, length us, event | category | flops | bytes accessed | tf_op | source)
XLA Modules:
  0.0 184.6 jit_solution(14476467260691136697)
XLA Ops:
  0.7 0.0 copy-start.3
  0.7 0.0 copy-start.4
  0.7 0.0 copy-start.7
  0.7 1.5 pack.1
  2.2 0.4 copy-done
  2.6 1.0 logits.1
  3.6 0.6 collective-permute-start.1
  4.2 1.3 collective-permute-start
  5.5 0.0 collective-permute-done.1.refs_0_
  5.5 67.7 %inner_head.1 = (f32[1024,128]{1,0:T(8,128)S(1)}, f32[8,128]{1,0:T(8,128)S(1)}, bf16[768,256]{1,0:T(8,128)(2,1)S(1)}, f32[8,128]{1,0:T(8,128)S(1)}) custom-call(f32[96,128]{1,0:T(8,128)S(1)} %collective-permute-done.1.refs_0_, bf16[256,896]{1,0:T(8,128)(2,1)S(1)} %copy-done.4, bf16[1792,128]{1,0:T(8,128)(2,1)S(1)} %copy-done.3, s32[224,896]{1,0:T(8,128)S(1)} %copy-done.1, ...), custom_call_target="tpu_custom_call" | custom-call | flops 1000000000 | bytes 2000000 | tf_op jit(solution)/shard_map/inner_head/pallas_call | solution.py:587
  73.2 0.0 copy-start.5
  73.2 0.0 copy-start.6
  73.2 0.0 collective-permute-done.side_ref.refs_8_
  73.2 0.2 beside.1
  73.4 0.1 collective-permute-start.2
  73.5 44.4 %inner_middle.1 = (f32[1024,128]{1,0:T(8,128)S(1)}, f32[8,128]{1,0:T(8,128)S(1)}) custom-call(f32[96,128]{1,0:T(8,128)S(1)} %collective-permute-done.1.refs_0_, bf16[256,896]{1,0:T(8,128)(2,1)S(1)} %copy-done.4, bf16[1792,128]{1,0:T(8,128)(2,1)S(1)} %copy-done.3, s32[224,896]{1,0:T(8,128)S(1)} %copy-done.1, s32[224,896]{1,0:T(8,128)S(1)} %copy-done.2, ...), custom_call_target="tpu_custom_call" | custom-call | flops 1000000000 | bytes 2000000 | tf_op jit(solution)/shard_map/inner_middle/pallas_call | solution.py:587
  117.9 0.0 collective-permute-done.2.refs_7_
  117.9 44.5 %inner_tail.1 = (f32[768,128]{1,0:T(8,128)S(1)}, f32[32,128]{1,0:T(8,128)S(1)}, f32[8,128]{1,0:T(8,128)S(1)}) custom-call(f32[96,128]{1,0:T(8,128)S(1)} %collective-permute-done.1.refs_0_, bf16[256,896]{1,0:T(8,128)(2,1)S(1)} %copy-done.4, bf16[1792,128]{1,0:T(8,128)(2,1)S(1)} %copy-done.3, s32[224,896]{1,0:T(8,128)S(1)} %copy-done.1, ...), custom_call_target="tpu_custom_call" | custom-call | flops 1000000000 | bytes 2000000 | tf_op jit(solution)/shard_map/inner_tail/pallas_call | solution.py:587
  162.4 0.5 collective-permute-start.3
  163.6 0.2 collective-permute-done.3.got_ref
  163.8 0.7 grad.1
  164.5 0.4 collective-permute-start.4
  164.9 0.9 collective-permute-done.4
  165.9 2.6 %collective-permute-start.5 = (f32[168,128]{1,0:T(8,128)S(1)}, f32[168,128]{1,0:T(8,128)S(1)}, u32[]{:S(2)}, u32[]{:S(2)}) collective-permute-start(f32[168,128]{1,0:T(8,128)S(1)} %add.12), channel_id=1, source_target_pairs={{0,2},{2,0},{4,6},{6,4},{8,10},{10,8},{12,14},{14,12},{1,3},{3,1},... | collective-permute-start | bytes 258056 | tf_op jit(solution)/shard_map/ppermute | solution.py:636
  168.5 2.9 %collective-permute-done.5 = f32[168,128]{1,0:T(8,128)S(1)} collective-permute-done((f32[168,128]{1,0:T(8,128)S(1)}, f32[168,128]{1,0:T(8,128)S(1)}, u32[]{:S(2)}, u32[]{:S(2)}) %collective-permute-start.5) | collective-permute-done | bytes 86048 | tf_op jit(solution)/shard_map/ppermute | solution.py:636
  171.4 3.1 %collective-permute-start.6 = (f32[168,128]{1,0:T(8,128)S(1)}, f32[168,128]{1,0:T(8,128)S(1)}, u32[]{:S(2)}, u32[]{:S(2)}) collective-permute-start(f32[168,128]{1,0:T(8,128)S(1)} %add.13), channel_id=1, source_target_pairs={{0,4},{2,6},{4,0},{6,2},{8,12},{10,14},{12,8},{14,10},{1,5},{3,7},... | collective-permute-start | bytes 258056 | tf_op jit(solution)/shard_map/ppermute | solution.py:636
  174.5 2.5 %collective-permute-done.6 = f32[168,128]{1,0:T(8,128)S(1)} collective-permute-done((f32[168,128]{1,0:T(8,128)S(1)}, f32[168,128]{1,0:T(8,128)S(1)}, u32[]{:S(2)}, u32[]{:S(2)}) %collective-permute-start.6) | collective-permute-done | bytes 86048 | tf_op jit(solution)/shard_map/ppermute | solution.py:636
  177.0 3.1 %collective-permute-start.7 = (f32[168,128]{1,0:T(8,128)S(1)}, f32[168,128]{1,0:T(8,128)S(1)}, u32[]{:S(2)}, u32[]{:S(2)}) collective-permute-start(f32[168,128]{1,0:T(8,128)S(1)} %add.14), channel_id=1, source_target_pairs={{0,8},{2,10},{4,12},{6,14},{8,0},{10,2},{12,4},{14,6},{1,9},{3,11}... | collective-permute-start | bytes 258056 | tf_op jit(solution)/shard_map/ppermute | solution.py:636
  180.1 2.5 %collective-permute-done.7 = f32[168,128]{1,0:T(8,128)S(1)} collective-permute-done((f32[168,128]{1,0:T(8,128)S(1)}, f32[168,128]{1,0:T(8,128)S(1)}, u32[]{:S(2)}, u32[]{:S(2)}) %collective-permute-start.7) | collective-permute-done | bytes 86048 | tf_op jit(solution)/shard_map/ppermute | solution.py:636
  182.6 0.1 collective-permute-start.8
  182.6 1.3 collective-permute-done.8.z_ref
  183.9 0.7 final.1
  (14 shorter events, 0.1 us)
Async XLA Ops:
  0.6 2.0 %copy-start = (bf16[16,64,1280]{2,1,0:T(8,128)(2,1)S(1)}, bf16[16,64,1280]{2,1,0:T(8,128)(2,1)}, u32[]{:S(2)}) copy-start(bf16[16,64,1280]{2,1,0:T(8,128)(2,1)} %f_ref.5) | copy-start | bytes 7864324
  0.6 4.8 %copy-start.1 = (s32[224,896]{1,0:T(8,128)S(1)}, s32[224,896]{1,0:T(8,128)}, u32[]{:S(2)}) copy-start(s32[224,896]{1,0:T(8,128)} %refs_3_.5) | copy-start | bytes 2408452
  0.7 4.8 %copy-start.2 = (s32[224,896]{1,0:T(8,128)S(1)}, s32[224,896]{1,0:T(8,128)}, u32[]{:S(2)}) copy-start(s32[224,896]{1,0:T(8,128)} %refs_4_.5) | copy-start | bytes 2408452
  0.7 4.8 %copy-start.3 = (bf16[1792,128]{1,0:T(8,128)(2,1)S(1)}, bf16[1792,128]{1,0:T(8,128)(2,1)}, u32[]{:S(2)}) copy-start(bf16[1792,128]{1,0:T(8,128)(2,1)} %constant.12.clone.refs_2_) | copy-start | bytes 1376260
  0.7 4.8 %copy-start.4 = (bf16[256,896]{1,0:T(8,128)(2,1)S(1)}, bf16[256,896]{1,0:T(8,128)(2,1)}, u32[]{:S(2)}) copy-start(bf16[256,896]{1,0:T(8,128)(2,1)} %constant.10.clone.refs_1_) | copy-start | bytes 1376260
  0.7 4.8 %copy-start.7 = (bf16[512,128]{1,0:T(8,128)(2,1)S(1)}, bf16[512,128]{1,0:T(8,128)(2,1)}, u32[]{:S(2)}) copy-start(bf16[512,128]{1,0:T(8,128)(2,1)} %constant.14.clone.refs_7_) | copy-start | bytes 393220
  3.6 1.8 %collective-permute-start.1 = (f32[96,128]{1,0:T(8,128)S(1)}, f32[96,128]{1,0:T(8,128)S(1)}, u32[]{:S(2)}, u32[]{:S(2)}) collective-permute-start(f32[96,128]{1,0:T(8,128)S(1)} %get-tuple-element.31), channel_id=1, source_target_pairs={{0,1},{1,0},{2,3},{3,2},{4,5},{5,4},{6,7},{7,6},{8,9},{9,8},{10,11... | collective-permute-start | bytes 147464 | tf_op jit(solution)/shard_map/ppermute | solution.py:545
  4.2 69.1 %collective-permute-start = (f32[176,128]{1,0:T(8,128)S(1)}, f32[176,128]{1,0:T(8,128)S(1)}, u32[]{:S(2)}, u32[]{:S(2)}) collective-permute-start(f32[176,128]{1,0:T(8,128)S(1)} %get-tuple-element.27.side_ref.refs_6_), channel_id=1, source_target_pairs={{2,0},{4,2},{6,4},{8,6},{10,8},{12,10},{14,12},{3,1},{5,3},{7,5},{... | collective-permute-start | bytes 270344 | tf_op jit(solution)/shard_map/ppermute | solution.py:567
  73.2 44.7 %copy-start.5 = (bf16[512,128]{1,0:T(8,128)(2,1)S(1)}, bf16[512,128]{1,0:T(8,128)(2,1)}, u32[]{:S(2)}) copy-start(bf16[512,128]{1,0:T(8,128)(2,1)} %constant.13.clone.refs_12_) | copy-start | bytes 393220
  73.2 44.7 %copy-start.6 = (bf16[256,256]{1,0:T(8,128)(2,1)S(1)}, bf16[256,256]{1,0:T(8,128)(2,1)}, u32[]{:S(2)}) copy-start(bf16[256,256]{1,0:T(8,128)(2,1)} %constant.11.clone.refs_11_) | copy-start | bytes 393220
  73.4 44.5 %collective-permute-start.2 = (f32[40,128]{1,0:T(8,128)S(1)}, f32[40,128]{1,0:T(8,128)S(1)}, u32[]{:S(2)}, u32[]{:S(2)}) collective-permute-start(f32[40,128]{1,0:T(8,128)S(1)} %get-tuple-element.36.refs_6_), channel_id=1, source_target_pairs={{0,1},{1,0},{2,3},{3,2},{4,5},{5,4},{6,7},{7,6},{8,9},{9,8},{10,11... | collective-permute-start | bytes 61448 | tf_op jit(solution)/shard_map/ppermute | solution.py:545
  162.4 1.4 collective-permute-start.3
  164.5 1.3 collective-permute-start.4
  165.9 5.5 %collective-permute-start.5 = (f32[168,128]{1,0:T(8,128)S(1)}, f32[168,128]{1,0:T(8,128)S(1)}, u32[]{:S(2)}, u32[]{:S(2)}) collective-permute-start(f32[168,128]{1,0:T(8,128)S(1)} %add.12), channel_id=1, source_target_pairs={{0,2},{2,0},{4,6},{6,4},{8,10},{10,8},{12,14},{14,12},{1,3},{3,1},... | collective-permute-start | bytes 258056 | tf_op jit(solution)/shard_map/ppermute | solution.py:636
  171.4 5.6 %collective-permute-start.6 = (f32[168,128]{1,0:T(8,128)S(1)}, f32[168,128]{1,0:T(8,128)S(1)}, u32[]{:S(2)}, u32[]{:S(2)}) collective-permute-start(f32[168,128]{1,0:T(8,128)S(1)} %add.13), channel_id=1, source_target_pairs={{0,4},{2,6},{4,0},{6,2},{8,12},{10,14},{12,8},{14,10},{1,5},{3,7},... | collective-permute-start | bytes 258056 | tf_op jit(solution)/shard_map/ppermute | solution.py:636
  177.0 5.6 %collective-permute-start.7 = (f32[168,128]{1,0:T(8,128)S(1)}, f32[168,128]{1,0:T(8,128)S(1)}, u32[]{:S(2)}, u32[]{:S(2)}) collective-permute-start(f32[168,128]{1,0:T(8,128)S(1)} %add.14), channel_id=1, source_target_pairs={{0,8},{2,10},{4,12},{6,14},{8,0},{10,2},{12,4},{14,6},{1,9},{3,11}... | collective-permute-start | bytes 258056 | tf_op jit(solution)/shard_map/ppermute | solution.py:636
  182.6 1.3 collective-permute-start.8

commit v11 on v10

--- a/solution.py
+++ b/solution.py
@@ -604,7 +604,7 @@
             name=("inner_head", "inner_middle", "inner_tail")[part],
         )(*(here(v) for v in (got, lift, back, labels, valid_mask)), *args)
 
-    middle = tiles // 2 + 1
+    middle = tiles // 2 + 2
     total, loss, stack, floor = inner(0, 1, middle - 1, here(x), here(own), here(fill))
     side, total = lax.optimization_barrier((side, total))
     beside, beyond = pl.pallas_call(
@@ -631,10 +631,10 @@
     )(*(here(v) for v in (features, beside, grad, got, loss)), valid_count)
 
     total = mine + swap(other)
-    step = 1
-    while step < gx:
-        total = total + lax.ppermute(total, "gx", [(i, i ^ step) for i in range(gx)])
-        step *= 2
+    steps = [1 << k for k in range(gx.bit_length() - 1)]
+    for one, two in zip(steps, steps[1::-1] + steps[2:]):
+        pairs = [(gy * i + g, gy * (i ^ (two if g else one)) + g) for i in range(gx) for g in range(gy)]
+        total = total + lax.ppermute(total, ("gx", "gy"), pairs)
     loss, weight, bias = pl.pallas_call(
         functools.partial(final_kernel, chans),
         in_specs=[VMEM] * 2,

time: 185 us -> 184 us (level)
  no operation moved by 1% of the time
where the time goes in v11:
time: 184 us
  Pallas kernels  161 us (88%)
  starting transfers between devices  12 us (7%)
  waiting for transfers between devices  9.8 us (5%)
    pallas_call x3, Pallas kernels, inner(): pl.pallas_call(functools.partial(inner_kernel, rows, cols, chans, slots,...  156 us
    ppermute x3, starting transfers between devices, body(): total = total + lax.ppermute(total, ('gx', 'gy'), pairs)  8.98 us
    ppermute x3, waiting for transfers between devices, body(): total = total + lax.ppermute(total, ('gx', 'gy'), pairs)  7.39 us
  transfers between devices with their start and end apart: 9, of which 6 were waited for; matrix products, arithmetic and copies ran while one was open for 0% of the time, Pallas kernels for 61%

profile of v11, /device:TPU:0, one launch (start us, length us, event | category | flops | bytes accessed | tf_op | source)
XLA Modules:
  0.0 184.3 jit_solution(14061225859855707253)
XLA Ops:
  0.7 0.0 copy-start.3
  0.7 0.0 copy-start.4
  0.7 0.0 copy-start.7
  0.7 1.5 pack.1
  2.2 0.4 copy-done
  2.6 1.0 logits.1
  3.6 0.6 collective-permute-start.1
  4.2 1.3 collective-permute-start
  5.5 0.0 collective-permute-done.1.refs_0_
  5.5 89.8 %inner_head.1 = (f32[1024,128]{1,0:T(8,128)S(1)}, f32[8,128]{1,0:T(8,128)S(1)}, bf16[768,256]{1,0:T(8,128)(2,1)S(1)}, f32[8,128]{1,0:T(8,128)S(1)}) custom-call(f32[96,128]{1,0:T(8,128)S(1)} %collective-permute-done.1.refs_0_, bf16[256,896]{1,0:T(8,128)(2,1)S(1)} %copy-done.4, bf16[1792,128]{1,0:T(8,128)(2,1)S(1)} %copy-done.3, s32[224,896]{1,0:T(8,128)S(1)} %copy-done.1, ...), custom_call_target="tpu_custom_call" | custom-call | flops 1000000000 | bytes 2000000 | tf_op jit(solution)/shard_map/inner_head/pallas_call | solution.py:587
  95.3 0.0 copy-start.5
  95.3 0.0 copy-start.6
  95.3 0.0 collective-permute-done.side_ref.refs_8_
  95.3 0.2 beside.1
  95.5 0.1 collective-permute-start.2
  95.6 22.3 %inner_middle.1 = (f32[1024,128]{1,0:T(8,128)S(1)}, f32[8,128]{1,0:T(8,128)S(1)}) custom-call(f32[96,128]{1,0:T(8,128)S(1)} %collective-permute-done.1.refs_0_, bf16[256,896]{1,0:T(8,128)(2,1)S(1)} %copy-done.4, bf16[1792,128]{1,0:T(8,128)(2,1)S(1)} %copy-done.3, s32[224,896]{1,0:T(8,128)S(1)} %copy-done.1, s32[224,896]{1,0:T(8,128)S(1)} %copy-done.2, ...), custom_call_target="tpu_custom_call" | custom-call | flops 1000000000 | bytes 2000000 | tf_op jit(solution)/shard_map/inner_middle/pallas_call | solution.py:587
  117.9 0.0 collective-permute-done.2.refs_7_
  117.9 44.5 %inner_tail.1 = (f32[768,128]{1,0:T(8,128)S(1)}, f32[32,128]{1,0:T(8,128)S(1)}, f32[8,128]{1,0:T(8,128)S(1)}) custom-call(f32[96,128]{1,0:T(8,128)S(1)} %collective-permute-done.1.refs_0_, bf16[256,896]{1,0:T(8,128)(2,1)S(1)} %copy-done.4, bf16[1792,128]{1,0:T(8,128)(2,1)S(1)} %copy-done.3, s32[224,896]{1,0:T(8,128)S(1)} %copy-done.1, ...), custom_call_target="tpu_custom_call" | custom-call | flops 1000000000 | bytes 2000000 | tf_op jit(solution)/shard_map/inner_tail/pallas_call | solution.py:587
  162.3 0.6 collective-permute-start.3
  163.6 0.2 collective-permute-done.3.got_ref
  163.7 0.7 grad.1
  164.5 0.4 collective-permute-start.4
  164.9 0.9 collective-permute-done.4
  165.8 2.6 %collective-permute-start.5 = (f32[168,128]{1,0:T(8,128)S(1)}, f32[168,128]{1,0:T(8,128)S(1)}, u32[]{:S(2)}, u32[]{:S(2)}) collective-permute-start(f32[168,128]{1,0:T(8,128)S(1)} %add.12), channel_id=1, source_target_pairs={{0,2},{1,5},{2,0},{3,7},{4,6},{5,1},{6,4},{7,3},{8,10},{9,13},{10,... | collective-permute-start | bytes 258056 | tf_op jit(solution)/shard_map/ppermute | solution.py:637
  168.4 2.5 %collective-permute-done.5 = f32[168,128]{1,0:T(8,128)S(1)} collective-permute-done((f32[168,128]{1,0:T(8,128)S(1)}, f32[168,128]{1,0:T(8,128)S(1)}, u32[]{:S(2)}, u32[]{:S(2)}) %collective-permute-start.5) | collective-permute-done | bytes 86048 | tf_op jit(solution)/shard_map/ppermute | solution.py:637
  170.9 3.3 %collective-permute-start.6 = (f32[168,128]{1,0:T(8,128)S(1)}, f32[168,128]{1,0:T(8,128)S(1)}, u32[]{:S(2)}, u32[]{:S(2)}) collective-permute-start(f32[168,128]{1,0:T(8,128)S(1)} %add.13), channel_id=1, source_target_pairs={{0,4},{1,3},{2,6},{3,1},{4,0},{5,7},{6,2},{7,5},{8,12},{9,11},{10,... | collective-permute-start | bytes 258056 | tf_op jit(solution)/shard_map/ppermute | solution.py:637
  174.2 2.5 %collective-permute-done.6 = f32[168,128]{1,0:T(8,128)S(1)} collective-permute-done((f32[168,128]{1,0:T(8,128)S(1)}, f32[168,128]{1,0:T(8,128)S(1)}, u32[]{:S(2)}, u32[]{:S(2)}) %collective-permute-start.6) | collective-permute-done | bytes 86048 | tf_op jit(solution)/shard_map/ppermute | solution.py:637
  176.7 3.1 %collective-permute-start.7 = (f32[168,128]{1,0:T(8,128)S(1)}, f32[168,128]{1,0:T(8,128)S(1)}, u32[]{:S(2)}, u32[]{:S(2)}) collective-permute-start(f32[168,128]{1,0:T(8,128)S(1)} %add.14), channel_id=1, source_target_pairs={{0,8},{1,9},{2,10},{3,11},{4,12},{5,13},{6,14},{7,15},{8,0},{9,1},... | collective-permute-start | bytes 258056 | tf_op jit(solution)/shard_map/ppermute | solution.py:637
  179.8 2.5 %collective-permute-done.7 = f32[168,128]{1,0:T(8,128)S(1)} collective-permute-done((f32[168,128]{1,0:T(8,128)S(1)}, f32[168,128]{1,0:T(8,128)S(1)}, u32[]{:S(2)}, u32[]{:S(2)}) %collective-permute-start.7) | collective-permute-done | bytes 86048 | tf_op jit(solution)/shard_map/ppermute | solution.py:637
  182.2 0.1 collective-permute-start.8
  182.3 1.3 collective-permute-done.8.z_ref
  183.6 0.7 final.1
  (14 shorter events, 0.1 us)
Async XLA Ops:
  0.6 2.0 %copy-start = (bf16[16,64,1280]{2,1,0:T(8,128)(2,1)S(1)}, bf16[16,64,1280]{2,1,0:T(8,128)(2,1)}, u32[]{:S(2)}) copy-start(bf16[16,64,1280]{2,1,0:T(8,128)(2,1)} %f_ref.5) | copy-start | bytes 7864324
  0.6 4.8 %copy-start.1 = (s32[224,896]{1,0:T(8,128)S(1)}, s32[224,896]{1,0:T(8,128)}, u32[]{:S(2)}) copy-start(s32[224,896]{1,0:T(8,128)} %refs_3_.5) | copy-start | bytes 2408452
  0.7 4.8 %copy-start.2 = (s32[224,896]{1,0:T(8,128)S(1)}, s32[224,896]{1,0:T(8,128)}, u32[]{:S(2)}) copy-start(s32[224,896]{1,0:T(8,128)} %refs_4_.5) | copy-start | bytes 2408452
  0.7 4.8 %copy-start.3 = (bf16[1792,128]{1,0:T(8,128)(2,1)S(1)}, bf16[1792,128]{1,0:T(8,128)(2,1)}, u32[]{:S(2)}) copy-start(bf16[1792,128]{1,0:T(8,128)(2,1)} %constant.12.clone.refs_2_) | copy-start | bytes 1376260
  0.7 4.8 %copy-start.4 = (bf16[256,896]{1,0:T(8,128)(2,1)S(1)}, bf16[256,896]{1,0:T(8,128)(2,1)}, u32[]{:S(2)}) copy-start(bf16[256,896]{1,0:T(8,128)(2,1)} %constant.10.clone.refs_1_) | copy-start | bytes 1376260
  0.7 4.8 %copy-start.7 = (bf16[512,128]{1,0:T(8,128)(2,1)S(1)}, bf16[512,128]{1,0:T(8,128)(2,1)}, u32[]{:S(2)}) copy-start(bf16[512,128]{1,0:T(8,128)(2,1)} %constant.14.clone.refs_7_) | copy-start | bytes 393220
  3.6 1.8 %collective-permute-start.1 = (f32[96,128]{1,0:T(8,128)S(1)}, f32[96,128]{1,0:T(8,128)S(1)}, u32[]{:S(2)}, u32[]{:S(2)}) collective-permute-start(f32[96,128]{1,0:T(8,128)S(1)} %get-tuple-element.31), channel_id=1, source_target_pairs={{0,1},{1,0},{2,3},{3,2},{4,5},{5,4},{6,7},{7,6},{8,9},{9,8},{10,11... | collective-permute-start | bytes 147464 | tf_op jit(solution)/shard_map/ppermute | solution.py:545
  4.2 91.2 %collective-permute-start = (f32[176,128]{1,0:T(8,128)S(1)}, f32[176,128]{1,0:T(8,128)S(1)}, u32[]{:S(2)}, u32[]{:S(2)}) collective-permute-start(f32[176,128]{1,0:T(8,128)S(1)} %get-tuple-element.27.side_ref.refs_6_), channel_id=1, source_target_pairs={{2,0},{4,2},{6,4},{8,6},{10,8},{12,10},{14,12},{3,1},{5,3},{7,5},{... | collective-permute-start | bytes 270344 | tf_op jit(solution)/shard_map/ppermute | solution.py:567
  95.3 22.6 %copy-start.5 = (bf16[512,128]{1,0:T(8,128)(2,1)S(1)}, bf16[512,128]{1,0:T(8,128)(2,1)}, u32[]{:S(2)}) copy-start(bf16[512,128]{1,0:T(8,128)(2,1)} %constant.13.clone.refs_12_) | copy-start | bytes 393220
  95.3 22.6 %copy-start.6 = (bf16[256,256]{1,0:T(8,128)(2,1)S(1)}, bf16[256,256]{1,0:T(8,128)(2,1)}, u32[]{:S(2)}) copy-start(bf16[256,256]{1,0:T(8,128)(2,1)} %constant.11.clone.refs_11_) | copy-start | bytes 393220
  95.5 22.4 %collective-permute-start.2 = (f32[40,128]{1,0:T(8,128)S(1)}, f32[40,128]{1,0:T(8,128)S(1)}, u32[]{:S(2)}, u32[]{:S(2)}) collective-permute-start(f32[40,128]{1,0:T(8,128)S(1)} %get-tuple-element.36.refs_6_), channel_id=1, source_target_pairs={{0,1},{1,0},{2,3},{3,2},{4,5},{5,4},{6,7},{7,6},{8,9},{9,8},{10,11... | collective-permute-start | bytes 61448 | tf_op jit(solution)/shard_map/ppermute | solution.py:545
  162.3 1.4 collective-permute-start.3
  164.5 1.3 collective-permute-start.4
  165.8 5.1 %collective-permute-start.5 = (f32[168,128]{1,0:T(8,128)S(1)}, f32[168,128]{1,0:T(8,128)S(1)}, u32[]{:S(2)}, u32[]{:S(2)}) collective-permute-start(f32[168,128]{1,0:T(8,128)S(1)} %add.12), channel_id=1, source_target_pairs={{0,2},{1,5},{2,0},{3,7},{4,6},{5,1},{6,4},{7,3},{8,10},{9,13},{10,... | collective-permute-start | bytes 258056 | tf_op jit(solution)/shard_map/ppermute | solution.py:637
  170.9 5.7 %collective-permute-start.6 = (f32[168,128]{1,0:T(8,128)S(1)}, f32[168,128]{1,0:T(8,128)S(1)}, u32[]{:S(2)}, u32[]{:S(2)}) collective-permute-start(f32[168,128]{1,0:T(8,128)S(1)} %add.13), channel_id=1, source_target_pairs={{0,4},{1,3},{2,6},{3,1},{4,0},{5,7},{6,2},{7,5},{8,12},{9,11},{10,... | collective-permute-start | bytes 258056 | tf_op jit(solution)/shard_map/ppermute | solution.py:637
  176.7 5.6 %collective-permute-start.7 = (f32[168,128]{1,0:T(8,128)S(1)}, f32[168,128]{1,0:T(8,128)S(1)}, u32[]{:S(2)}, u32[]{:S(2)}) collective-permute-start(f32[168,128]{1,0:T(8,128)S(1)} %add.14), channel_id=1, source_target_pairs={{0,8},{1,9},{2,10},{3,11},{4,12},{5,13},{6,14},{7,15},{8,0},{9,1},... | collective-permute-start | bytes 258056 | tf_op jit(solution)/shard_map/ppermute | solution.py:637
  182.2 1.3 collective-permute-start.8

commit v12 on v11

--- a/solution.py
+++ b/solution.py
@@ -78,7 +78,7 @@
     for copy in copies:
         copy.start()
     at = lax.broadcasted_iota(jnp.int32, (SUB, LANES), 1)
-    for copy in copies:
+    for copy in copies[:2]:
         copy.wait()
     for b in range(rows // SUB):
         strip = jnp.full((SUB, LANES), -1.0, f32)
@@ -88,10 +88,13 @@
             here = (at >= j * HALF) & (at < j * HALF + HALF)
             strip = jnp.where(here, pltpu.roll(lab, j * HALF, 1) if j else lab, strip)
         out_ref[b * SUB : b * SUB + SUB, :] = strip
+    copies[2].wait()
     for i in range(rows):
         line = f_vmem[i].astype(f32)
         for k in range(width // LANES):
             out_ref[rows + k * rows + i : rows + k * rows + i + 1, :] = line[0:1, k * LANES : k * LANES + LANES]
+    for copy in copies[3:]:
+        copy.wait()
     for t in range(tiles):
         lanes = slice(t * LANES, t * LANES + LANES)
         head_ref[t * SUB : t * SUB + SUB, :] = jnp.where(h_vmem[1, :, lanes] != 0, h_vmem[0, :, lanes], -1).astype(f32)

time: 184 us -> 184 us (level)
  no operation moved by 1% of the time
where the time goes in v12:
time: 184 us
  Pallas kernels  160 us (87%)
  starting transfers between devices  12 us (7%)
  waiting for transfers between devices  9.8 us (5%)
    pallas_call x3, Pallas kernels, inner(): pl.pallas_call(functools.partial(inner_kernel, rows, cols, chans, slots,...  156 us
    ppermute x3, starting transfers between devices, body(): total = total + lax.ppermute(total, ('gx', 'gy'), pairs)  8.98 us
    ppermute x3, waiting for transfers between devices, body(): total = total + lax.ppermute(total, ('gx', 'gy'), pairs)  7.39 us
  transfers between devices with their start and end apart: 9, of which 6 were waited for; matrix products, arithmetic and copies ran while one was open for 0% of the time, Pallas kernels for 61%

profile of v12, /device:TPU:0, one launch (start us, length us, event | category | flops | bytes accessed | tf_op | source)
XLA Modules:
  0.0 184.3 jit_solution(15706976501622978711)
XLA Ops:
  0.7 0.0 copy-start.3
  0.7 0.0 copy-start.4
  0.7 0.0 copy-start.7
  0.7 1.4 pack.1
  2.1 0.5 copy-done
  2.6 1.0 logits.1
  3.6 0.6 collective-permute-start.1
  4.2 1.3 collective-permute-start
  5.5 0.0 collective-permute-done.1.refs_0_
  5.5 89.8 %inner_head.1 = (f32[1024,128]{1,0:T(8,128)S(1)}, f32[8,128]{1,0:T(8,128)S(1)}, bf16[768,256]{1,0:T(8,128)(2,1)S(1)}, f32[8,128]{1,0:T(8,128)S(1)}) custom-call(f32[96,128]{1,0:T(8,128)S(1)} %collective-permute-done.1.refs_0_, bf16[256,896]{1,0:T(8,128)(2,1)S(1)} %copy-done.4, bf16[1792,128]{1,0:T(8,128)(2,1)S(1)} %copy-done.3, s32[224,896]{1,0:T(8,128)S(1)} %copy-done.1, ...), custom_call_target="tpu_custom_call" | custom-call | flops 1000000000 | bytes 2000000 | tf_op jit(solution)/shard_map/inner_head/pallas_call | solution.py:590
  95.3 0.0 copy-start.5
  95.3 0.0 copy-start.6
  95.3 0.0 collective-permute-done.side_ref.refs_8_
  95.3 0.2 beside.1
  95.5 0.1 collective-permute-start.2
  95.6 22.3 %inner_middle.1 = (f32[1024,128]{1,0:T(8,128)S(1)}, f32[8,128]{1,0:T(8,128)S(1)}) custom-call(f32[96,128]{1,0:T(8,128)S(1)} %collective-permute-done.1.refs_0_, bf16[256,896]{1,0:T(8,128)(2,1)S(1)} %copy-done.4, bf16[1792,128]{1,0:T(8,128)(2,1)S(1)} %copy-done.3, s32[224,896]{1,0:T(8,128)S(1)} %copy-done.1, s32[224,896]{1,0:T(8,128)S(1)} %copy-done.2, ...), custom_call_target="tpu_custom_call" | custom-call | flops 1000000000 | bytes 2000000 | tf_op jit(solution)/shard_map/inner_middle/pallas_call | solution.py:590
  117.9 0.0 collective-permute-done.2.refs_7_
  117.9 44.5 %inner_tail.1 = (f32[768,128]{1,0:T(8,128)S(1)}, f32[32,128]{1,0:T(8,128)S(1)}, f32[8,128]{1,0:T(8,128)S(1)}) custom-call(f32[96,128]{1,0:T(8,128)S(1)} %collective-permute-done.1.refs_0_, bf16[256,896]{1,0:T(8,128)(2,1)S(1)} %copy-done.4, bf16[1792,128]{1,0:T(8,128)(2,1)S(1)} %copy-done.3, s32[224,896]{1,0:T(8,128)S(1)} %copy-done.1, ...), custom_call_target="tpu_custom_call" | custom-call | flops 1000000000 | bytes 2000000 | tf_op jit(solution)/shard_map/inner_tail/pallas_call | solution.py:590
  162.3 0.6 collective-permute-start.3
  163.6 0.2 collective-permute-done.3.got_ref
  163.7 0.7 grad.1
  164.5 0.4 collective-permute-start.4
  164.9 0.9 collective-permute-done.4
  165.8 2.6 %collective-permute-start.5 = (f32[168,128]{1,0:T(8,128)S(1)}, f32[168,128]{1,0:T(8,128)S(1)}, u32[]{:S(2)}, u32[]{:S(2)}) collective-permute-start(f32[168,128]{1,0:T(8,128)S(1)} %add.12), channel_id=1, source_target_pairs={{0,2},{1,5},{2,0},{3,7},{4,6},{5,1},{6,4},{7,3},{8,10},{9,13},{10,... | collective-permute-start | bytes 258056 | tf_op jit(solution)/shard_map/ppermute | solution.py:640
  168.4 2.5 %collective-permute-done.5 = f32[168,128]{1,0:T(8,128)S(1)} collective-permute-done((f32[168,128]{1,0:T(8,128)S(1)}, f32[168,128]{1,0:T(8,128)S(1)}, u32[]{:S(2)}, u32[]{:S(2)}) %collective-permute-start.5) | collective-permute-done | bytes 86048 | tf_op jit(solution)/shard_map/ppermute | solution.py:640
  170.9 3.3 %collective-permute-start.6 = (f32[168,128]{1,0:T(8,128)S(1)}, f32[168,128]{1,0:T(8,128)S(1)}, u32[]{:S(2)}, u32[]{:S(2)}) collective-permute-start(f32[168,128]{1,0:T(8,128)S(1)} %add.13), channel_id=1, source_target_pairs={{0,4},{1,3},{2,6},{3,1},{4,0},{5,7},{6,2},{7,5},{8,12},{9,11},{10,... | collective-permute-start | bytes 258056 | tf_op jit(solution)/shard_map/ppermute | solution.py:640
  174.2 2.5 %collective-permute-done.6 = f32[168,128]{1,0:T(8,128)S(1)} collective-permute-done((f32[168,128]{1,0:T(8,128)S(1)}, f32[168,128]{1,0:T(8,128)S(1)}, u32[]{:S(2)}, u32[]{:S(2)}) %collective-permute-start.6) | collective-permute-done | bytes 86048 | tf_op jit(solution)/shard_map/ppermute | solution.py:640
  176.7 3.1 %collective-permute-start.7 = (f32[168,128]{1,0:T(8,128)S(1)}, f32[168,128]{1,0:T(8,128)S(1)}, u32[]{:S(2)}, u32[]{:S(2)}) collective-permute-start(f32[168,128]{1,0:T(8,128)S(1)} %add.14), channel_id=1, source_target_pairs={{0,8},{1,9},{2,10},{3,11},{4,12},{5,13},{6,14},{7,15},{8,0},{9,1},... | collective-permute-start | bytes 258056 | tf_op jit(solution)/shard_map/ppermute | solution.py:640
  179.8 2.5 %collective-permute-done.7 = f32[168,128]{1,0:T(8,128)S(1)} collective-permute-done((f32[168,128]{1,0:T(8,128)S(1)}, f32[168,128]{1,0:T(8,128)S(1)}, u32[]{:S(2)}, u32[]{:S(2)}) %collective-permute-start.7) | collective-permute-done | bytes 86048 | tf_op jit(solution)/shard_map/ppermute | solution.py:640
  182.2 0.1 collective-permute-start.8
  182.3 1.3 collective-permute-done.8.z_ref
  183.6 0.7 final.1
  (14 shorter events, 0.1 us)
Async XLA Ops:
  0.6 2.0 %copy-start = (bf16[16,64,1280]{2,1,0:T(8,128)(2,1)S(1)}, bf16[16,64,1280]{2,1,0:T(8,128)(2,1)}, u32[]{:S(2)}) copy-start(bf16[16,64,1280]{2,1,0:T(8,128)(2,1)} %f_ref.5) | copy-start | bytes 7864324
  0.6 4.8 %copy-start.1 = (s32[224,896]{1,0:T(8,128)S(1)}, s32[224,896]{1,0:T(8,128)}, u32[]{:S(2)}) copy-start(s32[224,896]{1,0:T(8,128)} %refs_3_.5) | copy-start | bytes 2408452
  0.7 4.8 %copy-start.2 = (s32[224,896]{1,0:T(8,128)S(1)}, s32[224,896]{1,0:T(8,128)}, u32[]{:S(2)}) copy-start(s32[224,896]{1,0:T(8,128)} %refs_4_.5) | copy-start | bytes 2408452
  0.7 4.8 %copy-start.3 = (bf16[1792,128]{1,0:T(8,128)(2,1)S(1)}, bf16[1792,128]{1,0:T(8,128)(2,1)}, u32[]{:S(2)}) copy-start(bf16[1792,128]{1,0:T(8,128)(2,1)} %constant.12.clone.refs_2_) | copy-start | bytes 1376260
  0.7 4.8 %copy-start.4 = (bf16[256,896]{1,0:T(8,128)(2,1)S(1)}, bf16[256,896]{1,0:T(8,128)(2,1)}, u32[]{:S(2)}) copy-start(bf16[256,896]{1,0:T(8,128)(2,1)} %constant.10.clone.refs_1_) | copy-start | bytes 1376260
  0.7 4.8 %copy-start.7 = (bf16[512,128]{1,0:T(8,128)(2,1)S(1)}, bf16[512,128]{1,0:T(8,128)(2,1)}, u32[]{:S(2)}) copy-start(bf16[512,128]{1,0:T(8,128)(2,1)} %constant.14.clone.refs_7_) | copy-start | bytes 393220
  3.6 1.8 %collective-permute-start.1 = (f32[96,128]{1,0:T(8,128)S(1)}, f32[96,128]{1,0:T(8,128)S(1)}, u32[]{:S(2)}, u32[]{:S(2)}) collective-permute-start(f32[96,128]{1,0:T(8,128)S(1)} %get-tuple-element.31), channel_id=1, source_target_pairs={{0,1},{1,0},{2,3},{3,2},{4,5},{5,4},{6,7},{7,6},{8,9},{9,8},{10,11... | collective-permute-start | bytes 147464 | tf_op jit(solution)/shard_map/ppermute | solution.py:548
  4.2 91.2 %collective-permute-start = (f32[176,128]{1,0:T(8,128)S(1)}, f32[176,128]{1,0:T(8,128)S(1)}, u32[]{:S(2)}, u32[]{:S(2)}) collective-permute-start(f32[176,128]{1,0:T(8,128)S(1)} %get-tuple-element.27.side_ref.refs_6_), channel_id=1, source_target_pairs={{2,0},{4,2},{6,4},{8,6},{10,8},{12,10},{14,12},{3,1},{5,3},{7,5},{... | collective-permute-start | bytes 270344 | tf_op jit(solution)/shard_map/ppermute | solution.py:570
  95.3 22.6 %copy-start.5 = (bf16[512,128]{1,0:T(8,128)(2,1)S(1)}, bf16[512,128]{1,0:T(8,128)(2,1)}, u32[]{:S(2)}) copy-start(bf16[512,128]{1,0:T(8,128)(2,1)} %constant.13.clone.refs_12_) | copy-start | bytes 393220
  95.3 22.6 %copy-start.6 = (bf16[256,256]{1,0:T(8,128)(2,1)S(1)}, bf16[256,256]{1,0:T(8,128)(2,1)}, u32[]{:S(2)}) copy-start(bf16[256,256]{1,0:T(8,128)(2,1)} %constant.11.clone.refs_11_) | copy-start | bytes 393220
  95.5 22.4 %collective-permute-start.2 = (f32[40,128]{1,0:T(8,128)S(1)}, f32[40,128]{1,0:T(8,128)S(1)}, u32[]{:S(2)}, u32[]{:S(2)}) collective-permute-start(f32[40,128]{1,0:T(8,128)S(1)} %get-tuple-element.36.refs_6_), channel_id=1, source_target_pairs={{0,1},{1,0},{2,3},{3,2},{4,5},{5,4},{6,7},{7,6},{8,9},{9,8},{10,11... | collective-permute-start | bytes 61448 | tf_op jit(solution)/shard_map/ppermute | solution.py:548
  162.3 1.4 collective-permute-start.3
  164.5 1.3 collective-permute-start.4
  165.8 5.1 %collective-permute-start.5 = (f32[168,128]{1,0:T(8,128)S(1)}, f32[168,128]{1,0:T(8,128)S(1)}, u32[]{:S(2)}, u32[]{:S(2)}) collective-permute-start(f32[168,128]{1,0:T(8,128)S(1)} %add.12), channel_id=1, source_target_pairs={{0,2},{1,5},{2,0},{3,7},{4,6},{5,1},{6,4},{7,3},{8,10},{9,13},{10,... | collective-permute-start | bytes 258056 | tf_op jit(solution)/shard_map/ppermute | solution.py:640
  170.9 5.7 %collective-permute-start.6 = (f32[168,128]{1,0:T(8,128)S(1)}, f32[168,128]{1,0:T(8,128)S(1)}, u32[]{:S(2)}, u32[]{:S(2)}) collective-permute-start(f32[168,128]{1,0:T(8,128)S(1)} %add.13), channel_id=1, source_target_pairs={{0,4},{1,3},{2,6},{3,1},{4,0},{5,7},{6,2},{7,5},{8,12},{9,11},{10,... | collective-permute-start | bytes 258056 | tf_op jit(solution)/shard_map/ppermute | solution.py:640
  176.7 5.6 %collective-permute-start.7 = (f32[168,128]{1,0:T(8,128)S(1)}, f32[168,128]{1,0:T(8,128)S(1)}, u32[]{:S(2)}, u32[]{:S(2)}) collective-permute-start(f32[168,128]{1,0:T(8,128)S(1)} %add.14), channel_id=1, source_target_pairs={{0,8},{1,9},{2,10},{3,11},{4,12},{5,13},{6,14},{7,15},{8,0},{9,1},... | collective-permute-start | bytes 258056 | tf_op jit(solution)/shard_map/ppermute | solution.py:640
  182.2 1.3 collective-permute-start.8
